TPU v7x, 32 devices: a whole 2x2x4 slice. The times are simulated.
32 devices in a mesh: mem: 2 (over y), gy: 4 (over z), gx: 4 (over x, core).
Axes of the slice: x: 2, y: 2, z: 4, core: 2. Of those that a mesh axis runs over, the one named last changes fastest.
Arguments:
- perturbations: bfloat16 [4, 5, 16, 32, 512], P('mem', None, None, 'gy', 'gx'), may hold values from -6 to 6
- control: float32 [4, 16, 32, 512], P('mem', None, 'gy', 'gx'), may hold values from -6 to 6
- background: float32 [5, 16, 32, 512], P(None, 'mem', 'gy', 'gx'), may hold values from -6 to 6
- obs_cell: int32 [128, 512], P('gy', 'gx'), may hold values from 0 to 81919
- huber_flag: int32 [128, 512], P('gy', 'gx'), may hold values 0 or 1
- innovation: float32 [128, 512], P('gy', 'gx'), may hold values from -6 to 6
- precision: float32 [128, 512], P('gy', 'gx'), may hold values from 10 to 100
Outputs:
- analysis: float32 [5, 16, 32, 512], P(None, 'mem', 'gy', 'gx')
- control_out: float32 [4, 16, 32, 512], P('mem', None, 'gy', 'gx')
Inputs may be any that keep to these rules, and one draw needn't show every extreme that they name: `obs_cell`: a cell of its tile, ordered by variable, then level, then row, then column.
All inputs are finite; a program needn't handle non-finite values. No bound on the sum of `huber_flag` on one device may be relied on, other than what follows from the above.
Results may differ from a plain program's by a relative error of at most 0.0003.
Values sent between devices are 32-bit elements; how exact they have to be, the bound alone decides.
No kernel may reach another device: no remote copies, remote signals or barrier semaphores. Data moves between devices by JAX's collectives and lax.ppermute only.
A program may use at most 64 MiB of HBM per device.

v0:
```python
import jax
import jax.numpy as jnp
from jax import lax
from jax.sharding import PartitionSpec as P

ITERS = 2


huber_width = 1.0


def extended(value, sides, width):
    for axis, dim in sides:
        peers, length = (lax.axis_size(axis), value.shape[dim])
        up = [(i, (i + 1) % peers) for i in range(peers - 1)]
        down = [(j, i) for i, j in up]
        last = lax.slice_in_dim(value, length - width, length, axis=dim)
        initial = lax.slice_in_dim(value, 0, width, axis=dim)
        before = lax.ppermute(last, axis, up)
        after = lax.ppermute(initial, axis, down)
        value = jnp.concatenate([before, value, after], axis=dim)
    return value


def filter_taps():
    offsets = jnp.arange(-4, 5).astype(jnp.float32)
    raw = jnp.exp(-offsets * offsets / 8.0)
    return raw / jnp.sum(raw)


def smooth(field):
    weights = filter_taps()
    rows, cols = (field.shape[2], field.shape[3])
    padded = extended(field, (("gy", 2), ("gx", 3)), 4)
    along = sum((weights[offset] * padded[..., :, offset : offset + cols] for offset in range(9)))
    return sum((weights[offset] * along[..., offset : offset + rows, :] for offset in range(9)))


def member_sum(perturbations, alpha):
    return jnp.sum(perturbations.astype(jnp.float32) * alpha[:, None], axis=0)


def project(perturbations, adjoint):
    return jnp.sum(perturbations.astype(jnp.float32) * adjoint[None], axis=1)


def seen_total(values):
    return lax.psum(values, "mem")


def step_size(grad_local, grad_total, curv_local):
    grad_total, curv_total = lax.psum((grad_local, curv_local), ("mem", "gy", "gx"))
    return grad_total / (grad_total + curv_total)


def robust_weight(misfit, flagged):
    scaled = misfit / huber_width
    return jnp.where(flagged, 1.0 / jnp.sqrt(1.0 + scaled * scaled), 1.0)


def per_device(perturbations, control, background, obs_cell, huber_flag, innovation, precision):
    flat_cell = obs_cell.reshape(-1)
    observed = innovation.reshape(-1)
    inverse_var = precision.reshape(-1)
    flagged = huber_flag.reshape(-1) == 1
    state = control
    smoothed = smooth(state)
    partial_value = member_sum(perturbations, smoothed)
    seen_inc = seen_total(partial_value.reshape(-1)[flat_cell])
    counted = jnp.ones(flat_cell.shape, bool) & (lax.axis_index("mem") == 0)
    for iteration in range(ITERS):
        misfit = seen_inc - observed
        weight = robust_weight(misfit, flagged)
        weighted = inverse_var * weight * misfit
        adjoint = (
            jnp.zeros((partial_value.size,), jnp.float32)
            .at[flat_cell]
            .add(weighted)
            .reshape(partial_value.shape)
        )
        grad = state + smooth(project(perturbations, adjoint))
        grad_local = jnp.sum(grad * grad)
        smooth_grad = smooth(grad)
        seen_step = seen_total(member_sum(perturbations, smooth_grad).reshape(-1)[flat_cell])
        curv_local = jnp.sum(jnp.where(counted, inverse_var * weight * seen_step * seen_step, 0.0))
        step = step_size(grad_local, grad_local, curv_local)
        state = state - step * grad
        seen_inc = seen_inc - step * seen_step
        smoothed = smoothed - step * smooth_grad
    mine = lax.psum_scatter(
        member_sum(perturbations, smoothed), "mem", scatter_dimension=1, tiled=True
    )
    return (background + mine, state)


def solution(mesh):
    in_specs = (
        P("mem", None, None, "gy", "gx"),
        P("mem", None, "gy", "gx"),
        P(None, "mem", "gy", "gx"),
        P("gy", "gx"),
        P("gy", "gx"),
        P("gy", "gx"),
        P("gy", "gx"),
    )
    out_specs = (P(None, "mem", "gy", "gx"), P("mem", None, "gy", "gx"))
    return jax.shard_map(
        per_device, mesh=mesh, in_specs=in_specs, out_specs=out_specs, check_vma=False
    )
```

profile of v0, /device:TPU:0, one launch (start us, length us, event | category | flops | bytes accessed | tf_op | source)
XLA Modules:
  0.0 416.0 jit_solution(11802760068327610708)
XLA Ops:
  26.4 6.1 %fusion.38 = f32[2,16,16,128]{3,2,1,0:T(8,128)S(1)} fusion(f32[2,16,16,132]{3,2,1,0:T(8,128)S(1)} %get-tuple-element.31, f32[2,16,16,132]{3,2,1,0:T(8,128)S(1)} %get-tuple-element.30, f32[]{:T(128)} %bitcast.12, f32[]{:T(128)} %bitcast.11, f32[]{:T(128)} %bitcast.10, f32[]{:T(128)} %bitcast.9, f32[]{:T(128)} %bitcast.8, f32[]{:T(128)} %bitcast.7, ...), kind=kLoop, calls=%fused_computation.93 | loop fusion | flops 1245184 | bytes 2621476 | tf_op jit(solution)/shard_map/add | solution.py:35
  32.5 5.8 %fusion.84 = f32[2,16,8,128]{3,2,1,0:T(8,128)S(1)} fusion(f32[2,16,16,128]{3,2,1,0:T(8,128)S(1)} %fusion.38, f32[]{:T(128)} %bitcast.12, f32[]{:T(128)} %bitcast.11, f32[]{:T(128)} %bitcast.10, f32[]{:T(128)} %bitcast.9, f32[]{:T(128)} %bitcast.8, f32[]{:T(128)} %bitcast.7, f32[]{:T(128)} %bitcast.6, f32[]{:T(128)} %bitcast.5, f32[]{:T(128)} %bitcast.4), kind=kLoop, calls=%fused_computation.190 | loop fusion | flops 557056 | bytes 1310756 | tf_op jit(solution)/shard_map/add | solution.py:36
  38.4 23.0 %gather_fusion = f32[4096]{0:T(1024)S(1)} fusion(f32[81920]{0:T(1024)S(1)} %bitcast.63, s32[4096]{0:T(1024)S(1)} %broadcast_clamp_fusion), kind=kCustom, calls=%fused_computation | custom fusion | bytes 49152 | tf_op jit(solution)/shard_map/gather | solution.py:69
  61.4 8.2 %psum.49 = f32[4096]{0:T(1024)S(1)} all-reduce(f32[4096]{0:T(1024)S(1)} %gather_fusion), channel_id=1, replica_groups=mesh['mem'=2,'gy'=4,'gx'=4] {'mem'}, use_global_device_ids=true, to_apply=%region_2.0 | all-reduce | flops 4096 | bytes 32768 | tf_op jit(solution)/shard_map/psum | solution.py:48
  69.7 22.0 %scatter_custom_fusion = f32[81920]{0:T(1024)S(1)} fusion(s32[4096]{0:T(1024)S(1)} %bitcast.71, f32[4096]{0:T(1024)S(1)} %get-tuple-element.12, f32[]{:T(128)} %constant.11.clone.1), kind=kCustom, calls=%fused_computation.117 | custom fusion | flops 4096 | bytes 327684 | tf_op jit(solution)/shard_map/scatter-add | solution.py:78
  111.4 6.1 %fusion.30 = f32[2,16,16,128]{3,2,1,0:T(8,128)S(1)} fusion(f32[2,16,16,132]{3,2,1,0:T(8,128)S(1)} %get-tuple-element.27, f32[2,16,16,132]{3,2,1,0:T(8,128)S(1)} %get-tuple-element.26, f32[]{:T(128)} %bitcast.12, f32[]{:T(128)} %bitcast.11, f32[]{:T(128)} %bitcast.10, f32[]{:T(128)} %bitcast.9, f32[]{:T(128)} %bitcast.8, f32[]{:T(128)} %bitcast.7, ...), kind=kLoop, calls=%fused_computation.77 | loop fusion | flops 1245184 | bytes 2621476 | tf_op jit(solution)/shard_map/add | solution.py:35
  117.5 6.4 %multiply_reduce_fusion.1 = (f32[]{:T(128)}, f32[2,16,8,128]{3,2,1,0:T(8,128)S(1)}) fusion(f32[2,16,8,128]{3,2,1,0:T(8,128)S(1)} %copy-done.1, f32[2,16,16,128]{3,2,1,0:T(8,128)S(1)} %fusion.30, f32[]{:T(128)} %bitcast.12, f32[]{:T(128)} %bitcast.11, f32[]{:T(128)} %bitcast.10, f32[]{:T(128)} %bitcast.9, f32[]{:T(128)} %bitcast.8, f32[]{:T(128)} %bitcast.7, ...), kind=kLoop, calls=%fused_computation.210 | loop fusion | flops 655359 | bytes 1441832 | tf_op jit(solution)/shard_map/reduce_sum | solution.py:82
  133.8 5.2 %collective-permute-start.10 = (f32[2,16,16,4]{3,2,1,0:T(8,128)S(1)}, f32[2,16,16,4]{3,2,1,0:T(8,128)S(1)}, u32[]{:S(2)}, u32[]{:S(2)}) collective-permute-start(f32[2,16,16,4]{3,2,1,0:T(8,128)S(1)} %get-tuple-element.24), channel_id=1, source_target_pairs={{0,1},{1,2},{2,3},{4,5},{5,6},{6,7},{8,9},{9,10},{10,11},{12,13},{... | collective-permute-start | bytes 24584 | tf_op jit(solution)/shard_map/ppermute | solution.py:19
  143.6 6.1 %fusion.22 = f32[2,16,16,128]{3,2,1,0:T(8,128)S(1)} fusion(f32[2,16,16,132]{3,2,1,0:T(8,128)S(1)} %get-tuple-element.23, f32[2,16,16,132]{3,2,1,0:T(8,128)S(1)} %get-tuple-element.22, f32[]{:T(128)} %bitcast.12, f32[]{:T(128)} %bitcast.11, f32[]{:T(128)} %bitcast.10, f32[]{:T(128)} %bitcast.9, f32[]{:T(128)} %bitcast.8, f32[]{:T(128)} %bitcast.7, ...), kind=kLoop, calls=%fused_computation.61 | loop fusion | flops 1245184 | bytes 2621476 | tf_op jit(solution)/shard_map/add | solution.py:35
  149.7 5.7 %fusion.67 = f32[2,16,8,128]{3,2,1,0:T(8,128)S(1)} fusion(f32[2,16,16,128]{3,2,1,0:T(8,128)S(1)} %fusion.22, f32[]{:T(128)} %bitcast.12, f32[]{:T(128)} %bitcast.11, f32[]{:T(128)} %bitcast.10, f32[]{:T(128)} %bitcast.9, f32[]{:T(128)} %bitcast.8, f32[]{:T(128)} %bitcast.7, f32[]{:T(128)} %bitcast.6, f32[]{:T(128)} %bitcast.5, f32[]{:T(128)} %bitcast.4), kind=kLoop, calls=%fused_computation.155 | loop fusion | flops 557056 | bytes 1310756 | tf_op jit(solution)/shard_map/add | solution.py:36
  155.5 23.0 %gather_fusion.1 = f32[4096]{0:T(1024)S(1)} fusion(f32[81920]{0:T(1024)S(1)} %bitcast.64, s32[4096]{0:T(1024)S(1)} %broadcast_clamp_fusion), kind=kCustom, calls=%fused_computation.1 | custom fusion | bytes 49152 | tf_op jit(solution)/shard_map/gather | solution.py:84
  178.6 7.2 %psum.51 = f32[4096]{0:T(1024)S(1)} all-reduce(f32[4096]{0:T(1024)S(1)} %gather_fusion.1), channel_id=1, replica_groups=mesh['mem'=2,'gy'=4,'gx'=4] {'mem'}, use_global_device_ids=true, to_apply=%region_8.9 | all-reduce | flops 4096 | bytes 32768 | tf_op jit(solution)/shard_map/psum | solution.py:48
  186.4 41.9 %all-reduce.1 = (f32[]{:T(128)}, f32[]{:T(128)}) all-reduce(f32[]{:T(128)} %get-tuple-element.10, f32[]{:T(128)} %fusion.93), channel_id=1, replica_groups=mesh['mem'=2,'gy'=4,'gx'=4] {'mem','gy','gx'}, use_global_device_ids=true, to_apply=%region_6.7 | all-reduce | flops 2 | bytes 16 | tf_op jit(solution)/shard_map/psum | solution.py:52
  230.2 22.0 %scatter_custom_fusion.1 = f32[81920]{0:T(1024)S(1)} fusion(s32[4096]{0:T(1024)S(1)} %bitcast.72, f32[4096]{0:T(1024)S(1)} %get-tuple-element.8, f32[]{:T(128)} %constant.11.clone.1), kind=kCustom, calls=%fused_computation.115 | custom fusion | flops 4096 | bytes 327684 | tf_op jit(solution)/shard_map/scatter-add | solution.py:78
  270.1 6.1 %fusion.14 = f32[2,16,16,128]{3,2,1,0:T(8,128)S(1)} fusion(f32[2,16,16,132]{3,2,1,0:T(8,128)S(1)} %get-tuple-element.19, f32[2,16,16,132]{3,2,1,0:T(8,128)S(1)} %get-tuple-element.18, f32[]{:T(128)} %bitcast.12, f32[]{:T(128)} %bitcast.11, f32[]{:T(128)} %bitcast.10, f32[]{:T(128)} %bitcast.9, f32[]{:T(128)} %bitcast.8, f32[]{:T(128)} %bitcast.7, ...), kind=kLoop, calls=%fused_computation.45 | loop fusion | flops 1245184 | bytes 2621476 | tf_op jit(solution)/shard_map/add | solution.py:35
  276.3 6.4 %multiply_reduce_fusion = (f32[]{:T(128)}, f32[2,16,8,128]{3,2,1,0:T(8,128)S(1)}) fusion(f32[2,16,16,128]{3,2,1,0:T(8,128)S(1)} %fusion.14, f32[]{:T(128)} %bitcast.12, f32[]{:T(128)} %bitcast.11, f32[]{:T(128)} %bitcast.10, f32[]{:T(128)} %bitcast.9, f32[]{:T(128)} %bitcast.8, f32[]{:T(128)} %bitcast.7, f32[]{:T(128)} %bitcast.6, f32[]{:T(128)} %bitcast.5, ...), kind=kLoop, calls=%fused_computation.208 | loop fusion | flops 720895 | bytes 1572908 | tf_op jit(solution)/shard_map/reduce_sum | solution.py:82
  291.6 5.2 %collective-permute-start.18 = (f32[2,16,16,4]{3,2,1,0:T(8,128)S(1)}, f32[2,16,16,4]{3,2,1,0:T(8,128)S(1)}, u32[]{:S(2)}, u32[]{:S(2)}) collective-permute-start(f32[2,16,16,4]{3,2,1,0:T(8,128)S(1)} %get-tuple-element.16), channel_id=1, source_target_pairs={{0,1},{1,2},{2,3},{4,5},{5,6},{6,7},{8,9},{9,10},{10,11},{12,13},{... | collective-permute-start | bytes 24584 | tf_op jit(solution)/shard_map/ppermute | solution.py:19
  301.4 6.1 %fusion.6 = f32[2,16,16,128]{3,2,1,0:T(8,128)S(1)} fusion(f32[2,16,16,132]{3,2,1,0:T(8,128)S(1)} %get-tuple-element.15, f32[2,16,16,132]{3,2,1,0:T(8,128)S(1)} %get-tuple-element.14, f32[]{:T(128)} %bitcast.12, f32[]{:T(128)} %bitcast.11, f32[]{:T(128)} %bitcast.10, f32[]{:T(128)} %bitcast.9, f32[]{:T(128)} %bitcast.8, f32[]{:T(128)} %bitcast.7, f32[]{:T(128)} %bitcast.6, ...), kind=kLoop, calls=%fused_computation.29 | loop fusion | flops 1245184 | bytes 2621476 | tf_op jit(solution)/shard_map/add | solution.py:35
  307.6 5.7 %fusion.50 = f32[2,16,8,128]{3,2,1,0:T(8,128)S(1)} fusion(f32[2,16,16,128]{3,2,1,0:T(8,128)S(1)} %fusion.6, f32[]{:T(128)} %bitcast.12, f32[]{:T(128)} %bitcast.11, f32[]{:T(128)} %bitcast.10, f32[]{:T(128)} %bitcast.9, f32[]{:T(128)} %bitcast.8, f32[]{:T(128)} %bitcast.7, f32[]{:T(128)} %bitcast.6, f32[]{:T(128)} %bitcast.5, f32[]{:T(128)} %bitcast.4), kind=kLoop, calls=%fused_computation.120 | loop fusion | flops 557056 | bytes 1310756 | tf_op jit(solution)/shard_map/add | solution.py:36
  313.4 23.0 %gather_fusion.2 = f32[4096]{0:T(1024)S(1)} fusion(f32[81920]{0:T(1024)S(1)} %bitcast.62, s32[4096]{0:T(1024)S(1)} %broadcast_clamp_fusion), kind=kCustom, calls=%fused_computation.2 | custom fusion | bytes 49152 | tf_op jit(solution)/shard_map/gather | solution.py:84
  336.4 7.4 %psum.54 = f32[4096]{0:T(1024)S(1)} all-reduce(f32[4096]{0:T(1024)S(1)} %gather_fusion.2), channel_id=1, replica_groups=mesh['mem'=2,'gy'=4,'gx'=4] {'mem'}, use_global_device_ids=true, to_apply=%region_16.17 | all-reduce | flops 4096 | bytes 32768 | tf_op jit(solution)/shard_map/psum | solution.py:48
  344.5 41.6 %all-reduce = (f32[]{:T(128)}, f32[]{:T(128)}) all-reduce(f32[]{:T(128)} %get-tuple-element.6, f32[]{:T(128)} %fusion.95), channel_id=1, replica_groups=mesh['mem'=2,'gy'=4,'gx'=4] {'mem','gy','gx'}, use_global_device_ids=true, to_apply=%region_14.15 | all-reduce | flops 2 | bytes 16 | tf_op jit(solution)/shard_map/psum | solution.py:52
  388.0 6.0 %multiply_subtract_fusion.1 = f32[2,16,8,128]{3,2,1,0:T(8,128)S(1)} fusion(f32[]{:T(128)S(6)} %div.16, f32[]{:T(128)S(6)} %div.15, f32[2,16,16,128]{3,2,1,0:T(8,128)S(1)} %fusion.6, f32[]{:T(128)} %bitcast.12, f32[]{:T(128)} %bitcast.11, f32[]{:T(128)} %bitcast.10, f32[]{:T(128)} %bitcast.9, f32[]{:T(128)} %bitcast.8, f32[]{:T(128)} %bitcast.7, f32[]{:T(128)} %bitcast.6, ...), kind=kLoop, calls=%fused_computation.207 | loop fusion | flops 1802240 | bytes 3670060 | tf_op jit(solution)/shard_map/sub | solution.py:89
  395.6 12.0 %reduce-scatter.5.cloned.1.call-done = f32[8,5120]{1,0:T(8,128)} async-done(((f32[16,5120]{1,0:T(8,128)}), f32[8,5120]{1,0:T(8,128)}) %reduce-scatter.5.cloned.1.call-update) | async-done | bytes 163856
  (93 shorter events, 89.3 us)
Async XLA Ops:
  7.2 12.2 %copy-start.1 = (f32[2,16,8,128]{3,2,1,0:T(8,128)S(1)}, f32[2,16,8,128]{3,2,1,0:T(8,128)}, u32[]{:S(2)}) copy-start(f32[2,16,8,128]{3,2,1,0:T(8,128)} %param.8) | copy-start | bytes 393220
  7.2 400.4 %reduce-scatter.5.cloned.1.call-start = ((), (), s32[]{:S(2)}) async-start(), calls=%async_computation.1 | async-start | bytes 491520
  8.2 7.6 %collective-permute-start = (f32[2,16,4,128]{3,2,1,0:T(4,128)S(1)}, f32[2,16,4,128]{3,2,1,0:T(4,128)S(1)}, u32[]{:S(2)}, u32[]{:S(2)}) collective-permute-start(f32[2,16,4,128]{3,2,1,0:T(4,128)S(1)} %get-tuple-element.42), channel_id=1, source_target_pairs={{0,4},{4,8},{8,12},{1,5},{5,9},{9,13},{2,6},{6,10},{10,14},{3,7},{... | collective-permute-start | bytes 196616 | tf_op jit(solution)/shard_map/ppermute | solution.py:19
  13.2 6.2 %collective-permute-start.1 = (f32[2,16,4,128]{3,2,1,0:T(4,128)S(1)}, f32[2,16,4,128]{3,2,1,0:T(4,128)S(1)}, u32[]{:S(2)}, u32[]{:S(2)}) collective-permute-start(f32[2,16,4,128]{3,2,1,0:T(4,128)S(1)} %get-tuple-element.43), channel_id=1, source_target_pairs={{4,0},{8,4},{12,8},{5,1},{9,5},{13,9},{6,2},{10,6},{14,10},{7,3},{... | collective-permute-start | bytes 196616 | tf_op jit(solution)/shard_map/ppermute | solution.py:20
  19.6 3.3 collective-permute-start.2
  20.9 5.1 %collective-permute-start.3 = (f32[2,16,16,4]{3,2,1,0:T(8,128)S(1)}, f32[2,16,16,4]{3,2,1,0:T(8,128)S(1)}, u32[]{:S(2)}, u32[]{:S(2)}) collective-permute-start(f32[2,16,16,4]{3,2,1,0:T(8,128)S(1)} %get-tuple-element.33), channel_id=1, source_target_pairs={{1,0},{2,1},{3,2},{5,4},{6,5},{7,6},{9,8},{10,9},{11,10},{13,12},{... | collective-permute-start | bytes 24584 | tf_op jit(solution)/shard_map/ppermute | solution.py:20
  38.4 31.3 %copy-start.6 = (s32[32,128]{1,0:T(8,128)S(1)}, s32[32,128]{1,0:T(8,128)}, u32[]{:S(2)}) copy-start(s32[32,128]{1,0:T(8,128)} %param.11) | copy-start | bytes 49156
  91.8 5.4 %collective-permute-start.4 = (f32[2,16,4,128]{3,2,1,0:T(4,128)S(1)}, f32[2,16,4,128]{3,2,1,0:T(4,128)S(1)}, u32[]{:S(2)}, u32[]{:S(2)}) collective-permute-start(f32[2,16,4,128]{3,2,1,0:T(4,128)S(1)} %get-tuple-element.40), channel_id=1, source_target_pairs={{0,4},{4,8},{8,12},{1,5},{5,9},{9,13},{2,6},{6,10},{10,14},{3,7},{... | collective-permute-start | bytes 196616 | tf_op jit(solution)/shard_map/ppermute | solution.py:19
  95.3 6.2 %collective-permute-start.5 = (f32[2,16,4,128]{3,2,1,0:T(4,128)S(1)}, f32[2,16,4,128]{3,2,1,0:T(4,128)S(1)}, u32[]{:S(2)}, u32[]{:S(2)}) collective-permute-start(f32[2,16,4,128]{3,2,1,0:T(4,128)S(1)} %get-tuple-element.41), channel_id=1, source_target_pairs={{4,0},{8,4},{12,8},{5,1},{9,5},{13,9},{6,2},{10,6},{14,10},{7,3},{... | collective-permute-start | bytes 196616 | tf_op jit(solution)/shard_map/ppermute | solution.py:20
  101.6 4.5 %collective-permute-start.6 = (f32[2,16,16,4]{3,2,1,0:T(8,128)S(1)}, f32[2,16,16,4]{3,2,1,0:T(8,128)S(1)}, u32[]{:S(2)}, u32[]{:S(2)}) collective-permute-start(f32[2,16,16,4]{3,2,1,0:T(8,128)S(1)} %get-tuple-element.28), channel_id=1, source_target_pairs={{0,1},{1,2},{2,3},{4,5},{5,6},{6,7},{8,9},{9,10},{10,11},{12,13},{... | collective-permute-start | bytes 24584 | tf_op jit(solution)/shard_map/ppermute | solution.py:19
  104.8 6.2 %collective-permute-start.7 = (f32[2,16,16,4]{3,2,1,0:T(8,128)S(1)}, f32[2,16,16,4]{3,2,1,0:T(8,128)S(1)}, u32[]{:S(2)}, u32[]{:S(2)}) collective-permute-start(f32[2,16,16,4]{3,2,1,0:T(8,128)S(1)} %get-tuple-element.29), channel_id=1, source_target_pairs={{1,0},{2,1},{3,2},{5,4},{6,5},{7,6},{9,8},{10,9},{11,10},{13,12},{... | collective-permute-start | bytes 24584 | tf_op jit(solution)/shard_map/ppermute | solution.py:20
  124.0 5.4 %collective-permute-start.8 = (f32[2,16,4,128]{3,2,1,0:T(4,128)S(1)}, f32[2,16,4,128]{3,2,1,0:T(4,128)S(1)}, u32[]{:S(2)}, u32[]{:S(2)}) collective-permute-start(f32[2,16,4,128]{3,2,1,0:T(4,128)S(1)} %get-tuple-element.38), channel_id=1, source_target_pairs={{0,4},{4,8},{8,12},{1,5},{5,9},{9,13},{2,6},{6,10},{10,14},{3,7},{... | collective-permute-start | bytes 196616 | tf_op jit(solution)/shard_map/ppermute | solution.py:19
  127.5 6.2 %collective-permute-start.9 = (f32[2,16,4,128]{3,2,1,0:T(4,128)S(1)}, f32[2,16,4,128]{3,2,1,0:T(4,128)S(1)}, u32[]{:S(2)}, u32[]{:S(2)}) collective-permute-start(f32[2,16,4,128]{3,2,1,0:T(4,128)S(1)} %get-tuple-element.39), channel_id=1, source_target_pairs={{4,0},{8,4},{12,8},{5,1},{9,5},{13,9},{6,2},{10,6},{14,10},{7,3},{... | collective-permute-start | bytes 196616 | tf_op jit(solution)/shard_map/ppermute | solution.py:20
  133.8 6.6 %collective-permute-start.10 = (f32[2,16,16,4]{3,2,1,0:T(8,128)S(1)}, f32[2,16,16,4]{3,2,1,0:T(8,128)S(1)}, u32[]{:S(2)}, u32[]{:S(2)}) collective-permute-start(f32[2,16,16,4]{3,2,1,0:T(8,128)S(1)} %get-tuple-element.24), channel_id=1, source_target_pairs={{0,1},{1,2},{2,3},{4,5},{5,6},{6,7},{8,9},{9,10},{10,11},{12,13},{... | collective-permute-start | bytes 24584 | tf_op jit(solution)/shard_map/ppermute | solution.py:19
  139.1 4.2 %collective-permute-start.11 = (f32[2,16,16,4]{3,2,1,0:T(8,128)S(1)}, f32[2,16,16,4]{3,2,1,0:T(8,128)S(1)}, u32[]{:S(2)}, u32[]{:S(2)}) collective-permute-start(f32[2,16,16,4]{3,2,1,0:T(8,128)S(1)} %get-tuple-element.25), channel_id=1, source_target_pairs={{1,0},{2,1},{3,2},{5,4},{6,5},{7,6},{9,8},{10,9},{11,10},{13,12},{... | collective-permute-start | bytes 24584 | tf_op jit(solution)/shard_map/ppermute | solution.py:20
  252.3 5.8 %collective-permute-start.12 = (f32[2,16,4,128]{3,2,1,0:T(4,128)S(1)}, f32[2,16,4,128]{3,2,1,0:T(4,128)S(1)}, u32[]{:S(2)}, u32[]{:S(2)}) collective-permute-start(f32[2,16,4,128]{3,2,1,0:T(4,128)S(1)} %get-tuple-element.36), channel_id=1, source_target_pairs={{0,4},{4,8},{8,12},{1,5},{5,9},{9,13},{2,6},{6,10},{10,14},{3,7},{... | collective-permute-start | bytes 196616 | tf_op jit(solution)/shard_map/ppermute | solution.py:19
  256.2 6.2 %collective-permute-start.13 = (f32[2,16,4,128]{3,2,1,0:T(4,128)S(1)}, f32[2,16,4,128]{3,2,1,0:T(4,128)S(1)}, u32[]{:S(2)}, u32[]{:S(2)}) collective-permute-start(f32[2,16,4,128]{3,2,1,0:T(4,128)S(1)} %get-tuple-element.37), channel_id=1, source_target_pairs={{4,0},{8,4},{12,8},{5,1},{9,5},{13,9},{6,2},{10,6},{14,10},{7,3},{... | collective-permute-start | bytes 196616 | tf_op jit(solution)/shard_map/ppermute | solution.py:20
  262.5 2.6 collective-permute-start.14
  263.9 5.9 %collective-permute-start.15 = (f32[2,16,16,4]{3,2,1,0:T(8,128)S(1)}, f32[2,16,16,4]{3,2,1,0:T(8,128)S(1)}, u32[]{:S(2)}, u32[]{:S(2)}) collective-permute-start(f32[2,16,16,4]{3,2,1,0:T(8,128)S(1)} %get-tuple-element.21), channel_id=1, source_target_pairs={{1,0},{2,1},{3,2},{5,4},{6,5},{7,6},{9,8},{10,9},{11,10},{13,12},{... | collective-permute-start | bytes 24584 | tf_op jit(solution)/shard_map/ppermute | solution.py:20
  282.7 4.5 %collective-permute-start.16 = (f32[2,16,4,128]{3,2,1,0:T(4,128)S(1)}, f32[2,16,4,128]{3,2,1,0:T(4,128)S(1)}, u32[]{:S(2)}, u32[]{:S(2)}) collective-permute-start(f32[2,16,4,128]{3,2,1,0:T(4,128)S(1)} %get-tuple-element.34), channel_id=1, source_target_pairs={{0,4},{4,8},{8,12},{1,5},{5,9},{9,13},{2,6},{6,10},{10,14},{3,7},{... | collective-permute-start | bytes 196616 | tf_op jit(solution)/shard_map/ppermute | solution.py:19
  285.3 6.2 %collective-permute-start.17 = (f32[2,16,4,128]{3,2,1,0:T(4,128)S(1)}, f32[2,16,4,128]{3,2,1,0:T(4,128)S(1)}, u32[]{:S(2)}, u32[]{:S(2)}) collective-permute-start(f32[2,16,4,128]{3,2,1,0:T(4,128)S(1)} %get-tuple-element.35), channel_id=1, source_target_pairs={{4,0},{8,4},{12,8},{5,1},{9,5},{13,9},{6,2},{10,6},{14,10},{7,3},{... | collective-permute-start | bytes 196616 | tf_op jit(solution)/shard_map/ppermute | solution.py:20
  291.6 6.7 %collective-permute-start.18 = (f32[2,16,16,4]{3,2,1,0:T(8,128)S(1)}, f32[2,16,16,4]{3,2,1,0:T(8,128)S(1)}, u32[]{:S(2)}, u32[]{:S(2)}) collective-permute-start(f32[2,16,16,4]{3,2,1,0:T(8,128)S(1)} %get-tuple-element.16), channel_id=1, source_target_pairs={{0,1},{1,2},{2,3},{4,5},{5,6},{6,7},{8,9},{9,10},{10,11},{12,13},{... | collective-permute-start | bytes 24584 | tf_op jit(solution)/shard_map/ppermute | solution.py:19
  296.9 4.2 %collective-permute-start.19 = (f32[2,16,16,4]{3,2,1,0:T(8,128)S(1)}, f32[2,16,16,4]{3,2,1,0:T(8,128)S(1)}, u32[]{:S(2)}, u32[]{:S(2)}) collective-permute-start(f32[2,16,16,4]{3,2,1,0:T(8,128)S(1)} %get-tuple-element.17), channel_id=1, source_target_pairs={{1,0},{2,1},{3,2},{5,4},{6,5},{7,6},{9,8},{10,9},{11,10},{13,12},{... | collective-permute-start | bytes 24584 | tf_op jit(solution)/shard_map/ppermute | solution.py:20
  394.9 12.7 %copy-start.3 = (f32[5,8,8,128]{3,2,1,0:T(8,128)S(1)}, f32[5,8,8,128]{3,2,1,0:T(8,128)}, u32[]{:S(2)}) copy-start(f32[5,8,8,128]{3,2,1,0:T(8,128)} %param.9) | copy-start | bytes 491524
  (4 other events, 30.1 us)
Sparse Core Ops, SparseCore 0:
  395.0 12.5 reduce-scatter.4
where the time goes:
time: 418 us; the launch traced here: 416 us
  other arithmetic  118 us (28%)
  blocking collectives  106 us (25%)
  local copies, waits for them, and re-layouts  72.4 us (17%)
  waiting for transfers between devices  53.2 us (13%)
  starting transfers between devices  47.9 us (11%)
  between operations  18.2 us (4%)
    psum x2, blocking collectives, step_size(): lax.psum((grad_local, curv_local), ('mem', 'gy', 'gx'))  83.5 us
    gather x2, local copies, waits for them, and re-layouts, per_device(): member_sum(perturbations, smooth_grad).reshape(-1)[flat_cell]  46.1 us
    scatter-add x2, other arithmetic, per_device(): adjoint = jnp.zeros((partial_value.size,), jnp.float32).at[flat_cell].add...  44 us
    ppermute x10, waiting for transfers between devices, extended(): after = lax.ppermute(initial, axis, down)  38.9 us
    ppermute x10, starting transfers between devices, extended(): before = lax.ppermute(last, axis, up)  34.7 us
    add x5, other arithmetic, smooth(): sum((weights[offset] * padded[..., :, offset:offset + cols] for offset in...  30.6 us
    gather x1, local copies, waits for them, and re-layouts, per_device(): seen_inc = seen_total(partial_value.reshape(-1)[flat_cell])  23 us
    psum x3, blocking collectives, seen_total(): return lax.psum(values, 'mem')  22.8 us
  transfers between devices with their start and end apart: 21, of which 15 were waited for; matrix products, arithmetic and copies ran while one was open for 1% of the time, Pallas kernels for 0%

commit v1 on v0

v1 whole, which is shorter than its diff:
```python
import functools
import math

import jax
import jax.numpy as jnp
from jax import lax
from jax.experimental import pallas as pl
from jax.experimental.pallas import tpu as pltpu
from jax.sharding import PartitionSpec as P

ITERS = 2
RADIUS = 4
RAW = [math.exp(-o * o / 8.0) for o in range(-RADIUS, RADIUS + 1)]
TAPS = [r / sum(RAW) for r in RAW]
HALO = 2 * RADIUS
F32 = jnp.float32
BF16 = jnp.bfloat16
EXACT = lax.Precision.HIGHEST
CHUNK = 4


def iota(shape, dim):
    return lax.broadcasted_iota(jnp.int32, shape, dim)


def over(k, n):
    return lax.shift_right_logical(k, n.bit_length() - 1) if n & (n - 1) == 0 else k // n


def rem(k, n):
    return k & (n - 1) if n & (n - 1) == 0 else k % n


def tap(d):
    d = jnp.abs(d)
    value = jnp.zeros(d.shape, F32)
    for o in range(RADIUS + 1):
        value = jnp.where(d == o, TAPS[RADIUS + o], value)
    return value


def exact_dot(a, b):
    return jnp.dot(a, b, precision=EXACT, preferred_element_type=F32)


def halves(f32):
    high = f32.astype(BF16)
    low = (f32 - high.astype(F32)).astype(BF16)
    return high, low


def split_x(field):
    half = field.shape[0] // 2
    return jnp.concatenate([field[:half], field[half:]], axis=1)


def join_x(field):
    half = field.shape[1] // 2
    return jnp.concatenate([field[:, :half], field[:, half:]], axis=0)


def onehot_rows(index, rows):
    wide = jnp.broadcast_to(index, (rows, index.shape[1]))
    return jnp.where(iota(wide.shape, 0) == wide, 1.0, 0.0).astype(BF16)


def cell_row(cell, zy, tx):
    return over(rem(cell, tx), tx // 2) * zy + rem(over(cell, tx), zy)


def cell_low(cell, tx):
    return rem(cell, tx // 2)


def chunk_of(ref, j):
    return jnp.concatenate([ref[j + i : j + i + 1, :] for i in range(CHUNK)], axis=1)


def store_chunk(ref, j, row):
    wide = row.shape[1] // CHUNK
    for i in range(CHUNK):
        ref[j + i : j + i + 1, :] = row[:, i * wide : (i + 1) * wide]


def y_geometry(k, zy, ty, gy, ngy):
    tile, at = over(k, zy), rem(k, zy)
    side = jnp.where(rem(gy, 2) == 0, 1, -1)
    moved = gy + jnp.where(tile == 0, 0, jnp.where(tile == 1, side, -side))
    return over(at, ty), moved * ty + rem(at, ty), (moved >= 0) & (moved < ngy)


def prep_kernel(pert, cell, flag, innov, prec, info, table):
    members, variables, zy, tx = pert.shape
    half = tx // 2
    for m in range(members):
        for v in range(variables):
            block = split_x(pert[m, v].astype(F32).T)
            at = (m * variables + v) * half
            table[at : at + half, :] = block.astype(BF16)
    for j in range(0, cell.shape[0], CHUNK):
        k = chunk_of(cell, j)
        hot = onehot_rows(cell_row(k, zy, tx), 2 * zy)
        found = jnp.dot(table[...], hot, preferred_element_type=F32)
        want = over(k, tx * zy) * half + cell_low(k, tx)
        rows = variables * half
        mask = iota((rows, k.shape[1]), 0) == jnp.broadcast_to(want, (rows, k.shape[1]))
        for m in range(members):
            mine = jnp.where(mask, found[m * rows : (m + 1) * rows], 0.0)
            store_chunk(info.at[3 + m], j, jnp.sum(mine, axis=0, keepdims=True))
    info[0] = cell[...].astype(F32)
    info[1] = jnp.where(flag[...] == 1, -prec[...], prec[...])
    info[2] = innov[...]


def matrices_kernel(ty, pos, ky, kx):
    wide, zy = ky.shape[0], ky.shape[1] // 2
    tx = kx.shape[1]
    gy, ngy, gx, ngx = pos[0], pos[1], pos[2], pos[3]

    def along_y(shape):
        zs, ys, oks = y_geometry(iota(shape, 0), zy, ty, gy, ngy)
        zt, yt, okt = y_geometry(iota(shape, 1), zy, ty, gy, ngy)
        return jnp.where((zs == zt) & oks & okt, tap(ys - yt), 0.0)

    once = along_y((wide, zy))
    ky[:, :zy] = once
    ky[:, zy:] = exact_dot(along_y((wide, wide)), once)

    def x_of(k):
        at = jnp.where(k < tx, k, jnp.where(k < tx + HALO, k - tx - HALO, k - HALO))
        full = gx * tx + at
        return at, (full >= 0) & (full < ngx * tx)

    def along_x(shape):
        xt, okt = x_of(iota(shape, 0))
        xs, oks = x_of(iota(shape, 1))
        return jnp.where(oks & okt, tap(xs - xt), 0.0)

    long = tx + 2 * HALO
    kx[0] = along_x((tx, long))
    kx[1] = exact_dot(along_x((tx, long)), along_x((long, long)))


def start_kernel(own, a, b, ky, y1, right, left):
    members, zy, tx = own.shape
    for m in range(members):
        wide = jnp.concatenate([own[m].T, a[m].T, b[m].T], axis=1)
        out = exact_dot(wide, ky[:, :zy])
        y1[m] = out
        right[m] = out[tx - HALO :]
        left[m] = out[:HALO]


def x_smooth(matrix, fields, lefts, rights):
    wide = [jnp.concatenate([f, l, r], axis=0) for f, l, r in zip(fields, lefts, rights)]
    out = exact_dot(matrix, jnp.concatenate(wide, axis=1))
    zy = fields[0].shape[1]
    return [out[:, i * zy : (i + 1) * zy] for i in range(len(fields))]


def gather_at(fields, info, seen, tx, zy):
    members, half = len(fields), tx // 2
    parts = [halves(split_x(f)) for f in fields]
    stacked = jnp.concatenate([p[0] for p in parts] + [p[1] for p in parts], axis=0)
    rows = members * half
    for j in range(0, info.shape[1], CHUNK):
        k = chunk_of(info.at[0], j).astype(jnp.int32)
        hot = onehot_rows(cell_row(k, zy, tx), 2 * zy)
        found = jnp.dot(stacked, hot, preferred_element_type=F32)
        low = jnp.broadcast_to(cell_low(k, tx), (half, k.shape[1]))
        mask = iota(low.shape, 0) == low
        total = None
        for m in range(members):
            both = found[m * half : (m + 1) * half] + found[rows + m * half : rows + (m + 1) * half]
            term = jnp.where(mask, both, 0.0) * jnp.broadcast_to(chunk_of(info.at[3 + m], j), both.shape)
            total = term if total is None else total + term
        store_chunk(seen, j, jnp.sum(total, axis=0, keepdims=True))


def first_seen_kernel(y1, from_left, from_right, v, kx, info, smoothed, control, seen):
    members, tx, zy = y1.shape
    outs = x_smooth(kx[0], [y1[m] for m in range(members)], [from_left[m] for m in range(members)], [from_right[m] for m in range(members)])
    for m in range(members):
        smoothed[m] = outs[m]
        control[m] = v[m].T
    gather_at(outs, info, seen, tx, zy)


def step_rows(sums):
    total = jnp.sum(sums, axis=0, keepdims=True)
    lane = iota(total.shape, 1)
    g = jnp.sum(jnp.where(lane == 0, total, 0.0), axis=1, keepdims=True)
    c = jnp.sum(jnp.where(lane == 1, total, 0.0), axis=1, keepdims=True)
    return g / (g + c)


def scatter_kernel(has_step, tx, zy, *refs):
    infos, incs = refs[0:3], refs[3:6]
    refs = refs[6:]
    if has_step:
        steps, sums = refs[0:3], refs[3]
        refs = refs[4:]
        step = step_rows(sums[...])
    ky, y1, y2, right, left, weights, inc_out, vals = refs
    members = infos[0].shape[0] - 3
    half = tx // 2
    tiles = []
    for t in range(3):
        info = infos[t]
        inc = incs[t][...]
        if has_step:
            inc = inc - step * steps[t][...]
        misfit = inc - info[2]
        prec = info[1]
        weight = jnp.where(prec < 0, 1.0 / jnp.sqrt(1.0 + misfit * misfit), 1.0)
        pw = jnp.abs(prec) * weight
        q = pw * misfit
        if t == 0:
            weights[...] = pw
            inc_out[...] = inc
        for m in range(members):
            val = info[3 + m] * q
            high = val.astype(BF16).astype(F32)
            vals[2 * m] = high
            vals[2 * m + 1] = val - high
        acc = None
        for j in range(0, info.shape[1], CHUNK):
            k = chunk_of(info.at[0], j).astype(jnp.int32)
            hot = onehot_rows(cell_row(k, zy, tx), 2 * zy)
            low = jnp.broadcast_to(cell_low(k, tx), (half, k.shape[1]))
            mask = iota(low.shape, 0) == low
            rows = []
            for i in range(2 * members):
                row = jnp.broadcast_to(chunk_of(vals.at[i], j), low.shape)
                rows.append(jnp.where(mask, row, 0.0).astype(BF16))
            part = lax.dot_general(jnp.concatenate(rows, axis=0), hot, (((1,), (1,)), ((), ())), preferred_element_type=F32)
            acc = part if acc is None else acc + part
        fields = []
        for m in range(members):
            at = 2 * m * half
            fields.append(join_x(acc[at : at + half] + acc[at + half : at + 2 * half]))
        tiles.append(jnp.concatenate(fields, axis=0))
    out = exact_dot(jnp.concatenate(tiles, axis=1), ky[...])
    for m in range(members):
        for i, y in enumerate((y1, y2)):
            field = out[m * tx : (m + 1) * tx, i * zy : (i + 1) * zy]
            y[m] = field
            right[i, m] = field[tx - HALO :]
            left[i, m] = field[:HALO]


def gather_kernel(has_step, *refs):
    y1, y2, from_left, from_right, kx, info, control, smoothed = refs[:8]
    refs = refs[8:]
    members, tx, zy = y1.shape
    if has_step:
        old_grad, old_smooth, sums, new_control, new_smoothed = refs[:5]
        refs = refs[5:]
        step = step_rows(sums[...])
    grad_out, smooth_out, seen, gnorm = refs
    each = range(members)
    once = x_smooth(kx[0], [y1[m] for m in each], [from_left[0, m] for m in each], [from_right[0, m] for m in each])
    twice = x_smooth(kx[1], [y2[m] for m in each], [from_left[1, m] for m in each], [from_right[1, m] for m in each])
    squares = None
    outs = []
    for m in each:
        v, s = control[m], smoothed[m]
        if has_step:
            v = v - step * old_grad[m]
            s = s - step * old_smooth[m]
            new_control[m] = v
            new_smoothed[m] = s
        grad = v + once[m]
        smooth_grad = s + twice[m]
        grad_out[m] = grad
        smooth_out[m] = smooth_grad
        outs.append(smooth_grad)
        part = jnp.sum(grad * grad, axis=0, keepdims=True)
        squares = part if squares is None else squares + part
    gnorm[...] = squares
    gather_at(outs, info, seen, tx, zy)


def curv_kernel(pos, mine, other, weights, gnorm, seen, sums):
    total = mine[...] + other[...]
    seen[...] = total
    counted = jnp.where(pos[4] == 0, 1.0, 0.0)
    c = jnp.sum(jnp.sum(weights[...] * total * total, axis=0, keepdims=True), axis=1, keepdims=True) * counted
    g = jnp.sum(gnorm[...], axis=1, keepdims=True)
    lane = iota(sums.shape, 1)
    sums[...] = jnp.where(lane == 0, g, jnp.where(lane == 1, c, 0.0))


def final_kernel(pos, sums, control, smoothed, grad, smooth_grad, pert, control_out, keep, send):
    members, tx, zy = control.shape
    variables = pert.shape[1]
    step = step_rows(sums[...])
    fields = []
    for m in range(members):
        control_out[m] = (control[m] - step * grad[m]).T
        fields.append((smoothed[m] - step * smooth_grad[m]).T)
    rows = keep.shape[1]
    for v in range(variables):
        inc = None
        for m in range(members):
            term = pert[m, v].astype(F32) * fields[m]
            inc = term if inc is None else inc + term
        low, high = inc[:rows], inc[rows:]
        first = pos[4] == 0
        keep[v] = jnp.where(first, low, high)
        send[v] = jnp.where(first, high, low)


VMEM = pl.BlockSpec(memory_space=pltpu.VMEM)
SMEM = pl.BlockSpec(memory_space=pltpu.SMEM)


def call(kernel, ins, outs, scratch=(), smem=0, us=3.0, name=None):
    shapes = [jax.ShapeDtypeStruct(s, F32) for s in outs]
    return pl.pallas_call(
        kernel,
        out_shape=shapes,
        in_specs=[SMEM] * smem + [VMEM] * (len(ins) - smem),
        out_specs=[VMEM] * len(outs),
        scratch_shapes=list(scratch),
        cost_estimate=pl.CostEstimate(flops=int(us * 1e9), bytes_accessed=1 << 20, transcendentals=0),
        name=name,
    )(*ins)


def pairs_a(n):
    return [(i, i ^ 1 if i ^ 1 < n else i) for i in range(n)]


def pairs_b(n):
    to = [((i + 1) ^ 1) - 1 for i in range(n)]
    return [(i, t if 0 <= t < n else i) for i, t in enumerate(to)]


def both_y(value):
    n = lax.axis_size("gy")
    return lax.ppermute(value, "gy", pairs_a(n)), lax.ppermute(value, "gy", pairs_b(n))


def both_x(right, left):
    n = lax.axis_size("gx")
    up = [(i, (i + 1) % n) for i in range(n)]
    down = [(j, i) for i, j in up]
    return lax.ppermute(right, "gx", up), lax.ppermute(left, "gx", down)


def other_members(value):
    n = lax.axis_size("mem")
    if n == 2:
        return lax.ppermute(value, "mem", [(0, 1), (1, 0)])
    return lax.psum(value, "mem") - value


def per_device(perturbations, control, background, obs_cell, huber_flag, innovation, precision):
    members, variables, nz, ty, tx = perturbations.shape
    zy = nz * ty
    obs = obs_cell.shape
    axes = ("mem", "gy", "gx")
    pos = jnp.stack([lax.axis_index("gy"), lax.axis_size("gy"), lax.axis_index("gx"), lax.axis_size("gx"), lax.axis_index("mem")]).astype(jnp.int32)
    n_all = math.prod(lax.axis_size(a) for a in axes)
    pert = perturbations.reshape(members, variables, zy, tx)
    field = (members, tx, zy)
    strip = (members, HALO, zy)

    own = control.reshape(members, zy, tx)
    above, below = both_y(own)
    (info,) = call(
        prep_kernel,
        [pert, obs_cell, huber_flag, innovation, precision],
        [(3 + members,) + obs],
        [pltpu.VMEM((members * variables * tx // 2, 2 * zy), BF16)],
        us=6.0,
        name="prep",
    )
    ky, kx = call(functools.partial(matrices_kernel, ty), [pos], [(3 * zy, 2 * zy), (2, tx, tx + 2 * HALO)], smem=1, us=3.0, name="matrices")
    y1, right, left = call(start_kernel, [own, above, below, ky], [field, strip, strip], us=1.5, name="start")
    from_left, from_right = both_x(right, left)
    smoothed, state, seen_part = call(first_seen_kernel, [y1, from_left, from_right, own, kx, info], [field, field, obs], us=3.0, name="first_seen")
    inc = seen_part + other_members(seen_part)
    packed = jnp.concatenate([info, inc[None]], axis=0)
    packs = (packed,) + both_y(packed)
    infos = [p[:-1] for p in packs]
    incs = [p[-1] for p in packs]
    steps, sums, grad, smooth_grad = None, None, None, None
    double = (2,) + strip
    for iteration in range(ITERS):
        later = iteration > 0
        ins = infos + incs + (steps + [sums] if later else []) + [ky]
        y1, y2, right, left, weights, own_inc = call(
            functools.partial(scatter_kernel, later, tx, zy),
            ins,
            [field, field, double, double, obs, obs],
            [pltpu.VMEM((2 * members,) + obs, F32)],
            us=6.0,
            name="scatter",
        )
        from_left, from_right = both_x(right, left)
        ins = [y1, y2, from_left, from_right, kx, info, state, smoothed]
        outs = [field, field, obs, (1, zy)]
        if later:
            ins += [grad, smooth_grad, sums]
            outs = [field, field] + outs
        result = call(functools.partial(gather_kernel, later), ins, outs, us=4.0, name="gather")
        if later:
            state, smoothed = result[:2]
        grad, smooth_grad, seen_part, gnorm = result[-4:]
        seen_step, to_all = call(curv_kernel, [pos, seen_part, other_members(seen_part), weights, gnorm], [obs, (n_all, 128)], smem=1, us=1.0, name="curv")
        if iteration + 1 < ITERS:
            steps = [seen_step, *both_y(seen_step)]
        sums = lax.all_to_all(to_all, axes, 0, 0, tiled=True)
    n_mem = lax.axis_size("mem")
    part = (variables, zy // 2, tx)
    if n_mem == 2:
        control_out, keep, send = call(final_kernel, [pos, sums, state, smoothed, grad, smooth_grad, pert], [(members, zy, tx), part, part], smem=1, us=3.0, name="final")
        mine = keep + lax.ppermute(send, "mem", [(0, 1), (1, 0)])
    else:
        control_out, low, high = call(final_kernel, [pos * 0, sums, state, smoothed, grad, smooth_grad, pert], [(members, zy, tx), part, part], smem=1, us=3.0, name="final")
        mine = lax.psum_scatter(jnp.concatenate([low, high], axis=1), "mem", scatter_dimension=1, tiled=True)
    return background + mine.reshape(background.shape), control_out.reshape(control.shape)


def solution(mesh):
    in_specs = (
        P("mem", None, None, "gy", "gx"),
        P("mem", None, "gy", "gx"),
        P(None, "mem", "gy", "gx"),
        P("gy", "gx"),
        P("gy", "gx"),
        P("gy", "gx"),
        P("gy", "gx"),
    )
    out_specs = (P(None, "mem", "gy", "gx"), P("mem", None, "gy", "gx"))
    return jax.shard_map(per_device, mesh=mesh, in_specs=in_specs, out_specs=out_specs, check_vma=False)
```

time: 418 us -> 108 us (0.26)
  other arithmetic: 118 us -> 2.35 us
  blocking collectives: 106 us -> 11.3 us
  local copies, waits for them, and re-layouts: 72.4 us -> 7.91 us
  waiting for transfers between devices: 53.2 us -> 19.7 us
  Pallas kernels: 0 us -> 33.4 us
  between operations: 18.2 us -> 0.73 us
  starting transfers between devices: 47.9 us -> 31.9 us
    psum x5 -> x0, blocking collectives: 106 us -> none  [the longest x2 83.5 us: step_size(): lax.psum((grad_local, curv_local), ('mem', 'gy', 'gx'))]
    gather x3 -> x0, local copies, waits for them, and re-layouts: 69.1 us -> none  [the longest x2 46.1 us: per_device(): member_sum(perturbations, smooth_grad).reshape(-1)[flat_cell]]
    add x9 -> x2, other arithmetic: 49.5 us -> 2.34 us  [the longest x1 1.62 us: per_device(): background + mine.reshape(background.shape)]
    scatter-add x2 -> x0, other arithmetic: 44 us -> none  [per_device(): adjoint = jnp.zeros((partial_value.size,), jnp.float32).at[flat_cell].add...]
    pallas_call x0 -> x11, Pallas kernels: none -> 33.4 us  [call(): pl.pallas_call(kernel, out_shape=shapes, in_specs=[SMEM] * smem + [VMEM]...]
    ppermute x20 -> x16, waiting for transfers between devices: 41.2 us -> 19.6 us  [the longest x3 7.34 us: other_members(): return lax.ppermute(value, 'mem', [(0, 1), (1, 0)])]
    ppermute x20 -> x16, starting transfers between devices: 47.8 us -> 26.6 us  [the longest x3 13.1 us: both_y(): lax.ppermute(value, 'gy', pairs_a(n))]
    reduce_sum x11 -> x0, other arithmetic: 15.2 us -> none  [the longest x2 12.8 us: per_device(): grad_local = jnp.sum(grad * grad)]
  transfers between devices with their start and end apart: 21 -> 17, of which waited for: 15 -> 9; matrix products, arithmetic and copies ran while one was open for 1% -> 2% of each run, Pallas kernels for 0% -> 6%
where the time goes in v1:
time: 108 us; the launch traced here: 107 us
  Pallas kernels  33.4 us (31%)
  starting transfers between devices  31.9 us (30%)
  waiting for transfers between devices  19.7 us (18%)
  blocking collectives  11.3 us (10%)
  local copies, waits for them, and re-layouts  7.91 us (7%)
  other arithmetic  2.35 us (2%)
    pallas_call x11, Pallas kernels, call(): pl.pallas_call(kernel, out_shape=shapes, in_specs=[SMEM] * smem + [VMEM]...  33.4 us
    ppermute x3, starting transfers between devices, both_y(): lax.ppermute(value, 'gy', pairs_a(n))  13.1 us
    all_to_all x1, blocking collectives, per_device(): sums = lax.all_to_all(to_all, axes, 0, 0, tiled=True)  11.3 us
    ppermute x3, waiting for transfers between devices, other_members(): return lax.ppermute(value, 'mem', [(0, 1), (1, 0)])  7.34 us
    ppermute x1, waiting for transfers between devices, per_device(): mine = keep + lax.ppermute(send, 'mem', [(0, 1), (1, 0)])  5.68 us
    all_to_all x1, starting transfers between devices, per_device(): sums = lax.all_to_all(to_all, axes, 0, 0, tiled=True)  5.28 us
    ppermute x6, starting transfers between devices, both_x(): return (lax.ppermute(right, 'gx', up), lax.ppermute(left, 'gx', down))  5.24 us
    unnamed x34, local copies, waits for them, and re-layouts  4.84 us
  transfers between devices with their start and end apart: 17, of which 9 were waited for; matrix products, arithmetic and copies ran while one was open for 2% of the time, Pallas kernels for 6%

profile of v1, /device:TPU:0, one launch (start us, length us, event | category | flops | bytes accessed | tf_op | source)
XLA Modules:
  0.0 107.2 jit_solution(6334188104015232036)
XLA Ops:
  2.2 5.0 %collective-permute-start = (f32[2,128,128]{2,1,0:T(8,128)}, f32[2,128,128]{2,1,0:T(8,128)S(1)}, u32[]{:S(2)}, u32[]{:S(2)}) collective-permute-start(f32[2,128,128]{2,1,0:T(8,128)} %bitcast.30), channel_id=1, source_target_pairs={{0,4},{4,0},{8,12},{12,8},{1,5},{5,1},{9,13},{13,9},{2,6},{6,2},{1... | collective-permute-start | bytes 393224 | tf_op jit(solution)/shard_map/ppermute | solution.py:342
  7.8 2.6 %matrices.1 = (f32[384,256]{1,0:T(8,128)}, f32[2,128,144]{2,1,0:T(8,128)}) custom-call(s32[5]{0:T(128)} %stack.15.pos), custom_call_target="tpu_custom_call" | custom-call | flops 3000000000 | bytes 1048576 | tf_op jit(solution)/shard_map/matrices/pallas_call | solution.py:320
  11.3 2.4 %start.1 = (f32[2,128,128]{2,1,0:T(8,128)}, f32[2,8,128]{2,1,0:T(8,128)}, f32[2,8,128]{2,1,0:T(8,128)}) custom-call(f32[2,128,128]{2,1,0:T(8,128)} %bitcast.31, f32[2,128,128]{2,1,0:T(8,128)} %copy-done.5, f32[2,128,128]{2,1,0:T(8,128)} %copy-done.4, f32[384,256]{1,0:T(8,128)} %get-tuple-element.36.ky.refs_6_.refs_10_), custom_call_target="tpu_custom_call" | custom-call | flops 1500000000 | bytes 1048576 | tf_op jit(solution)/shard_map/start/pallas_call | solution.py:320
  13.7 1.7 %collective-permute-start.3 = (f32[2,8,128]{2,1,0:T(8,128)}, f32[2,8,128]{2,1,0:T(8,128)S(1)}, u32[]{:S(2)}, u32[]{:S(2)}) collective-permute-start(f32[2,8,128]{2,1,0:T(8,128)} %get-tuple-element.39), channel_id=1, source_target_pairs={{1,0},{2,1},{3,2},{0,3},{5,4},{6,5},{7,6},{4,7},{9,8},{10,9},{11,1... | collective-permute-start | bytes 24584 | tf_op jit(solution)/shard_map/ppermute | solution.py:349
  15.4 3.9 %prep.1.info.refs_0_.refs_5_ = f32[5,32,128]{2,1,0:T(8,128)} custom-call(bf16[2,5,128,128]{3,2,1,0:T(8,128)(2,1)} %bitcast.27, s32[32,128]{1,0:T(8,128)} %cell.1, s32[32,128]{1,0:T(8,128)} %flag.1, f32[32,128]{1,0:T(8,128)} %innov.1, f32[32,128]{1,0:T(8,128)} %prec.1), custom_call_target="tpu_custom_call" | custom-call | flops 6000000000 | bytes 1048576 | tf_op jit(solution)/shard_map/prep/pallas_call | solution.py:320
  19.9 3.2 %first_seen.1 = (f32[2,128,128]{2,1,0:T(8,128)}, f32[2,128,128]{2,1,0:T(8,128)}, f32[32,128]{1,0:T(8,128)}) custom-call(f32[2,128,128]{2,1,0:T(8,128)} %get-tuple-element.37.y1, f32[2,8,128]{2,1,0:T(8,128)} %copy-done.15, f32[2,8,128]{2,1,0:T(8,128)} %copy-done.16, f32[2,128,128]{2,1,0:T(8,128)} %bitcast.32, f32[2,128,144]{2,1,0:T(8,128)} %get-tuple-element.40.kx.refs_4_, ...), custom_call_target="tpu_custom_call" | custom-call | flops 3000000000 | bytes 1048576 | tf_op jit(solution)/shard_map/first_seen/pallas_call | solution.py:320
  24.6 2.4 %collective-permute-done.4 = f32[32,128]{1,0:T(8,128)S(1)} collective-permute-done((f32[32,128]{1,0:T(8,128)}, f32[32,128]{1,0:T(8,128)S(1)}, u32[]{:S(2)}, u32[]{:S(2)}) %collective-permute-start.4) | collective-permute-done | bytes 16416 | tf_op jit(solution)/shard_map/ppermute | solution.py:355
  29.0 3.5 %collective-permute-start.5 = (f32[6,32,128]{2,1,0:T(8,128)S(1)}, f32[6,32,128]{2,1,0:T(8,128)S(1)}, u32[]{:S(2)}, u32[]{:S(2)}) collective-permute-start(f32[6,32,128]{2,1,0:T(8,128)S(1)} %pad_maximum_fusion), channel_id=1, source_target_pairs={{0,4},{4,0},{8,12},{12,8},{1,5},{5,1},{9,13},{13,9},{2,6},{6,2},{1... | collective-permute-start | bytes 294920 | tf_op jit(solution)/shard_map/ppermute | solution.py:342
  36.4 4.6 %scatter.2 = (f32[2,128,128]{2,1,0:T(8,128)}, f32[2,128,128]{2,1,0:T(8,128)}, f32[2,2,8,128]{3,2,1,0:T(8,128)}, f32[2,2,8,128]{3,2,1,0:T(8,128)}, f32[32,128]{1,0:T(8,128)}, /*index=5*/f32[32,128]{1,0:T(8,128)}) custom-call(f32[5,32,128]{2,1,0:T(8,128)} %prep.1.info.refs_0_.refs_5_, f32[5,32,128]{2,1,0:T(8,128)} %slice.16.refs_1_, ...), custom_call_target="tpu_custom_call" | custom-call | flops 6000000000 | bytes 1048576 | tf_op jit(solution)/shard_map/scatter/pallas_call | solution.py:320
  41.0 1.7 %collective-permute-start.8 = (f32[2,2,8,128]{3,2,1,0:T(8,128)}, f32[2,2,8,128]{3,2,1,0:T(8,128)S(1)}, u32[]{:S(2)}, u32[]{:S(2)}) collective-permute-start(f32[2,2,8,128]{3,2,1,0:T(8,128)} %get-tuple-element.45), channel_id=1, source_target_pairs={{1,0},{2,1},{3,2},{0,3},{5,4},{6,5},{7,6},{4,7},{9,8},{10,9},{11,1... | collective-permute-start | bytes 49160 | tf_op jit(solution)/shard_map/ppermute | solution.py:349
  42.7 1.6 %collective-permute-done.7.refs_2_ = f32[2,2,8,128]{3,2,1,0:T(8,128)S(1)} collective-permute-done((f32[2,2,8,128]{3,2,1,0:T(8,128)}, f32[2,2,8,128]{3,2,1,0:T(8,128)S(1)}, u32[]{:S(2)}, u32[]{:S(2)}) %collective-permute-start.7) | collective-permute-done | bytes 16416 | tf_op jit(solution)/shard_map/ppermute | solution.py:349
  45.0 3.3 %gather.2 = (f32[2,128,128]{2,1,0:T(8,128)}, f32[2,128,128]{2,1,0:T(8,128)}, f32[32,128]{1,0:T(8,128)}, f32[1,128]{1,0:T(1,128)}) custom-call(f32[2,128,128]{2,1,0:T(8,128)} %get-tuple-element.42.refs_0_, f32[2,128,128]{2,1,0:T(8,128)} %get-tuple-element.43.refs_1_, f32[2,2,8,128]{3,2,1,0:T(8,128)} %copy-done.11, f32[2,2,8,128]{3,2,1,0:T(8,128)} %copy-done.12, ...), custom_call_target="tpu_custom_call" | custom-call | flops 4000000000 | bytes 1048576 | tf_op jit(solution)/shard_map/gather/pallas_call | solution.py:320
  49.8 2.4 %collective-permute-done.9.other = f32[32,128]{1,0:T(8,128)S(1)} collective-permute-done((f32[32,128]{1,0:T(8,128)}, f32[32,128]{1,0:T(8,128)S(1)}, u32[]{:S(2)}, u32[]{:S(2)}) %collective-permute-start.9) | collective-permute-done | bytes 16416 | tf_op jit(solution)/shard_map/ppermute | solution.py:355
  54.3 5.3 %all-to-all-start = ((f32[32,1,128]{2,1,0:T(1,128)}), f32[32,1,128]{2,1,0:T(1,128)S(1)}, u32[]{:S(2)}, u32[]{:S(2)}) async-start(f32[32,1,128]{2,1,0:T(1,128)} %bitcast.24), calls=%async_computation | async-start | bytes 32768 | tf_op jit(solution)/shard_map/all_to_all | solution.py:415
  60.4 4.5 %collective-permute-start.10 = (f32[32,128]{1,0:T(8,128)S(1)}, f32[32,128]{1,0:T(8,128)S(1)}, u32[]{:S(2)}, u32[]{:S(2)}) collective-permute-start(f32[32,128]{1,0:T(8,128)S(1)} %copy-done.6), channel_id=1, source_target_pairs={{0,4},{4,0},{8,12},{12,8},{1,5},{5,1},{9,13},{13,9},{2,6},{6,2},{1... | collective-permute-start | bytes 49160 | tf_op jit(solution)/shard_map/ppermute | solution.py:342
  65.0 1.7 %collective-permute-done.10.refs_7_ = f32[32,128]{1,0:T(8,128)S(1)} collective-permute-done((f32[32,128]{1,0:T(8,128)S(1)}, f32[32,128]{1,0:T(8,128)S(1)}, u32[]{:S(2)}, u32[]{:S(2)}) %collective-permute-start.10) | collective-permute-done | bytes 16416 | tf_op jit(solution)/shard_map/ppermute | solution.py:342
  67.4 4.8 %scatter.3 = (f32[2,128,128]{2,1,0:T(8,128)}, f32[2,128,128]{2,1,0:T(8,128)}, f32[2,2,8,128]{3,2,1,0:T(8,128)}, f32[2,2,8,128]{3,2,1,0:T(8,128)}, f32[32,128]{1,0:T(8,128)}, /*index=5*/f32[32,128]{1,0:T(8,128)}) custom-call(f32[5,32,128]{2,1,0:T(8,128)} %prep.1.info.refs_0_.refs_5_, f32[5,32,128]{2,1,0:T(8,128)} %slice.16.refs_1_, ...), custom_call_target="tpu_custom_call" | custom-call | flops 6000000000 | bytes 1048576 | tf_op jit(solution)/shard_map/scatter/pallas_call | solution.py:320
  72.2 1.7 %collective-permute-start.13 = (f32[2,2,8,128]{3,2,1,0:T(8,128)}, f32[2,2,8,128]{3,2,1,0:T(8,128)S(1)}, u32[]{:S(2)}, u32[]{:S(2)}) collective-permute-start(f32[2,2,8,128]{3,2,1,0:T(8,128)} %get-tuple-element.56), channel_id=1, source_target_pairs={{1,0},{2,1},{3,2},{0,3},{5,4},{6,5},{7,6},{4,7},{9,8},{10,9},{11,1... | collective-permute-start | bytes 49160 | tf_op jit(solution)/shard_map/ppermute | solution.py:349
  73.9 1.6 %collective-permute-done.12.refs_2_ = f32[2,2,8,128]{3,2,1,0:T(8,128)S(1)} collective-permute-done((f32[2,2,8,128]{3,2,1,0:T(8,128)}, f32[2,2,8,128]{3,2,1,0:T(8,128)S(1)}, u32[]{:S(2)}, u32[]{:S(2)}) %collective-permute-start.12) | collective-permute-done | bytes 16416 | tf_op jit(solution)/shard_map/ppermute | solution.py:349
  76.2 3.4 %gather.3 = (f32[2,128,128]{2,1,0:T(8,128)}, f32[2,128,128]{2,1,0:T(8,128)}, f32[2,128,128]{2,1,0:T(8,128)}, f32[2,128,128]{2,1,0:T(8,128)}, f32[32,128]{1,0:T(8,128)}, /*index=5*/f32[1,128]{1,0:T(1,128)}) custom-call(f32[2,128,128]{2,1,0:T(8,128)} %get-tuple-element.53.refs_0_, f32[2,128,128]{2,1,0:T(8,128)} %get-tuple-element.54.refs_1_, ...), custom_call_target="tpu_custom_call" | custom-call | flops 4000000000 | bytes 1048576 | tf_op jit(solution)/shard_map/gather/pallas_call | solution.py:320
  81.0 2.5 %collective-permute-done.14.other = f32[32,128]{1,0:T(8,128)S(1)} collective-permute-done((f32[32,128]{1,0:T(8,128)}, f32[32,128]{1,0:T(8,128)S(1)}, u32[]{:S(2)}, u32[]{:S(2)}) %collective-permute-start.14) | collective-permute-done | bytes 16416 | tf_op jit(solution)/shard_map/ppermute | solution.py:355
  85.6 11.3 %all_to_all.22 = f32[32,1,128]{2,1,0:T(1,128)} all-to-all(f32[32,1,128]{2,1,0:T(1,128)} %bitcast.26), channel_id=1, replica_groups=mesh['mem'=2,'gy'=4,'gx'=4] {'mem','gy','gx'}, dimensions={0} | all-to-all | bytes 32768 | tf_op jit(solution)/shard_map/all_to_all | solution.py:415
  96.9 2.3 %final.1 = (f32[2,128,128]{2,1,0:T(8,128)}, f32[5,64,128]{2,1,0:T(8,128)}, f32[5,64,128]{2,1,0:T(8,128)}) custom-call(s32[5]{0:T(128)} %stack.15.pos, f32[32,128]{1,0:T(8,128)} %bitcast.25, f32[2,128,128]{2,1,0:T(8,128)} %get-tuple-element.63.control, f32[2,128,128]{2,1,0:T(8,128)} %get-tuple-element.64.smoothed, f32[2,128,128]{2,1,0:T(8,128)} %get-tuple-element.65.grad, ...), custom_call_target="tpu_custom_call" | custom-call | flops 3000000000 | bytes 1048576 | tf_op jit(solution)/shard_map/final/pallas_call | solution.py:320
  99.9 5.7 %collective-permute-done.15 = f32[5,64,128]{2,1,0:T(8,128)S(1)} collective-permute-done((f32[5,64,128]{2,1,0:T(8,128)}, f32[5,64,128]{2,1,0:T(8,128)S(1)}, u32[]{:S(2)}, u32[]{:S(2)}) %collective-permute-start.15) | collective-permute-done | bytes 163872 | tf_op jit(solution)/shard_map/ppermute | solution.py:420
  (64 shorter events, 23.2 us)
Async XLA Ops:
  0.6 9.8 %collective-permute-start.1 = (f32[2,128,128]{2,1,0:T(8,128)}, f32[2,128,128]{2,1,0:T(8,128)S(1)}, u32[]{:S(2)}, u32[]{:S(2)}) collective-permute-start(f32[2,128,128]{2,1,0:T(8,128)} %bitcast.29), channel_id=1, source_target_pairs={{0,0},{4,8},{8,4},{12,12},{1,1},{5,9},{9,5},{13,13},{2,2},{6,10},{... | collective-permute-start | bytes 393224 | tf_op jit(solution)/shard_map/ppermute | solution.py:342
  2.2 8.5 %collective-permute-start = (f32[2,128,128]{2,1,0:T(8,128)}, f32[2,128,128]{2,1,0:T(8,128)S(1)}, u32[]{:S(2)}, u32[]{:S(2)}) collective-permute-start(f32[2,128,128]{2,1,0:T(8,128)} %bitcast.30), channel_id=1, source_target_pairs={{0,4},{4,0},{8,12},{12,8},{1,5},{5,1},{9,13},{13,9},{2,6},{6,2},{1... | collective-permute-start | bytes 393224 | tf_op jit(solution)/shard_map/ppermute | solution.py:342
  10.5 0.7 copy-start.4
  10.7 0.7 copy-start.5
  13.7 5.6 %collective-permute-start.2 = (f32[2,8,128]{2,1,0:T(8,128)}, f32[2,8,128]{2,1,0:T(8,128)S(1)}, u32[]{:S(2)}, u32[]{:S(2)}) collective-permute-start(f32[2,8,128]{2,1,0:T(8,128)} %get-tuple-element.38), channel_id=1, source_target_pairs={{0,1},{1,2},{2,3},{3,0},{4,5},{5,6},{6,7},{7,4},{8,9},{9,10},{10,1... | collective-permute-start | bytes 24584 | tf_op jit(solution)/shard_map/ppermute | solution.py:349
  13.7 5.6 %collective-permute-start.3 = (f32[2,8,128]{2,1,0:T(8,128)}, f32[2,8,128]{2,1,0:T(8,128)S(1)}, u32[]{:S(2)}, u32[]{:S(2)}) collective-permute-start(f32[2,8,128]{2,1,0:T(8,128)} %get-tuple-element.39), channel_id=1, source_target_pairs={{1,0},{2,1},{3,2},{0,3},{5,4},{6,5},{7,6},{4,7},{9,8},{10,9},{11,1... | collective-permute-start | bytes 24584 | tf_op jit(solution)/shard_map/ppermute | solution.py:349
  19.9 7.8 %copy-start.1 = (f32[5,32,128]{2,1,0:T(8,128)S(1)}, f32[5,32,128]{2,1,0:T(8,128)}, u32[]{:S(2)}) copy-start(f32[5,32,128]{2,1,0:T(8,128)} %prep.1.info.refs_0_.refs_5_) | copy-start | bytes 245764
  23.1 3.9 %collective-permute-start.4 = (f32[32,128]{1,0:T(8,128)}, f32[32,128]{1,0:T(8,128)S(1)}, u32[]{:S(2)}, u32[]{:S(2)}) collective-permute-start(f32[32,128]{1,0:T(8,128)} %get-tuple-element.41), channel_id=1, source_target_pairs={{0,16},{16,0},{1,17},{17,1},{2,18},{18,2},{3,19},{19,3},{4,20},{20... | collective-permute-start | bytes 49160 | tf_op jit(solution)/shard_map/ppermute | solution.py:355
  28.3 4.2 %collective-permute-start.6 = (f32[6,32,128]{2,1,0:T(8,128)S(1)}, f32[6,32,128]{2,1,0:T(8,128)S(1)}, u32[]{:S(2)}, u32[]{:S(2)}) collective-permute-start(f32[6,32,128]{2,1,0:T(8,128)S(1)} %pad_maximum_fusion), channel_id=1, source_target_pairs={{0,0},{4,8},{8,4},{12,12},{1,1},{5,9},{9,5},{13,13},{2,2},{6,10},{... | collective-permute-start | bytes 294920 | tf_op jit(solution)/shard_map/ppermute | solution.py:342
  29.0 6.1 %collective-permute-start.5 = (f32[6,32,128]{2,1,0:T(8,128)S(1)}, f32[6,32,128]{2,1,0:T(8,128)S(1)}, u32[]{:S(2)}, u32[]{:S(2)}) collective-permute-start(f32[6,32,128]{2,1,0:T(8,128)S(1)} %pad_maximum_fusion), channel_id=1, source_target_pairs={{0,4},{4,0},{8,12},{12,8},{1,5},{5,1},{9,13},{13,9},{2,6},{6,2},{1... | collective-permute-start | bytes 294920 | tf_op jit(solution)/shard_map/ppermute | solution.py:342
  41.0 3.4 %collective-permute-start.7 = (f32[2,2,8,128]{3,2,1,0:T(8,128)}, f32[2,2,8,128]{3,2,1,0:T(8,128)S(1)}, u32[]{:S(2)}, u32[]{:S(2)}) collective-permute-start(f32[2,2,8,128]{3,2,1,0:T(8,128)} %get-tuple-element.44), channel_id=1, source_target_pairs={{0,1},{1,2},{2,3},{3,0},{4,5},{5,6},{6,7},{7,4},{8,9},{9,10},{10,1... | collective-permute-start | bytes 49160 | tf_op jit(solution)/shard_map/ppermute | solution.py:349
  41.0 3.4 %collective-permute-start.8 = (f32[2,2,8,128]{3,2,1,0:T(8,128)}, f32[2,2,8,128]{3,2,1,0:T(8,128)S(1)}, u32[]{:S(2)}, u32[]{:S(2)}) collective-permute-start(f32[2,2,8,128]{3,2,1,0:T(8,128)} %get-tuple-element.45), channel_id=1, source_target_pairs={{1,0},{2,1},{3,2},{0,3},{5,4},{6,5},{7,6},{4,7},{9,8},{10,9},{11,1... | collective-permute-start | bytes 49160 | tf_op jit(solution)/shard_map/ppermute | solution.py:349
  48.3 3.9 %collective-permute-start.9 = (f32[32,128]{1,0:T(8,128)}, f32[32,128]{1,0:T(8,128)S(1)}, u32[]{:S(2)}, u32[]{:S(2)}) collective-permute-start(f32[32,128]{1,0:T(8,128)} %get-tuple-element.48.mine), channel_id=1, source_target_pairs={{0,16},{16,0},{1,17},{17,1},{2,18},{18,2},{3,19},{19,3},{4,20},{20... | collective-permute-start | bytes 49160 | tf_op jit(solution)/shard_map/ppermute | solution.py:355
  54.3 5.3 %copy-start.6 = (f32[32,128]{1,0:T(8,128)S(1)}, f32[32,128]{1,0:T(8,128)}, u32[]{:S(2)}) copy-start(f32[32,128]{1,0:T(8,128)} %get-tuple-element.51.refs_6_) | copy-start | bytes 49156
  54.3 12.5 %all-to-all-start = ((f32[32,1,128]{2,1,0:T(1,128)}), f32[32,1,128]{2,1,0:T(1,128)S(1)}, u32[]{:S(2)}, u32[]{:S(2)}) async-start(f32[32,1,128]{2,1,0:T(1,128)} %bitcast.24), calls=%async_computation | async-start | bytes 32768 | tf_op jit(solution)/shard_map/all_to_all | solution.py:415
  59.6 5.4 %collective-permute-start.11 = (f32[32,128]{1,0:T(8,128)S(1)}, f32[32,128]{1,0:T(8,128)S(1)}, u32[]{:S(2)}, u32[]{:S(2)}) collective-permute-start(f32[32,128]{1,0:T(8,128)S(1)} %copy-done.6), channel_id=1, source_target_pairs={{0,0},{4,8},{8,4},{12,12},{1,1},{5,9},{9,5},{13,13},{2,2},{6,10},{... | collective-permute-start | bytes 49160 | tf_op jit(solution)/shard_map/ppermute | solution.py:342
  60.4 6.3 %collective-permute-start.10 = (f32[32,128]{1,0:T(8,128)S(1)}, f32[32,128]{1,0:T(8,128)S(1)}, u32[]{:S(2)}, u32[]{:S(2)}) collective-permute-start(f32[32,128]{1,0:T(8,128)S(1)} %copy-done.6), channel_id=1, source_target_pairs={{0,4},{4,0},{8,12},{12,8},{1,5},{5,1},{9,13},{13,9},{2,6},{6,2},{1... | collective-permute-start | bytes 49160 | tf_op jit(solution)/shard_map/ppermute | solution.py:342
  65.0 1.8 %copy-start.7 = (f32[32,128]{1,0:T(8,128)}, f32[32,128]{1,0:T(8,128)S(1)}, u32[]{:S(2)}) copy-start(f32[32,128]{1,0:T(8,128)S(1)} %collective-permute-done.11.refs_8_) | copy-start | bytes 49156
  72.1 3.4 %collective-permute-start.12 = (f32[2,2,8,128]{3,2,1,0:T(8,128)}, f32[2,2,8,128]{3,2,1,0:T(8,128)S(1)}, u32[]{:S(2)}, u32[]{:S(2)}) collective-permute-start(f32[2,2,8,128]{3,2,1,0:T(8,128)} %get-tuple-element.55), channel_id=1, source_target_pairs={{0,1},{1,2},{2,3},{3,0},{4,5},{5,6},{6,7},{7,4},{8,9},{9,10},{10,1... | collective-permute-start | bytes 49160 | tf_op jit(solution)/shard_map/ppermute | solution.py:349
  72.2 3.4 %collective-permute-start.13 = (f32[2,2,8,128]{3,2,1,0:T(8,128)}, f32[2,2,8,128]{3,2,1,0:T(8,128)S(1)}, u32[]{:S(2)}, u32[]{:S(2)}) collective-permute-start(f32[2,2,8,128]{3,2,1,0:T(8,128)} %get-tuple-element.56), channel_id=1, source_target_pairs={{1,0},{2,1},{3,2},{0,3},{5,4},{6,5},{7,6},{4,7},{9,8},{10,9},{11,1... | collective-permute-start | bytes 49160 | tf_op jit(solution)/shard_map/ppermute | solution.py:349
  79.5 3.9 %collective-permute-start.14 = (f32[32,128]{1,0:T(8,128)}, f32[32,128]{1,0:T(8,128)S(1)}, u32[]{:S(2)}, u32[]{:S(2)}) collective-permute-start(f32[32,128]{1,0:T(8,128)} %get-tuple-element.59.mine), channel_id=1, source_target_pairs={{0,16},{16,0},{1,17},{17,1},{2,18},{18,2},{3,19},{19,3},{4,20},{20... | collective-permute-start | bytes 49160 | tf_op jit(solution)/shard_map/ppermute | solution.py:355
  83.5 0.6 copy-start.14
  96.9 8.7 %copy-start = (f32[5,8,8,128]{3,2,1,0:T(8,128)S(1)}, f32[5,8,8,128]{3,2,1,0:T(8,128)}, u32[]{:S(2)}) copy-start(f32[5,8,8,128]{3,2,1,0:T(8,128)} %param.9) | copy-start | bytes 491524
  99.2 6.4 %collective-permute-start.15 = (f32[5,64,128]{2,1,0:T(8,128)}, f32[5,64,128]{2,1,0:T(8,128)S(1)}, u32[]{:S(2)}, u32[]{:S(2)}) collective-permute-start(f32[5,64,128]{2,1,0:T(8,128)} %get-tuple-element.68), channel_id=1, source_target_pairs={{0,16},{16,0},{1,17},{17,1},{2,18},{18,2},{3,19},{19,3},{4,20},{20... | collective-permute-start | bytes 491528 | tf_op jit(solution)/shard_map/ppermute | solution.py:420
  (10 other events, 6.0 us)

commit v2 on v1

--- a/solution.py
+++ b/solution.py
@@ -323,6 +323,7 @@
         in_specs=[SMEM] * smem + [VMEM] * (len(ins) - smem),
         out_specs=[VMEM] * len(outs),
         scratch_shapes=list(scratch),
+        compiler_params=pltpu.CompilerParams(vmem_limit_bytes=16 << 20),
         cost_estimate=pl.CostEstimate(flops=int(us * 1e9), bytes_accessed=1 << 20, transcendentals=0),
         name=name,
     )(*ins)

time: 108 us -> 84.3 us (0.78)
  Pallas kernels: 33.4 us -> 18.1 us
  local copies, waits for them, and re-layouts: 7.91 us -> 0.13 us
  other arithmetic: 2.35 us -> 0.71 us
  waiting for transfers between devices: 19.7 us -> 21 us
    pallas_call x11, Pallas kernels: 33.4 us -> 18.1 us  [call(): pl.pallas_call(kernel, out_shape=shapes, in_specs=[SMEM] * smem + [VMEM]...]
    unnamed x34 -> x14, local copies, waits for them, and re-layouts: 4.84 us -> 0.03 us
    ppermute x3, waiting for transfers between devices: 3.29 us -> 5.99 us  [both_y(): lax.ppermute(value, 'gy', pairs_a(n))]
    slice x2, local copies, waits for them, and re-layouts: 1.26 us -> 0.01 us  [per_device(): infos = [p[:-1] for p in packs]]
    squeeze x2, local copies, waits for them, and re-layouts: 1.21 us -> 0.01 us  [per_device(): incs = [p[-1] for p in packs]]
  transfers between devices with their start and end apart: 17 -> 17, of which waited for: 9 -> 9; matrix products, arithmetic and copies ran while one was open for 2% -> 0% of each run, Pallas kernels for 6% -> 5%
where the time goes in v2:
time: 84.3 us; the launch traced here: 84.1 us
  starting transfers between devices  32.2 us (38%)
  waiting for transfers between devices  21 us (25%)
  Pallas kernels  18.1 us (21%)
  blocking collectives  11.2 us (13%)
    pallas_call x11, Pallas kernels, call(): pl.pallas_call(kernel, out_shape=shapes, in_specs=[SMEM] * smem + [VMEM]...  18.1 us
    ppermute x3, starting transfers between devices, both_y(): lax.ppermute(value, 'gy', pairs_a(n))  13.1 us
    all_to_all x1, blocking collectives, per_device(): sums = lax.all_to_all(to_all, axes, 0, 0, tiled=True)  11.2 us
    ppermute x3, waiting for transfers between devices, other_members(): return lax.ppermute(value, 'mem', [(0, 1), (1, 0)])  6.68 us
    ppermute x3, waiting for transfers between devices, both_y(): lax.ppermute(value, 'gy', pairs_a(n))  5.99 us
    ppermute x1, waiting for transfers between devices, per_device(): mine = keep + lax.ppermute(send, 'mem', [(0, 1), (1, 0)])  5.39 us
    ppermute x6, starting transfers between devices, both_x(): return (lax.ppermute(right, 'gx', up), lax.ppermute(left, 'gx', down))  5.37 us
    all_to_all x1, starting transfers between devices, per_device(): sums = lax.all_to_all(to_all, axes, 0, 0, tiled=True)  5.3 us
  transfers between devices with their start and end apart: 17, of which 9 were waited for; matrix products, arithmetic and copies ran while one was open for 0% of the time, Pallas kernels for 5%

profile of v2, /device:TPU:0, one launch (start us, length us, event | category | flops | bytes accessed | tf_op | source)
XLA Modules:
  0.0 84.1 jit_solution(5271048902732549116)
XLA Ops:
  0.6 1.6 %collective-permute-start.1 = (f32[2,128,128]{2,1,0:T(8,128)}, f32[2,128,128]{2,1,0:T(8,128)S(1)}, u32[]{:S(2)}, u32[]{:S(2)}) collective-permute-start(f32[2,128,128]{2,1,0:T(8,128)} %bitcast.28), channel_id=1, source_target_pairs={{0,0},{4,8},{8,4},{12,12},{1,1},{5,9},{9,5},{13,13},{2,2},{6,10},{... | collective-permute-start | bytes 393224 | tf_op jit(solution)/shard_map/ppermute | solution.py:343
  2.2 5.0 %collective-permute-start = (f32[2,128,128]{2,1,0:T(8,128)}, f32[2,128,128]{2,1,0:T(8,128)S(1)}, u32[]{:S(2)}, u32[]{:S(2)}) collective-permute-start(f32[2,128,128]{2,1,0:T(8,128)} %bitcast.29), channel_id=1, source_target_pairs={{0,4},{4,0},{8,12},{12,8},{1,5},{5,1},{9,13},{13,9},{2,6},{6,2},{1... | collective-permute-start | bytes 393224 | tf_op jit(solution)/shard_map/ppermute | solution.py:343
  7.3 1.6 %matrices.1 = (f32[384,256]{1,0:T(8,128)S(1)}, f32[2,128,144]{2,1,0:T(8,128)S(1)}) custom-call(s32[5]{0:T(128)S(1)} %stack.15.pos), custom_call_target="tpu_custom_call" | custom-call | flops 3000000000 | bytes 1048576 | tf_op jit(solution)/shard_map/matrices/pallas_call | solution.py:320
  9.0 1.7 %collective-permute-done.a = f32[2,128,128]{2,1,0:T(8,128)S(1)} collective-permute-done((f32[2,128,128]{2,1,0:T(8,128)}, f32[2,128,128]{2,1,0:T(8,128)S(1)}, u32[]{:S(2)}, u32[]{:S(2)}) %collective-permute-start) | collective-permute-done | bytes 131104 | tf_op jit(solution)/shard_map/ppermute | solution.py:343
  11.3 1.7 %collective-permute-start.3 = (f32[2,8,128]{2,1,0:T(8,128)S(1)}, f32[2,8,128]{2,1,0:T(8,128)S(1)}, u32[]{:S(2)}, u32[]{:S(2)}) collective-permute-start(f32[2,8,128]{2,1,0:T(8,128)S(1)} %get-tuple-element.39), channel_id=1, source_target_pairs={{1,0},{2,1},{3,2},{0,3},{5,4},{6,5},{7,6},{4,7},{9,8},{10,9},{11,1... | collective-permute-start | bytes 24584 | tf_op jit(solution)/shard_map/ppermute | solution.py:350
  13.1 2.2 %prep.1.info.refs_0_.refs_5_ = f32[5,32,128]{2,1,0:T(8,128)S(1)} custom-call(bf16[2,5,128,128]{3,2,1,0:T(8,128)(2,1)S(1)} %bitcast.26, s32[32,128]{1,0:T(8,128)S(1)} %copy-done.2, s32[32,128]{1,0:T(8,128)S(1)} %copy-done.3, f32[32,128]{1,0:T(8,128)S(1)} %copy-done.4, f32[32,128]{1,0:T(8,128)S(1)} %copy-done.5), custom_call_target="tpu_custom_call" | custom-call | flops 6000000000 | bytes 1048576 | tf_op jit(solution)/shard_map/prep/pallas_call | solution.py:320
  16.7 1.6 %collective-permute-start.4 = (f32[32,128]{1,0:T(8,128)S(1)}, f32[32,128]{1,0:T(8,128)S(1)}, u32[]{:S(2)}, u32[]{:S(2)}) collective-permute-start(f32[32,128]{1,0:T(8,128)S(1)} %get-tuple-element.41), channel_id=1, source_target_pairs={{0,16},{16,0},{1,17},{17,1},{2,18},{18,2},{3,19},{19,3},{4,20},{20... | collective-permute-start | bytes 49160 | tf_op jit(solution)/shard_map/ppermute | solution.py:356
  18.3 2.2 %collective-permute-done.4 = f32[32,128]{1,0:T(8,128)S(1)} collective-permute-done((f32[32,128]{1,0:T(8,128)S(1)}, f32[32,128]{1,0:T(8,128)S(1)}, u32[]{:S(2)}, u32[]{:S(2)}) %collective-permute-start.4) | collective-permute-done | bytes 16416 | tf_op jit(solution)/shard_map/ppermute | solution.py:356
  21.2 3.5 %collective-permute-start.5 = (f32[6,32,128]{2,1,0:T(8,128)S(1)}, f32[6,32,128]{2,1,0:T(8,128)S(1)}, u32[]{:S(2)}, u32[]{:S(2)}) collective-permute-start(f32[6,32,128]{2,1,0:T(8,128)S(1)} %pad_maximum_fusion), channel_id=1, source_target_pairs={{0,4},{4,0},{8,12},{12,8},{1,5},{5,1},{9,13},{13,9},{2,6},{6,2},{1... | collective-permute-start | bytes 294920 | tf_op jit(solution)/shard_map/ppermute | solution.py:343
  24.7 2.6 %collective-permute-done.5 = f32[6,32,128]{2,1,0:T(8,128)S(1)} collective-permute-done((f32[6,32,128]{2,1,0:T(8,128)S(1)}, f32[6,32,128]{2,1,0:T(8,128)S(1)}, u32[]{:S(2)}, u32[]{:S(2)}) %collective-permute-start.5) | collective-permute-done | bytes 98336 | tf_op jit(solution)/shard_map/ppermute | solution.py:343
  27.3 2.7 %scatter.2 = (f32[2,128,128]{2,1,0:T(8,128)S(1)}, f32[2,128,128]{2,1,0:T(8,128)S(1)}, f32[2,2,8,128]{3,2,1,0:T(8,128)S(1)}, f32[2,2,8,128]{3,2,1,0:T(8,128)S(1)}...) custom-call(f32[5,32,128]{2,1,0:T(8,128)S(1)} %prep.1.info.refs_0_.refs_5_, f32[5,32,128]{2,1,0:T(8,128)S(1)} %slice.16.refs_1_, ...), custom_call_target="tpu_custom_call" | custom-call | flops 6000000000 | bytes 1048576 | tf_op jit(solution)/shard_map/scatter/pallas_call | solution.py:320
  30.2 1.7 %collective-permute-start.8 = (f32[2,2,8,128]{3,2,1,0:T(8,128)S(1)}, f32[2,2,8,128]{3,2,1,0:T(8,128)S(1)}, u32[]{:S(2)}, u32[]{:S(2)}) collective-permute-start(f32[2,2,8,128]{3,2,1,0:T(8,128)S(1)} %get-tuple-element.45), channel_id=1, source_target_pairs={{1,0},{2,1},{3,2},{0,3},{5,4},{6,5},{7,6},{4,7},{9,8},{10,9},{11,1... | collective-permute-start | bytes 49160 | tf_op jit(solution)/shard_map/ppermute | solution.py:350
  34.8 1.6 %collective-permute-start.9 = (f32[32,128]{1,0:T(8,128)S(1)}, f32[32,128]{1,0:T(8,128)S(1)}, u32[]{:S(2)}, u32[]{:S(2)}) collective-permute-start(f32[32,128]{1,0:T(8,128)S(1)} %get-tuple-element.48.mine), channel_id=1, source_target_pairs={{0,16},{16,0},{1,17},{17,1},{2,18},{18,2},{3,19},{19,3},{4,20},{20... | collective-permute-start | bytes 49160 | tf_op jit(solution)/shard_map/ppermute | solution.py:356
  36.4 2.2 %collective-permute-done.9.other = f32[32,128]{1,0:T(8,128)S(1)} collective-permute-done((f32[32,128]{1,0:T(8,128)S(1)}, f32[32,128]{1,0:T(8,128)S(1)}, u32[]{:S(2)}, u32[]{:S(2)}) %collective-permute-start.9) | collective-permute-done | bytes 16416 | tf_op jit(solution)/shard_map/ppermute | solution.py:356
  39.8 5.3 %all-to-all-start = ((f32[32,1,128]{2,1,0:T(1,128)}), f32[32,1,128]{2,1,0:T(1,128)S(1)}, u32[]{:S(2)}, u32[]{:S(2)}) async-start(f32[32,1,128]{2,1,0:T(1,128)} %bitcast.9), calls=%async_computation | async-start | bytes 32768 | tf_op jit(solution)/shard_map/all_to_all | solution.py:416
  46.0 4.5 %collective-permute-start.10 = (f32[32,128]{1,0:T(8,128)S(1)}, f32[32,128]{1,0:T(8,128)S(1)}, u32[]{:S(2)}, u32[]{:S(2)}) collective-permute-start(f32[32,128]{1,0:T(8,128)S(1)} %get-tuple-element.51.refs_6_), channel_id=1, source_target_pairs={{0,4},{4,0},{8,12},{12,8},{1,5},{5,1},{9,13},{13,9},{2,6},{6,2},{1... | collective-permute-start | bytes 49160 | tf_op jit(solution)/shard_map/ppermute | solution.py:343
  50.5 1.7 %collective-permute-done.10.refs_7_ = f32[32,128]{1,0:T(8,128)S(1)} collective-permute-done((f32[32,128]{1,0:T(8,128)S(1)}, f32[32,128]{1,0:T(8,128)S(1)}, u32[]{:S(2)}, u32[]{:S(2)}) %collective-permute-start.10) | collective-permute-done | bytes 16416 | tf_op jit(solution)/shard_map/ppermute | solution.py:343
  52.2 2.8 %scatter.3 = (f32[2,128,128]{2,1,0:T(8,128)S(1)}, f32[2,128,128]{2,1,0:T(8,128)S(1)}, f32[2,2,8,128]{3,2,1,0:T(8,128)S(1)}, f32[2,2,8,128]{3,2,1,0:T(8,128)S(1)}...) custom-call(f32[5,32,128]{2,1,0:T(8,128)S(1)} %prep.1.info.refs_0_.refs_5_, f32[5,32,128]{2,1,0:T(8,128)S(1)} %slice.16.refs_1_, ...), custom_call_target="tpu_custom_call" | custom-call | flops 6000000000 | bytes 1048576 | tf_op jit(solution)/shard_map/scatter/pallas_call | solution.py:320
  55.1 1.7 %collective-permute-start.13 = (f32[2,2,8,128]{3,2,1,0:T(8,128)S(1)}, f32[2,2,8,128]{3,2,1,0:T(8,128)S(1)}, u32[]{:S(2)}, u32[]{:S(2)}) collective-permute-start(f32[2,2,8,128]{3,2,1,0:T(8,128)S(1)} %get-tuple-element.56), channel_id=1, source_target_pairs={{1,0},{2,1},{3,2},{0,3},{5,4},{6,5},{7,6},{4,7},{9,8},{10,9},{11,1... | collective-permute-start | bytes 49160 | tf_op jit(solution)/shard_map/ppermute | solution.py:350
  59.8 1.5 %collective-permute-start.14 = (f32[32,128]{1,0:T(8,128)S(1)}, f32[32,128]{1,0:T(8,128)S(1)}, u32[]{:S(2)}, u32[]{:S(2)}) collective-permute-start(f32[32,128]{1,0:T(8,128)S(1)} %get-tuple-element.59.mine), channel_id=1, source_target_pairs={{0,16},{16,0},{1,17},{17,1},{2,18},{18,2},{3,19},{19,3},{4,20},{20... | collective-permute-start | bytes 49160 | tf_op jit(solution)/shard_map/ppermute | solution.py:356
  61.3 2.3 %collective-permute-done.14.other = f32[32,128]{1,0:T(8,128)S(1)} collective-permute-done((f32[32,128]{1,0:T(8,128)S(1)}, f32[32,128]{1,0:T(8,128)S(1)}, u32[]{:S(2)}, u32[]{:S(2)}) %collective-permute-start.14) | collective-permute-done | bytes 16416 | tf_op jit(solution)/shard_map/ppermute | solution.py:356
  64.7 11.2 %all_to_all.22 = f32[32,1,128]{2,1,0:T(1,128)S(1)} all-to-all(f32[32,1,128]{2,1,0:T(1,128)S(1)} %bitcast.25), channel_id=1, replica_groups=mesh['mem'=2,'gy'=4,'gx'=4] {'mem','gy','gx'}, dimensions={0} | all-to-all | bytes 32768 | tf_op jit(solution)/shard_map/all_to_all | solution.py:416
  75.9 1.4 %final.1 = (f32[2,128,128]{2,1,0:T(8,128)}, f32[5,64,128]{2,1,0:T(8,128)S(1)}, f32[5,64,128]{2,1,0:T(8,128)S(1)}) custom-call(s32[5]{0:T(128)S(1)} %stack.15.pos, f32[32,128]{1,0:T(8,128)S(1)} %bitcast.24, f32[2,128,128]{2,1,0:T(8,128)S(1)} %get-tuple-element.63.control, f32[2,128,128]{2,1,0:T(8,128)S(1)} %get-tuple-element.64.smoothed, ...), custom_call_target="tpu_custom_call" | custom-call | flops 3000000000 | bytes 1048576 | tf_op jit(solution)/shard_map/final/pallas_call | solution.py:320
  78.0 5.4 %collective-permute-done.15 = f32[5,64,128]{2,1,0:T(8,128)S(1)} collective-permute-done((f32[5,64,128]{2,1,0:T(8,128)S(1)}, f32[5,64,128]{2,1,0:T(8,128)S(1)}, u32[]{:S(2)}, u32[]{:S(2)}) %collective-permute-start.15) | collective-permute-done | bytes 163872 | tf_op jit(solution)/shard_map/ppermute | solution.py:421
  (44 shorter events, 13.2 us)
Async XLA Ops:
  0.6 8.3 %collective-permute-start.1 = (f32[2,128,128]{2,1,0:T(8,128)}, f32[2,128,128]{2,1,0:T(8,128)S(1)}, u32[]{:S(2)}, u32[]{:S(2)}) collective-permute-start(f32[2,128,128]{2,1,0:T(8,128)} %bitcast.28), channel_id=1, source_target_pairs={{0,0},{4,8},{8,4},{12,12},{1,1},{5,9},{9,5},{13,13},{2,2},{6,10},{... | collective-permute-start | bytes 393224 | tf_op jit(solution)/shard_map/ppermute | solution.py:343
  2.2 8.5 %collective-permute-start = (f32[2,128,128]{2,1,0:T(8,128)}, f32[2,128,128]{2,1,0:T(8,128)S(1)}, u32[]{:S(2)}, u32[]{:S(2)}) collective-permute-start(f32[2,128,128]{2,1,0:T(8,128)} %bitcast.29), channel_id=1, source_target_pairs={{0,4},{4,0},{8,12},{12,8},{1,5},{5,1},{9,13},{13,9},{2,6},{6,2},{1... | collective-permute-start | bytes 393224 | tf_op jit(solution)/shard_map/ppermute | solution.py:343
  7.3 3.3 %copy-start.1 = (f32[2,16,8,128]{3,2,1,0:T(8,128)S(1)}, f32[2,16,8,128]{3,2,1,0:T(8,128)}, u32[]{:S(2)}) copy-start(f32[2,16,8,128]{3,2,1,0:T(8,128)} %param.8) | copy-start | bytes 393220
  10.7 2.4 %copy-start = (bf16[2,5,16,8,128]{4,3,2,1,0:T(8,128)(2,1)S(1)}, bf16[2,5,16,8,128]{4,3,2,1,0:T(8,128)(2,1)}, u32[]{:S(2)}) copy-start(bf16[2,5,16,8,128]{4,3,2,1,0:T(8,128)(2,1)} %param.7) | copy-start | bytes 983044
  10.7 2.4 %copy-start.2 = (s32[32,128]{1,0:T(8,128)S(1)}, s32[32,128]{1,0:T(8,128)}, u32[]{:S(2)}) copy-start(s32[32,128]{1,0:T(8,128)} %cell.1) | copy-start | bytes 49156
  10.7 2.4 %copy-start.3 = (s32[32,128]{1,0:T(8,128)S(1)}, s32[32,128]{1,0:T(8,128)}, u32[]{:S(2)}) copy-start(s32[32,128]{1,0:T(8,128)} %flag.1) | copy-start | bytes 49156
  10.7 2.4 %copy-start.4 = (f32[32,128]{1,0:T(8,128)S(1)}, f32[32,128]{1,0:T(8,128)}, u32[]{:S(2)}) copy-start(f32[32,128]{1,0:T(8,128)} %innov.1) | copy-start | bytes 49156
  10.7 2.4 %copy-start.5 = (f32[32,128]{1,0:T(8,128)S(1)}, f32[32,128]{1,0:T(8,128)}, u32[]{:S(2)}) copy-start(f32[32,128]{1,0:T(8,128)} %prec.1) | copy-start | bytes 49156
  11.2 4.1 %collective-permute-start.2 = (f32[2,8,128]{2,1,0:T(8,128)S(1)}, f32[2,8,128]{2,1,0:T(8,128)S(1)}, u32[]{:S(2)}, u32[]{:S(2)}) collective-permute-start(f32[2,8,128]{2,1,0:T(8,128)S(1)} %get-tuple-element.38), channel_id=1, source_target_pairs={{0,1},{1,2},{2,3},{3,0},{4,5},{5,6},{6,7},{7,4},{8,9},{9,10},{10,1... | collective-permute-start | bytes 24584 | tf_op jit(solution)/shard_map/ppermute | solution.py:350
  11.3 4.0 %collective-permute-start.3 = (f32[2,8,128]{2,1,0:T(8,128)S(1)}, f32[2,8,128]{2,1,0:T(8,128)S(1)}, u32[]{:S(2)}, u32[]{:S(2)}) collective-permute-start(f32[2,8,128]{2,1,0:T(8,128)S(1)} %get-tuple-element.39), channel_id=1, source_target_pairs={{1,0},{2,1},{3,2},{0,3},{5,4},{6,5},{7,6},{4,7},{9,8},{10,9},{11,1... | collective-permute-start | bytes 24584 | tf_op jit(solution)/shard_map/ppermute | solution.py:350
  16.7 3.8 %collective-permute-start.4 = (f32[32,128]{1,0:T(8,128)S(1)}, f32[32,128]{1,0:T(8,128)S(1)}, u32[]{:S(2)}, u32[]{:S(2)}) collective-permute-start(f32[32,128]{1,0:T(8,128)S(1)} %get-tuple-element.41), channel_id=1, source_target_pairs={{0,16},{16,0},{1,17},{17,1},{2,18},{18,2},{3,19},{19,3},{4,20},{20... | collective-permute-start | bytes 49160 | tf_op jit(solution)/shard_map/ppermute | solution.py:356
  20.6 4.2 %collective-permute-start.6 = (f32[6,32,128]{2,1,0:T(8,128)S(1)}, f32[6,32,128]{2,1,0:T(8,128)S(1)}, u32[]{:S(2)}, u32[]{:S(2)}) collective-permute-start(f32[6,32,128]{2,1,0:T(8,128)S(1)} %pad_maximum_fusion), channel_id=1, source_target_pairs={{0,0},{4,8},{8,4},{12,12},{1,1},{5,9},{9,5},{13,13},{2,2},{6,10},{... | collective-permute-start | bytes 294920 | tf_op jit(solution)/shard_map/ppermute | solution.py:343
  21.2 6.1 %collective-permute-start.5 = (f32[6,32,128]{2,1,0:T(8,128)S(1)}, f32[6,32,128]{2,1,0:T(8,128)S(1)}, u32[]{:S(2)}, u32[]{:S(2)}) collective-permute-start(f32[6,32,128]{2,1,0:T(8,128)S(1)} %pad_maximum_fusion), channel_id=1, source_target_pairs={{0,4},{4,0},{8,12},{12,8},{1,5},{5,1},{9,13},{13,9},{2,6},{6,2},{1... | collective-permute-start | bytes 294920 | tf_op jit(solution)/shard_map/ppermute | solution.py:343
  30.1 3.2 %collective-permute-start.7 = (f32[2,2,8,128]{3,2,1,0:T(8,128)S(1)}, f32[2,2,8,128]{3,2,1,0:T(8,128)S(1)}, u32[]{:S(2)}, u32[]{:S(2)}) collective-permute-start(f32[2,2,8,128]{3,2,1,0:T(8,128)S(1)} %get-tuple-element.44), channel_id=1, source_target_pairs={{0,1},{1,2},{2,3},{3,0},{4,5},{5,6},{6,7},{7,4},{8,9},{9,10},{10,1... | collective-permute-start | bytes 49160 | tf_op jit(solution)/shard_map/ppermute | solution.py:350
  30.2 3.2 %collective-permute-start.8 = (f32[2,2,8,128]{3,2,1,0:T(8,128)S(1)}, f32[2,2,8,128]{3,2,1,0:T(8,128)S(1)}, u32[]{:S(2)}, u32[]{:S(2)}) collective-permute-start(f32[2,2,8,128]{3,2,1,0:T(8,128)S(1)} %get-tuple-element.45), channel_id=1, source_target_pairs={{1,0},{2,1},{3,2},{0,3},{5,4},{6,5},{7,6},{4,7},{9,8},{10,9},{11,1... | collective-permute-start | bytes 49160 | tf_op jit(solution)/shard_map/ppermute | solution.py:350
  34.8 3.8 %collective-permute-start.9 = (f32[32,128]{1,0:T(8,128)S(1)}, f32[32,128]{1,0:T(8,128)S(1)}, u32[]{:S(2)}, u32[]{:S(2)}) collective-permute-start(f32[32,128]{1,0:T(8,128)S(1)} %get-tuple-element.48.mine), channel_id=1, source_target_pairs={{0,16},{16,0},{1,17},{17,1},{2,18},{18,2},{3,19},{19,3},{4,20},{20... | collective-permute-start | bytes 49160 | tf_op jit(solution)/shard_map/ppermute | solution.py:356
  39.8 12.4 %all-to-all-start = ((f32[32,1,128]{2,1,0:T(1,128)}), f32[32,1,128]{2,1,0:T(1,128)S(1)}, u32[]{:S(2)}, u32[]{:S(2)}) async-start(f32[32,1,128]{2,1,0:T(1,128)} %bitcast.9), calls=%async_computation | async-start | bytes 32768 | tf_op jit(solution)/shard_map/all_to_all | solution.py:416
  45.1 5.4 %collective-permute-start.11 = (f32[32,128]{1,0:T(8,128)S(1)}, f32[32,128]{1,0:T(8,128)S(1)}, u32[]{:S(2)}, u32[]{:S(2)}) collective-permute-start(f32[32,128]{1,0:T(8,128)S(1)} %get-tuple-element.51.refs_6_), channel_id=1, source_target_pairs={{0,0},{4,8},{8,4},{12,12},{1,1},{5,9},{9,5},{13,13},{2,2},{6,10},{... | collective-permute-start | bytes 49160 | tf_op jit(solution)/shard_map/ppermute | solution.py:343
  46.0 6.3 %collective-permute-start.10 = (f32[32,128]{1,0:T(8,128)S(1)}, f32[32,128]{1,0:T(8,128)S(1)}, u32[]{:S(2)}, u32[]{:S(2)}) collective-permute-start(f32[32,128]{1,0:T(8,128)S(1)} %get-tuple-element.51.refs_6_), channel_id=1, source_target_pairs={{0,4},{4,0},{8,12},{12,8},{1,5},{5,1},{9,13},{13,9},{2,6},{6,2},{1... | collective-permute-start | bytes 49160 | tf_op jit(solution)/shard_map/ppermute | solution.py:343
  55.1 3.2 %collective-permute-start.12 = (f32[2,2,8,128]{3,2,1,0:T(8,128)S(1)}, f32[2,2,8,128]{3,2,1,0:T(8,128)S(1)}, u32[]{:S(2)}, u32[]{:S(2)}) collective-permute-start(f32[2,2,8,128]{3,2,1,0:T(8,128)S(1)} %get-tuple-element.55), channel_id=1, source_target_pairs={{0,1},{1,2},{2,3},{3,0},{4,5},{5,6},{6,7},{7,4},{8,9},{9,10},{10,1... | collective-permute-start | bytes 49160 | tf_op jit(solution)/shard_map/ppermute | solution.py:350
  55.1 3.2 %collective-permute-start.13 = (f32[2,2,8,128]{3,2,1,0:T(8,128)S(1)}, f32[2,2,8,128]{3,2,1,0:T(8,128)S(1)}, u32[]{:S(2)}, u32[]{:S(2)}) collective-permute-start(f32[2,2,8,128]{3,2,1,0:T(8,128)S(1)} %get-tuple-element.56), channel_id=1, source_target_pairs={{1,0},{2,1},{3,2},{0,3},{5,4},{6,5},{7,6},{4,7},{9,8},{10,9},{11,1... | collective-permute-start | bytes 49160 | tf_op jit(solution)/shard_map/ppermute | solution.py:350
  59.8 3.8 %collective-permute-start.14 = (f32[32,128]{1,0:T(8,128)S(1)}, f32[32,128]{1,0:T(8,128)S(1)}, u32[]{:S(2)}, u32[]{:S(2)}) collective-permute-start(f32[32,128]{1,0:T(8,128)S(1)} %get-tuple-element.59.mine), channel_id=1, source_target_pairs={{0,16},{16,0},{1,17},{17,1},{2,18},{18,2},{3,19},{19,3},{4,20},{20... | collective-permute-start | bytes 49160 | tf_op jit(solution)/shard_map/ppermute | solution.py:356
  75.9 7.4 %copy-start.6 = (f32[5,8,8,128]{3,2,1,0:T(8,128)S(1)}, f32[5,8,8,128]{3,2,1,0:T(8,128)}, u32[]{:S(2)}) copy-start(f32[5,8,8,128]{3,2,1,0:T(8,128)} %param.9) | copy-start | bytes 491524
  77.4 6.0 %collective-permute-start.15 = (f32[5,64,128]{2,1,0:T(8,128)S(1)}, f32[5,64,128]{2,1,0:T(8,128)S(1)}, u32[]{:S(2)}, u32[]{:S(2)}) collective-permute-start(f32[5,64,128]{2,1,0:T(8,128)S(1)} %get-tuple-element.68), channel_id=1, source_target_pairs={{0,16},{16,0},{1,17},{17,1},{2,18},{18,2},{3,19},{19,3},{4,20},{20... | collective-permute-start | bytes 491528 | tf_op jit(solution)/shard_map/ppermute | solution.py:421

commit v3 on v2

v3 whole, which is shorter than its diff:
```python
import functools
import math

import jax
import jax.numpy as jnp
from jax import lax
from jax.experimental import pallas as pl
from jax.experimental.pallas import tpu as pltpu
from jax.sharding import PartitionSpec as P


ITERS = 2
RADIUS = 4
RAW = [math.exp(-o * o / 8.0) for o in range(-RADIUS, RADIUS + 1)]
TAPS = [r / sum(RAW) for r in RAW]
HALO = 2 * RADIUS
F32 = jnp.float32
BF16 = jnp.bfloat16
EXACT = lax.Precision.HIGHEST
CHUNK = 4


def iota(shape, dim):
    return lax.broadcasted_iota(jnp.int32, shape, dim)


def over(k, n):
    return lax.shift_right_logical(k, n.bit_length() - 1) if n & (n - 1) == 0 else k // n


def rem(k, n):
    return k & (n - 1) if n & (n - 1) == 0 else k % n


def tap(d):
    d = jnp.abs(d)
    value = jnp.zeros(d.shape, F32)
    for o in range(RADIUS + 1):
        value = jnp.where(d == o, TAPS[RADIUS + o], value)
    return value


def exact_dot(a, b):
    return jnp.dot(a, b, precision=EXACT, preferred_element_type=F32)


def halves(f32):
    high = f32.astype(BF16)
    low = (f32 - high.astype(F32)).astype(BF16)
    return high, low


def at_lane_block(shape, wide, s):
    return over(iota(shape, 1), wide) == s


def moved(piece, source, target, wide):
    if source == target:
        return piece
    return pltpu.roll(piece, (target - source) * wide % piece.shape[1], 1)


def chunks(tx, wide, lanes):
    parts = 2 * lanes // wide
    return parts, tx // parts


def to_table(groups, wide):
    tx, lanes = groups[0].shape
    parts, short = chunks(tx, wide, lanes)
    per = lanes // wide
    tables = []
    for group in groups:
        for m in range(per):
            blocks = []
            for p in range(parts // per):
                block = None
                for s in range(per):
                    at = (p * per + s) * short
                    piece = moved(group[at : at + short], m, s, wide)
                    block = piece if block is None else jnp.where(at_lane_block(piece.shape, wide, s), piece, block)
                blocks.append(block)
            tables.append(jnp.concatenate(blocks, axis=1))
    return tables


def from_table(tables, wide, lanes):
    per = lanes // wide
    parts = tables[0].shape[1] // wide
    groups = []
    for first in range(0, len(tables), per):
        rows = []
        for x in range(parts):
            p, s = x // per, x % per
            block = None
            for m in range(per):
                piece = moved(tables[first + m][:, p * lanes : (p + 1) * lanes], s, m, wide)
                block = piece if block is None else jnp.where(at_lane_block(piece.shape, wide, m), piece, block)
            rows.append(block)
        groups.append(jnp.concatenate(rows, axis=0))
    return groups


def split_x(field):
    half = field.shape[0] // 2
    return jnp.concatenate([field[:half], field[half:]], axis=1)


def onehot_rows(index, rows):
    wide = jnp.broadcast_to(index, (rows, index.shape[1]))
    return jnp.where(iota(wide.shape, 0) == wide, 1.0, 0.0).astype(BF16)


def chunk_of(ref, j):
    return jnp.concatenate([ref[j + i : j + i + 1, :] for i in range(CHUNK)], axis=1)


def store_chunk(ref, j, row):
    wide = row.shape[1] // CHUNK
    for i in range(CHUNK):
        ref[j + i : j + i + 1, :] = row[:, i * wide : (i + 1) * wide]


def pair_side(index):
    return jnp.where(rem(index, 2) == 0, 1, -1)


def y_geometry(k, zy, ty):
    gy, ngy = lax.axis_index("gy"), lax.axis_size("gy")
    tile, at = over(k, zy), rem(k, zy)
    side = pair_side(gy)
    where = gy + jnp.where(tile == 0, 0, jnp.where(tile == 1, side, -side))
    return over(at, ty), where * ty + rem(at, ty), (where >= 0) & (where < ngy)


def matrices(ty, ky, ky_first, kx):
    wide, zy = ky.shape[0], ky.shape[1] // 2
    tx = kx.shape[1]

    def along_y(shape):
        zs, ys, oks = y_geometry(iota(shape, 0), zy, ty)
        zt, yt, okt = y_geometry(iota(shape, 1), zy, ty)
        return jnp.where((zs == zt) & oks & okt, tap(ys - yt), 0.0)

    once = along_y((wide, zy))
    ky[:, :zy] = once
    ky[:, zy:] = exact_dot(along_y((wide, wide)), once)

    shape = ky_first.shape
    k = iota(shape, 0)
    gy, ngy = lax.axis_index("gy"), lax.axis_size("gy")
    tile = jnp.where(k < zy, 0, jnp.where(k < zy + zy * RADIUS // ty, 1, 2))
    at = k - jnp.where(tile == 0, 0, jnp.where(tile == 1, zy, zy + zy * RADIUS // ty))
    side = jnp.where(tile == 1, pair_side(gy), -pair_side(gy))
    strip_row = (gy + side) * ty + rem(at, RADIUS) + jnp.where(side == 1, 0, ty - RADIUS)
    row = jnp.where(tile == 0, gy * ty + rem(at, ty), strip_row)
    level = jnp.where(tile == 0, over(at, ty), over(at, RADIUS))
    zt, yt, _ = y_geometry(iota(shape, 1), zy, ty)
    ky_first[...] = jnp.where((level == zt) & (row >= 0) & (row < ngy * ty), tap(row - yt), 0.0)
    gx, ngx = lax.axis_index("gx"), lax.axis_size("gx")
    side = pair_side(gx)

    def x_of(k):
        tile, r = jnp.where(k < tx, 0, jnp.where(k < tx + HALO, 1, 2)), rem(k - tx, HALO)
        right = (tile == 1) == (side == 1)
        at = jnp.where(tile == 0, k, jnp.where(right, tx + r, r - HALO))
        full = gx * tx + at
        return at, (full >= 0) & (full < ngx * tx)

    def along_x(shape):
        xt, okt = x_of(iota(shape, 0))
        xs, oks = x_of(iota(shape, 1))
        return jnp.where(oks & okt, tap(xs - xt), 0.0)

    long = tx + 2 * HALO
    kx[0] = along_x((tx, long))
    kx[1] = exact_dot(along_x((tx, long)), along_x((long, long)))


def halves_kernel(control, mine, theirs, sems):
    members, zy, _ = control.shape
    wide = zy // 2
    mem = lax.axis_index("mem")
    copies = []
    for m in range(members):
        for i, (target, part) in enumerate(((theirs, 1 - mem), (mine, mem))):
            source = control.at[m, pl.ds(pl.multiple_of(part * wide, wide), wide), :]
            copies.append(pltpu.make_async_copy(source, target.at[pl.ds(m * wide, wide), :], sems.at[m, i]))
    for copy in copies:
        copy.start()
    for copy in copies:
        copy.wait()


def strips_kernel(ty, *refs):
    *blocks, first, second = refs
    lanes, tx = blocks[0].shape
    next_first = pair_side(lax.axis_index("gy")) == 1
    rows = lanes * RADIUS // ty
    for b, block in enumerate(blocks):
        value = block[...].reshape(lanes // (2 * ty), 2, ty, tx)
        even, odd = value[:, 0], value[:, 1]
        low = iota(even.shape, 1) < RADIUS
        last = jnp.where(low, pltpu.roll(even, RADIUS, 1), odd).reshape(rows, tx)
        initial = jnp.where(low, even, pltpu.roll(odd, RADIUS, 1)).reshape(rows, tx)
        first[b * rows : (b + 1) * rows] = jnp.where(next_first, last, initial)
        second[b * rows : (b + 1) * rows] = jnp.where(next_first, initial, last)


def prep_kernel(ty, wide, pert_in, cell_in, flag_in, innov_in, prec_in, info, pobs, ky, ky_first, kx, table, pert, cell, flag, innov, prec, sems):
    members, variables, zy, tx = pert.shape
    pairs = [(pert_in, pert), (cell_in, cell), (flag_in, flag), (innov_in, innov), (prec_in, prec)]
    copies = [pltpu.make_async_copy(a, b, sems.at[i]) for i, (a, b) in enumerate(pairs)]
    for copy in copies:
        copy.start()
    matrices(ty, ky, ky_first, kx)
    for copy in copies:
        copy.wait()
    half = tx // 2
    for m in range(members):
        for v in range(variables):
            block = split_x(pert[m, v].astype(F32).T)
            at = (m * variables + v) * half
            table[at : at + half, :] = block.astype(BF16)
    for j in range(0, cell.shape[0], CHUNK):
        k = chunk_of(cell, j)
        x, level_row = rem(k, tx), rem(over(k, tx), zy)
        hot = onehot_rows(over(x, half) * zy + level_row, 2 * zy)
        found = jnp.dot(table[...], hot, preferred_element_type=F32)
        want = over(k, tx * zy) * half + rem(x, half)
        rows = variables * half
        mask = iota((rows, k.shape[1]), 0) == jnp.broadcast_to(want, (rows, k.shape[1]))
        for m in range(members):
            got = jnp.where(mask, found[m * rows : (m + 1) * rows], 0.0)
            store_chunk(pobs.at[m], j, jnp.sum(got, axis=0, keepdims=True))
    k = cell[...]
    _, short = chunks(tx, wide, kx.shape[1])
    x = rem(k, tx)
    level_row = rem(over(k, tx), zy) - lax.axis_index("mem") * wide
    code = (over(x, short) * wide + level_row) * short + rem(x, short)
    info[0] = jnp.where((level_row >= 0) & (level_row < wide), code, -short).astype(F32)
    info[1] = jnp.where(flag[...] == 1, -prec[...], prec[...])
    info[2] = innov[...]


def decode(code, short):
    code = code.astype(jnp.int32)
    shift = short.bit_length() - 1
    return lax.shift_right_arithmetic(code, shift), code & (short - 1)


def send_strips(first, second, at, field):
    right, left = field[field.shape[0] - HALO :], field[:HALO]
    even = pair_side(lax.axis_index("gx")) == 1
    first[at] = jnp.where(even, right, left)
    second[at] = jnp.where(even, left, right)


def start_kernel(blocks, parts, *refs):
    tiles, refs = refs[:blocks], refs[blocks:]
    before, after, ky_first, info, refs = refs[0], refs[1], refs[2], refs[3], refs[4:]
    pobs, (y1, state, first, second, pack) = refs[:parts], refs[parts:]
    rows = before.shape[0] // blocks
    for b in range(blocks):
        own = tiles[b][...]
        at = slice(b * rows, (b + 1) * rows)
        wide = jnp.concatenate([own, before[at], after[at]], axis=0).T
        out = exact_dot(wide, ky_first[...])
        state[b] = wide[:, : own.shape[0]]
        y1[b] = out
        send_strips(first, second, b, out)
    pack[0:3] = info[...]
    at = 3
    for part in pobs:
        pack[at : at + part.shape[0]] = part[...]
        at += part.shape[0]


def x_smooth(matrix, fields, firsts, seconds):
    wide = [jnp.concatenate([f, l, r], axis=0) for f, l, r in zip(fields, firsts, seconds)]
    out = exact_dot(matrix, jnp.concatenate(wide, axis=1))
    zy = fields[0].shape[1]
    return [out[:, i * zy : (i + 1) * zy] for i in range(len(fields))]


def gather_at(groups, wide, pack, seen):
    tables = to_table(groups, wide)
    members, short = len(tables), tables[0].shape[0]
    parts = [halves(t) for t in tables]
    stacked = jnp.concatenate([p[0] for p in parts] + [p[1] for p in parts], axis=0)
    rows = members * short
    for j in range(0, pack.shape[1], CHUNK):
        row, low = decode(chunk_of(pack.at[0], j), short)
        hot = onehot_rows(row, stacked.shape[1])
        found = jnp.dot(stacked, hot, preferred_element_type=F32)
        low = jnp.broadcast_to(low, (short, low.shape[1]))
        mask = iota(low.shape, 0) == low
        total = None
        for m in range(members):
            both = found[m * short : (m + 1) * short] + found[rows + m * short : rows + (m + 1) * short]
            term = jnp.where(mask, both, 0.0) * jnp.broadcast_to(chunk_of(pack.at[3 + m], j), both.shape)
            total = term if total is None else total + term
        store_chunk(seen, j, jnp.sum(total, axis=0, keepdims=True))


def first_seen_kernel(wide, y1, from_first, from_second, kx, pack, smoothed, seen):
    each = range(y1.shape[0])
    outs = x_smooth(kx[0], [y1[b] for b in each], [from_first[b] for b in each], [from_second[b] for b in each])
    for b in each:
        smoothed[b] = outs[b]
    gather_at(outs, wide, pack, seen)


def step_rows(sums):
    total = jnp.sum(sums, axis=0, keepdims=True)
    lane = iota(total.shape, 1)
    g = jnp.sum(jnp.where(lane == 0, total, 0.0), axis=1, keepdims=True)
    c = jnp.sum(jnp.where(lane == 1, total, 0.0), axis=1, keepdims=True)
    return g / (g + c)


def scatter_kernel(has_step, wide, *refs):
    packs, incs = refs[0:3], refs[3:6]
    refs = refs[6:]
    if has_step:
        steps, sums = refs[0:3], refs[3]
        refs = refs[4:]
        step = step_rows(sums[...])
    ky, y1, y2, first, second, weights, vals = refs
    blocks, tx, lanes = y1.shape
    members = packs[0].shape[0] - 3
    parts, short = chunks(tx, wide, lanes)
    tiles = []
    for t in range(3):
        pack = packs[t]
        inc = incs[t][...]
        if has_step:
            inc = inc - step * steps[t][...]
        misfit = inc - pack[2]
        prec = pack[1]
        weight = jnp.where(prec < 0, 1.0 / jnp.sqrt(1.0 + misfit * misfit), 1.0)
        pw = jnp.abs(prec) * weight
        q = pw * misfit
        if t == 0:
            weights[...] = pw
        for m in range(members):
            val = pack[3 + m] * q
            high = val.astype(BF16).astype(F32)
            vals[2 * m] = high
            vals[2 * m + 1] = val - high
        acc = None
        for j in range(0, pack.shape[1], CHUNK):
            row, low = decode(chunk_of(pack.at[0], j), short)
            hot = onehot_rows(row, parts * wide)
            low = jnp.broadcast_to(low, (short, low.shape[1]))
            mask = iota(low.shape, 0) == low
            rows = []
            for i in range(2 * members):
                value = jnp.broadcast_to(chunk_of(vals.at[i], j), low.shape)
                rows.append(jnp.where(mask, value, 0.0).astype(BF16))
            part = lax.dot_general(jnp.concatenate(rows, axis=0), hot, (((1,), (1,)), ((), ())), preferred_element_type=F32)
            acc = part if acc is None else acc + part
        tables = []
        for m in range(members):
            at = 2 * m * short
            tables.append(acc[at : at + short] + acc[at + short : at + 2 * short])
        tiles.append(jnp.concatenate(from_table(tables, wide, lanes), axis=0))
    out = exact_dot(jnp.concatenate(tiles, axis=1), ky[...])
    for b in range(blocks):
        for i, y in enumerate((y1, y2)):
            field = out[b * tx : (b + 1) * tx, i * lanes : (i + 1) * lanes]
            y[b] = field
            send_strips(first, second, (i, b), field)


def gather_kernel(has_step, wide, *refs):
    y1, y2, from_first, from_second, kx, pack, weights, control, smoothed = refs[:9]
    refs = refs[9:]
    each = range(y1.shape[0])
    if has_step:
        old_grad, old_smooth, sums, new_control, new_smoothed = refs[:5]
        refs = refs[5:]
        step = step_rows(sums[...])
    grad_out, smooth_out, seen, to_all = refs[:4]
    once = x_smooth(kx[0], [y1[b] for b in each], [from_first[0, b] for b in each], [from_second[0, b] for b in each])
    twice = x_smooth(kx[1], [y2[b] for b in each], [from_first[1, b] for b in each], [from_second[1, b] for b in each])
    squares = None
    outs = []
    for b in each:
        v, s = control[b], smoothed[b]
        if has_step:
            v = v - step * old_grad[b]
            s = s - step * old_smooth[b]
            new_control[b] = v
            new_smoothed[b] = s
        grad = v + once[b]
        smooth_grad = s + twice[b]
        grad_out[b] = grad
        smooth_out[b] = smooth_grad
        outs.append(smooth_grad)
        part = jnp.sum(grad * grad, axis=0, keepdims=True)
        squares = part if squares is None else squares + part
        if len(refs) > 4 and b == y1.shape[0] - 1:
            refs[4][0] = v
            refs[4][1] = grad
    gather_at(outs, wide, pack, seen)
    total = seen[...]
    c = jnp.sum(jnp.sum(weights[...] * total * total, axis=0, keepdims=True), axis=1, keepdims=True)
    g = jnp.sum(squares, axis=1, keepdims=True)
    lane = iota(to_all.shape, 1)
    to_all[...] = jnp.where(lane == 0, g, jnp.where(lane == 1, c, 0.0))


def widen_kernel(pert, out):
    members, variables, zy, _ = pert.shape
    wide = zy // 2
    other = 1 - lax.axis_index("mem")
    for m in range(members):
        for v in range(variables):
            out[m, v] = pert[m, v, pl.ds(other * wide, wide), :].astype(F32)


def analysis_of(perts, smoothed, background, analysis, wide):
    variables = background.shape[0]
    for v in range(variables):
        inc = background[v]
        for m, pert in enumerate(perts):
            inc = inc + pert(v) * smoothed[m * wide : (m + 1) * wide]
        analysis[v] = inc


def final_pair_kernel(sums, control, grad, back, smoothed, smooth_grad, pert, pert_other, background, control_out, analysis):
    members, _, zy, _ = pert.shape
    wide = zy // 2
    mem = lax.axis_index("mem")
    step = step_rows(sums[...])
    mine = (control[0] - step * grad[0]).T
    other = (back[0] - step * back[1]).T
    for m in range(members):
        control_out[m, pl.ds(mem * wide, wide), :] = mine[m * wide : (m + 1) * wide]
        control_out[m, pl.ds((1 - mem) * wide, wide), :] = other[m * wide : (m + 1) * wide]
    fields = jnp.concatenate([(smoothed[b] - step * smooth_grad[b]).T for b in range(smoothed.shape[0])], axis=0)
    perts = [lambda v, m=m: pert[m, v, pl.ds(mem * wide, wide), :].astype(F32) for m in range(members)]
    perts += [lambda v, m=m: pert_other[m, v] for m in range(members)]
    analysis_of(perts, fields, background, analysis, wide)


def final_any_kernel(sums, control, grad, smoothed, smooth_grad, pert, background, control_out, analysis):
    members, _, wide, _ = pert.shape
    step = step_rows(sums[...])
    lanes = control.shape[2]
    for b in range(control.shape[0]):
        control_out[b * lanes : (b + 1) * lanes] = (control[b] - step * grad[b]).T
    fields = jnp.concatenate([(smoothed[b] - step * smooth_grad[b]).T for b in range(smoothed.shape[0])], axis=0)
    analysis_of([lambda v, m=m: pert[m, v] for m in range(members)], fields, background, analysis, wide)


VMEM = pl.BlockSpec(memory_space=pltpu.VMEM)


HBM = pl.BlockSpec(memory_space=pltpu.HBM)


def call(kernel, ins, outs, scratch=(), us=3.0, space=VMEM):
    shapes = [jax.ShapeDtypeStruct(s, F32) for s in outs]
    return pl.pallas_call(
        kernel,
        out_shape=shapes,
        in_specs=[space] * len(ins),
        out_specs=[VMEM] * len(outs),
        scratch_shapes=list(scratch),
        compiler_params=pltpu.CompilerParams(vmem_limit_bytes=16 << 20),
        cost_estimate=pl.CostEstimate(flops=int(us * 1e9), bytes_accessed=1 << 20, transcendentals=0),
    )(*ins)


def first_partner(i, n):
    return i ^ 1 if i ^ 1 < n else i


def second_partner(i, n):
    return (((i + 1) ^ 1) - 1) % n


def swap_first(value, axis):
    n = lax.axis_size(axis)
    return lax.ppermute(value, axis, [(i, first_partner(i, n)) for i in range(n)])


def swap_second(value, axis):
    n, k = lax.axis_size(axis), lax.axis_size("gx")
    if axis == "gx":
        return lax.ppermute(value, axis, [(i, second_partner(i, n)) for i in range(n)])
    sends = []
    for i in range(n):
        to = ((i + 1) ^ 1) - 1
        for g in range(k):
            sends.append((i * k + g, to * k + g if 0 <= to < n else i * k + first_partner(g, k)))
    return lax.ppermute(value, (axis, "gx"), sends)


def swap_pairs(value, axis):
    return [swap_first(value, axis), swap_second(value, axis)]


def swap_each(first, second, axis):
    return swap_first(first, axis), swap_second(second, axis)


def swap_mem(value):
    return lax.ppermute(value, "mem", [(0, 1), (1, 0)])


def levels_out(value):
    n = lax.axis_size("mem")
    wide = value.shape[-2] // n
    cut = value.reshape(value.shape[:-2] + (n, wide) + value.shape[-1:])
    sent = jnp.moveaxis(cut, -3, 0)
    got = lax.all_to_all(sent, "mem", 0, 0, tiled=True)
    return got.reshape((n * value.shape[0],) + value.shape[1:-2] + (wide,) + value.shape[-1:])


def per_device(perturbations, control, background, obs_cell, huber_flag, innovation, precision):
    members, variables, nz, ty, tx = perturbations.shape
    zy, n_mem = nz * ty, lax.axis_size("mem")
    wide = zy // n_mem
    lanes = 128
    blocks = members * zy // lanes
    obs = obs_cell.shape
    axes = ("mem", "gy", "gx")
    n_all = math.prod(lax.axis_size(a) for a in axes)
    everyone = members * n_mem
    pert = perturbations.reshape(members, variables, zy, tx)
    own = control.reshape(members, zy, tx)
    field = (blocks, tx, lanes)
    strip = (blocks, HALO, lanes)
    pair = n_mem == 2 and members * wide == lanes

    if pair:
        theirs, mine = call(
            lambda c, a, b, t: halves_kernel(c, b, a, t),
            [own],
            [(lanes, tx)] * 2,
            [pltpu.SemaphoreType.DMA((members, 2))],
            us=1.0,
            space=HBM,
        )
        tiles = [mine, swap_mem(theirs)]
    else:
        spread = levels_out(own).reshape(blocks * lanes, tx)
        tiles = [spread[b * lanes : (b + 1) * lanes] for b in range(blocks)]
    info, pobs, ky, ky_first, kx = call(
        functools.partial(prep_kernel, ty, wide),
        [pert, obs_cell, huber_flag, innovation, precision],
        [(3,) + obs, (members,) + obs, (3 * lanes, 2 * lanes), (lanes + 2 * lanes * RADIUS // ty, lanes), (2, tx, tx + 2 * HALO)],
        [
            pltpu.VMEM((members * variables * tx // 2, 2 * zy), BF16),
            pltpu.VMEM(pert.shape, BF16),
            pltpu.VMEM(obs, jnp.int32),
            pltpu.VMEM(obs, jnp.int32),
            pltpu.VMEM(obs, F32),
            pltpu.VMEM(obs, F32),
            pltpu.SemaphoreType.DMA((5,)),
        ],
        us=4.0,
        space=HBM,
    )
    first, second = call(functools.partial(strips_kernel, ty), tiles, [(blocks * lanes * RADIUS // ty, tx)] * 2, us=0.5)
    before, after = swap_each(first, second, "gy")
    if pair:
        pobs_parts = [pobs, swap_mem(pobs)]
    else:
        pobs_parts = [lax.all_gather(pobs, "mem", axis=0, tiled=True)]
    y1, state, first, second, pack = call(
        functools.partial(start_kernel, blocks, len(pobs_parts)),
        tiles + [before, after, ky_first, info] + pobs_parts,
        [field, field, strip, strip, (3 + everyone,) + obs],
        us=1.0,
    )
    from_first, from_second = swap_each(first, second, "gx")
    packs = [pack] + swap_pairs(pack, "gy")
    smoothed, seen = call(functools.partial(first_seen_kernel, wide), [y1, from_first, from_second, kx, pack], [field, obs], us=1.5)
    incs = [seen] + swap_pairs(seen, "gy")
    steps, sums, grad, smooth_grad = None, None, None, None
    double = (2,) + strip
    for iteration in range(ITERS):
        later, last = iteration > 0, iteration + 1 == ITERS
        ins = packs + incs + (steps + [sums] if later else []) + [ky]
        y1, y2, first, second, weights = call(
            functools.partial(scatter_kernel, later, wide),
            ins,
            [field, field, double, double, obs],
            [pltpu.VMEM((2 * everyone,) + obs, F32)],
            us=3.0,
        )
        from_first, from_second = swap_each(first, second, "gx")
        ins = [y1, y2, from_first, from_second, kx, pack, weights, state, smoothed]
        outs = [field, field, obs, (n_all, 128)]
        if later:
            ins += [grad, smooth_grad, sums]
            outs = [field, field] + outs
        if last and pair:
            outs = outs + [(2, tx, lanes)]
        result = list(call(functools.partial(gather_kernel, later, wide), ins, outs, us=1.5))
        if later:
            state, smoothed = result[:2]
            result = result[2:]
        grad, smooth_grad, seen, to_all = result[:4]
        if not last:
            steps = [seen] + swap_pairs(seen, "gy")
        sums = lax.all_to_all(to_all, axes, 0, 0, tiled=True)
    back_ground = background.reshape(variables, wide, tx)
    if pair:
        (sent,) = call(widen_kernel, [pert], [(members, variables, wide, tx)], us=1.0)
        pert_other = swap_mem(sent)
        back = swap_mem(result[4])
        control_out, analysis = call(
            final_pair_kernel,
            [sums, state, grad, back, smoothed, smooth_grad, pert, pert_other, back_ground],
            [(members, zy, tx), (variables, wide, tx)],
            us=1.5,
        )
    else:
        spread, analysis = call(
            final_any_kernel,
            [sums, state, grad, smoothed, smooth_grad, levels_out(pert.astype(F32)), back_ground],
            [(blocks * lanes, tx), (variables, wide, tx)],
            us=1.5,
        )
        cut = lax.all_to_all(spread.reshape(n_mem, members, wide, tx), "mem", 0, 0, tiled=True)
        control_out = jnp.moveaxis(cut, 0, 1)
    return analysis.reshape(background.shape), control_out.reshape(control.shape)


def solution(mesh):
    in_specs = (
        P("mem", None, None, "gy", "gx"),
        P("mem", None, "gy", "gx"),
        P(None, "mem", "gy", "gx"),
        P("gy", "gx"),
        P("gy", "gx"),
        P("gy", "gx"),
        P("gy", "gx"),
    )
    out_specs = (P(None, "mem", "gy", "gx"), P("mem", None, "gy", "gx"))

    return jax.shard_map(per_device, mesh=mesh, in_specs=in_specs, out_specs=out_specs, check_vma=False)
```

time: 84.3 us -> 68.4 us (0.81)
  blocking collectives: 11.2 us -> 0 us
  starting transfers between devices: 32.2 us -> 25.9 us
  waiting for transfers between devices: 21 us -> 23.7 us
  Pallas kernels: 18.1 us -> 16.8 us
    all_to_all x1 -> x2, waiting for transfers between devices: 0.01 us -> 12.3 us  [per_device(): sums = lax.all_to_all(to_all, axes, 0, 0, tiled=True)]
    all_to_all x1 -> x0, blocking collectives: 11.2 us -> none  [per_device(): sums = lax.all_to_all(to_all, axes, 0, 0, tiled=True)]
    ppermute x16 -> x18, waiting for transfers between devices: 21 us -> 11.4 us  [the longest x4 4.64 us: swap_mem(): return lax.ppermute(value, 'mem', [(0, 1), (1, 0)])]
    ppermute x16 -> x18, starting transfers between devices: 26.9 us -> 19.7 us  [the longest x7 9.12 us: swap_first(): lax.ppermute(value, axis, [(i, first_partner(i, n)) for i in range(n)])]
    pallas_call x11, Pallas kernels: 18.1 us -> 16.8 us  [call(): pl.pallas_call(kernel, out_shape=shapes, in_specs=[space] * len(ins), out...]
    all_to_all x1 -> x2, starting transfers between devices: 5.3 us -> 6.22 us  [per_device(): sums = lax.all_to_all(to_all, axes, 0, 0, tiled=True)]
    unnamed x14, local copies, waits for them, and re-layouts: 0.03 us -> 0.92 us
  transfers between devices with their start and end apart: 17 -> 20, of which waited for: 9 -> 9; matrix products, arithmetic and copies ran while one was open for 0% -> 0% of each run, Pallas kernels for 5% -> 15%
where the time goes in v3:
time: 68.4 us; the launch traced here: 68.2 us
  starting transfers between devices  25.9 us (38%)
  waiting for transfers between devices  23.7 us (35%)
  Pallas kernels  16.8 us (25%)
  local copies, waits for them, and re-layouts  0.92 us (1%)
  between operations  0.81 us (1%)
    pallas_call x11, Pallas kernels, call(): pl.pallas_call(kernel, out_shape=shapes, in_specs=[space] * len(ins), out...  16.8 us
    all_to_all x2, waiting for transfers between devices, per_device(): sums = lax.all_to_all(to_all, axes, 0, 0, tiled=True)  12.3 us
    ppermute x7, starting transfers between devices, swap_first(): lax.ppermute(value, axis, [(i, first_partner(i, n)) for i in range(n)])  9.12 us
    ppermute x4, starting transfers between devices, swap_mem(): return lax.ppermute(value, 'mem', [(0, 1), (1, 0)])  6.9 us
    all_to_all x2, starting transfers between devices, per_device(): sums = lax.all_to_all(to_all, axes, 0, 0, tiled=True)  6.22 us
    ppermute x4, waiting for transfers between devices, swap_mem(): return lax.ppermute(value, 'mem', [(0, 1), (1, 0)])  4.64 us
    ppermute x3, waiting for transfers between devices, swap_second(): lax.ppermute(value, axis, [(i, second_partner(i, n)) for i in range(n)])  4.12 us
    ppermute x3, starting transfers between devices, swap_second(): lax.ppermute(value, axis, [(i, second_partner(i, n)) for i in range(n)])  3.34 us
  transfers between devices with their start and end apart: 20, of which 9 were waited for; matrix products, arithmetic and copies ran while one was open for 0% of the time, Pallas kernels for 15%

profile of v3, /device:TPU:0, one launch (start us, length us, event | category | flops | bytes accessed | tf_op | source)
XLA Modules:
  0.0 68.2 jit_solution(12545358389762564115)
XLA Ops:
  1.7 3.1 %collective-permute-start = (f32[128,128]{1,0:T(8,128)S(1)}, f32[128,128]{1,0:T(8,128)S(1)}, u32[]{:S(2)}, u32[]{:S(2)}) collective-permute-start(f32[128,128]{1,0:T(8,128)S(1)} %get-tuple-element.41), channel_id=1, source_target_pairs={{0,16},{16,0},{1,17},{17,1},{2,18},{18,2},{3,19},{19,3},{4,20},{20... | collective-permute-start | bytes 196616 | tf_op jit(solution)/shard_map/ppermute | solution.py:511
  4.8 2.2 %collective-permute-done.refs_1_ = f32[128,128]{1,0:T(8,128)S(1)} collective-permute-done((f32[128,128]{1,0:T(8,128)S(1)}, f32[128,128]{1,0:T(8,128)S(1)}, u32[]{:S(2)}, u32[]{:S(2)}) %collective-permute-start) | collective-permute-done | bytes 65568 | tf_op jit(solution)/shard_map/ppermute | solution.py:511
  7.1 2.1 %collective-permute-start.1 = (f32[128,128]{1,0:T(8,128)S(1)}, f32[128,128]{1,0:T(8,128)S(1)}, u32[]{:S(2)}, u32[]{:S(2)}) collective-permute-start(f32[128,128]{1,0:T(8,128)S(1)} %get-tuple-element.42), channel_id=1, source_target_pairs={{0,4},{4,0},{8,12},{12,8},{1,5},{5,1},{9,13},{13,9},{2,6},{6,2},{1... | collective-permute-start | bytes 196616 | tf_op jit(solution)/shard_map/ppermute | solution.py:487
  9.3 3.6 %shard_map.88 = (f32[3,32,128]{2,1,0:T(8,128)S(1)}, f32[2,32,128]{2,1,0:T(8,128)S(1)}, f32[384,256]{1,0:T(8,128)S(1)}, f32[256,128]{1,0:T(8,128)S(1)}, f32[2,128,144]{2,1,0:T(8,128)S(1)}) custom-call(bf16[2,5,128,128]{3,2,1,0:T(8,128)(2,1)S(1)} %bitcast.16, s32[32,128]{1,0:T(8,128)S(1)} %copy-done.3, s32[32,128]{1,0:T(8,128)S(1)} %copy-done.4, ...), custom_call_target="tpu_custom_call" | custom-call | flops 4000000000 | bytes 1048576 | tf_op jit(solution)/shard_map/pallas_call | solution.py:466
  12.9 1.6 %collective-permute-start.3 = (f32[2,32,128]{2,1,0:T(8,128)S(1)}, f32[2,32,128]{2,1,0:T(8,128)S(1)}, u32[]{:S(2)}, u32[]{:S(2)}) collective-permute-start(f32[2,32,128]{2,1,0:T(8,128)S(1)} %get-tuple-element.46.refs_6_), channel_id=1, source_target_pairs={{0,16},{16,0},{1,17},{17,1},{2,18},{18,2},{3,19},{19,3},{4,20},{20... | collective-permute-start | bytes 98312 | tf_op jit(solution)/shard_map/ppermute | solution.py:511
  14.5 2.4 %collective-permute-done.3.refs_7_ = f32[2,32,128]{2,1,0:T(8,128)S(1)} collective-permute-done((f32[2,32,128]{2,1,0:T(8,128)S(1)}, f32[2,32,128]{2,1,0:T(8,128)S(1)}, u32[]{:S(2)}, u32[]{:S(2)}) %collective-permute-start.3) | collective-permute-done | bytes 32800 | tf_op jit(solution)/shard_map/ppermute | solution.py:511
  17.4 1.6 %collective-permute-start.7 = (f32[2,8,128]{2,1,0:T(8,128)S(1)}, f32[2,8,128]{2,1,0:T(8,128)S(1)}, u32[]{:S(2)}, u32[]{:S(2)}) collective-permute-start(f32[2,8,128]{2,1,0:T(8,128)S(1)} %get-tuple-element.50), channel_id=1, source_target_pairs={{0,3},{1,2},{2,1},{3,0},{4,7},{5,6},{6,5},{7,4},{8,11},{9,10},{10,... | collective-permute-start | bytes 24584 | tf_op jit(solution)/shard_map/ppermute | solution.py:493
  19.0 3.1 %collective-permute-start.4 = (f32[7,32,128]{2,1,0:T(8,128)S(1)}, f32[7,32,128]{2,1,0:T(8,128)S(1)}, u32[]{:S(2)}, u32[]{:S(2)}) collective-permute-start(f32[7,32,128]{2,1,0:T(8,128)S(1)} %get-tuple-element.47.pack.refs_0_.refs_5_), channel_id=1, source_target_pairs={{0,4},{4,0},{8,12},{12,8},{1,5},{5,1},{9,13},{13,9},{2,6},{6,2},{1... | collective-permute-start | bytes 344072 | tf_op jit(solution)/shard_map/ppermute | solution.py:487
  22.1 1.4 %shard_map.90 = (f32[2,128,128]{2,1,0:T(8,128)S(1)}, f32[32,128]{1,0:T(8,128)S(1)}) custom-call(f32[2,128,128]{2,1,0:T(8,128)S(1)} %get-tuple-element.48.y1, f32[2,8,128]{2,1,0:T(8,128)S(1)} %collective-permute-done.6.from_first, f32[2,8,128]{2,1,0:T(8,128)S(1)} %collective-permute-done.7.from_second, f32[2,128,144]{2,1,0:T(8,128)S(1)} %get-tuple-element.51.kx.refs_4_, ...), custom_call_target="tpu_custom_call" | custom-call | flops 1500000000 | bytes 1048576 | tf_op jit(solution)/shard_map/pallas_call | solution.py:466
  23.6 1.6 %collective-permute-start.8 = (f32[32,128]{1,0:T(8,128)S(1)}, f32[32,128]{1,0:T(8,128)S(1)}, u32[]{:S(2)}, u32[]{:S(2)}) collective-permute-start(f32[32,128]{1,0:T(8,128)S(1)} %get-tuple-element.52.refs_3_), channel_id=1, source_target_pairs={{0,4},{4,0},{8,12},{12,8},{1,5},{5,1},{9,13},{13,9},{2,6},{6,2},{1... | collective-permute-start | bytes 49160 | tf_op jit(solution)/shard_map/ppermute | solution.py:487
  25.3 2.0 %collective-permute-done.8.refs_4_ = f32[32,128]{1,0:T(8,128)S(1)} collective-permute-done((f32[32,128]{1,0:T(8,128)S(1)}, f32[32,128]{1,0:T(8,128)S(1)}, u32[]{:S(2)}, u32[]{:S(2)}) %collective-permute-start.8) | collective-permute-done | bytes 16416 | tf_op jit(solution)/shard_map/ppermute | solution.py:487
  27.4 2.8 %shard_map.91 = (f32[2,128,128]{2,1,0:T(8,128)S(1)}, f32[2,128,128]{2,1,0:T(8,128)S(1)}, f32[2,2,8,128]{3,2,1,0:T(8,128)S(1)}, f32[2,2,8,128]{3,2,1,0:T(8,128)S(1)}, f32[32,128]{1,0:T(8,128)S(1)}) custom-call(f32[7,32,128]{2,1,0:T(8,128)S(1)} %get-tuple-element.47.pack.refs_0_.refs_5_, f32[7,32,128]{2,1,0:T(8,128)S(1)} %collective-permute-done.4.refs_1_, ...), custom_call_target="tpu_custom_call" | custom-call | flops 3000000000 | bytes 1048576 | tf_op jit(solution)/shard_map/pallas_call | solution.py:466
  30.3 1.1 %collective-permute-start.11 = (f32[2,2,8,128]{3,2,1,0:T(8,128)S(1)}, f32[2,2,8,128]{3,2,1,0:T(8,128)S(1)}, u32[]{:S(2)}, u32[]{:S(2)}) collective-permute-start(f32[2,2,8,128]{3,2,1,0:T(8,128)S(1)} %get-tuple-element.57), channel_id=1, source_target_pairs={{0,3},{1,2},{2,1},{3,0},{4,7},{5,6},{6,5},{7,4},{8,11},{9,10},{10,... | collective-permute-start | bytes 49160 | tf_op jit(solution)/shard_map/ppermute | solution.py:493
  31.5 2.1 %collective-permute-done.11.refs_3_ = f32[2,2,8,128]{3,2,1,0:T(8,128)S(1)} collective-permute-done((f32[2,2,8,128]{3,2,1,0:T(8,128)S(1)}, f32[2,2,8,128]{3,2,1,0:T(8,128)S(1)}, u32[]{:S(2)}, u32[]{:S(2)}) %collective-permute-start.11) | collective-permute-done | bytes 16416 | tf_op jit(solution)/shard_map/ppermute | solution.py:493
  33.5 2.2 %shard_map.92 = (f32[2,128,128]{2,1,0:T(8,128)S(1)}, f32[2,128,128]{2,1,0:T(8,128)S(1)}, f32[32,128]{1,0:T(8,128)S(1)}, f32[32,128]{1,0:T(8,128)}) custom-call(f32[2,128,128]{2,1,0:T(8,128)S(1)} %get-tuple-element.54.refs_0_, f32[2,128,128]{2,1,0:T(8,128)S(1)} %get-tuple-element.55.refs_1_, f32[2,2,8,128]{3,2,1,0:T(8,128)S(1)} %collective-permute-done.10.refs_2_, ...), custom_call_target="tpu_custom_call" | custom-call | flops 1500000000 | bytes 1048576 | tf_op jit(solution)/shard_map/pallas_call | solution.py:466
  35.7 2.0 %collective-permute-start.12 = (f32[32,128]{1,0:T(8,128)S(1)}, f32[32,128]{1,0:T(8,128)S(1)}, u32[]{:S(2)}, u32[]{:S(2)}) collective-permute-start(f32[32,128]{1,0:T(8,128)S(1)} %get-tuple-element.61.refs_6_), channel_id=1, source_target_pairs={{0,4},{4,0},{8,12},{12,8},{1,5},{5,1},{9,13},{13,9},{2,6},{6,2},{1... | collective-permute-start | bytes 49160 | tf_op jit(solution)/shard_map/ppermute | solution.py:487
  37.9 3.7 %all-to-all-start = ((f32[32,1,128]{2,1,0:T(1,128)}), f32[32,1,128]{2,1,0:T(1,128)S(1)}, u32[]{:S(2)}, u32[]{:S(2)}) async-start(f32[32,1,128]{2,1,0:T(1,128)} %bitcast.3), calls=%async_computation | async-start | bytes 32768 | tf_op jit(solution)/shard_map/all_to_all | solution.py:611
  41.6 1.7 %collective-permute-start.17 = (f32[2,5,64,128]{3,2,1,0:T(8,128)S(1)}, f32[2,5,64,128]{3,2,1,0:T(8,128)S(1)}, u32[]{:S(2)}, u32[]{:S(2)}) collective-permute-start(f32[2,5,64,128]{3,2,1,0:T(8,128)S(1)} %shard_map.95), channel_id=1, source_target_pairs={{0,16},{16,0},{1,17},{17,1},{2,18},{18,2},{3,19},{19,3},{4,20},{20... | collective-permute-start | bytes 983048 | tf_op jit(solution)/shard_map/ppermute | solution.py:511
  43.3 5.2 %all-to-all-done = f32[32,1,128]{2,1,0:T(1,128)S(1)} async-done(((f32[32,1,128]{2,1,0:T(1,128)}), f32[32,1,128]{2,1,0:T(1,128)S(1)}, u32[]{:S(2)}, u32[]{:S(2)}) %all-to-all-start) | async-done | bytes 16416 | tf_op jit(solution)/shard_map/all_to_all | solution.py:611
  48.5 3.0 %shard_map.93 = (f32[2,128,128]{2,1,0:T(8,128)S(1)}, f32[2,128,128]{2,1,0:T(8,128)S(1)}, f32[2,2,8,128]{3,2,1,0:T(8,128)S(1)}, f32[2,2,8,128]{3,2,1,0:T(8,128)S(1)}, f32[32,128]{1,0:T(8,128)S(1)}) custom-call(f32[7,32,128]{2,1,0:T(8,128)S(1)} %get-tuple-element.47.pack.refs_0_.refs_5_, f32[7,32,128]{2,1,0:T(8,128)S(1)} %collective-permute-done.4.refs_1_, ...), custom_call_target="tpu_custom_call" | custom-call | flops 3000000000 | bytes 1048576 | tf_op jit(solution)/shard_map/pallas_call | solution.py:466
  52.8 2.1 %collective-permute-done.15.refs_3_ = f32[2,2,8,128]{3,2,1,0:T(8,128)S(1)} collective-permute-done((f32[2,2,8,128]{3,2,1,0:T(8,128)S(1)}, f32[2,2,8,128]{3,2,1,0:T(8,128)S(1)}, u32[]{:S(2)}, u32[]{:S(2)}) %collective-permute-start.15) | collective-permute-done | bytes 16416 | tf_op jit(solution)/shard_map/ppermute | solution.py:493
  54.8 2.2 %shard_map.94 = (f32[2,128,128]{2,1,0:T(8,128)S(1)}, f32[2,128,128]{2,1,0:T(8,128)S(1)}, f32[2,128,128]{2,1,0:T(8,128)S(1)}, f32[2,128,128]{2,1,0:T(8,128)S(1)},...) custom-call(f32[2,128,128]{2,1,0:T(8,128)S(1)} %get-tuple-element.63.refs_0_, ...), custom_call_target="tpu_custom_call" | custom-call | flops 1500000000 | bytes 1048576 | tf_op jit(solution)/shard_map/pallas_call | solution.py:466
  57.6 2.5 %all-to-all-start.1 = ((f32[32,1,128]{2,1,0:T(1,128)}), f32[32,1,128]{2,1,0:T(1,128)S(1)}, u32[]{:S(2)}, u32[]{:S(2)}) async-start(f32[32,1,128]{2,1,0:T(1,128)} %bitcast.6), calls=%async_computation.1 | async-start | bytes 32768 | tf_op jit(solution)/shard_map/all_to_all | solution.py:611
  60.1 7.1 %all-to-all-done.1 = f32[32,1,128]{2,1,0:T(1,128)S(1)} async-done(((f32[32,1,128]{2,1,0:T(1,128)}), f32[32,1,128]{2,1,0:T(1,128)S(1)}, u32[]{:S(2)}, u32[]{:S(2)}) %all-to-all-start.1) | async-done | bytes 16416 | tf_op jit(solution)/shard_map/all_to_all | solution.py:611
  (41 shorter events, 4.9 us)
Async XLA Ops:
  1.7 5.3 %collective-permute-start = (f32[128,128]{1,0:T(8,128)S(1)}, f32[128,128]{1,0:T(8,128)S(1)}, u32[]{:S(2)}, u32[]{:S(2)}) collective-permute-start(f32[128,128]{1,0:T(8,128)S(1)} %get-tuple-element.41), channel_id=1, source_target_pairs={{0,16},{16,0},{1,17},{17,1},{2,18},{18,2},{3,19},{19,3},{4,20},{20... | collective-permute-start | bytes 196616 | tf_op jit(solution)/shard_map/ppermute | solution.py:511
  7.0 2.2 %copy-start.4 = (s32[32,128]{1,0:T(8,128)S(1)}, s32[32,128]{1,0:T(8,128)}, u32[]{:S(2)}) copy-start(s32[32,128]{1,0:T(8,128)} %flag_in.1) | copy-start | bytes 49156
  7.0 2.2 %copy-start.5 = (f32[32,128]{1,0:T(8,128)S(1)}, f32[32,128]{1,0:T(8,128)}, u32[]{:S(2)}) copy-start(f32[32,128]{1,0:T(8,128)} %innov_in.1) | copy-start | bytes 49156
  7.0 2.2 %copy-start.6 = (f32[32,128]{1,0:T(8,128)S(1)}, f32[32,128]{1,0:T(8,128)}, u32[]{:S(2)}) copy-start(f32[32,128]{1,0:T(8,128)} %prec_in.1) | copy-start | bytes 49156
  7.1 9.8 %collective-permute-start.1 = (f32[128,128]{1,0:T(8,128)S(1)}, f32[128,128]{1,0:T(8,128)S(1)}, u32[]{:S(2)}, u32[]{:S(2)}) collective-permute-start(f32[128,128]{1,0:T(8,128)S(1)} %get-tuple-element.42), channel_id=1, source_target_pairs={{0,4},{4,0},{8,12},{12,8},{1,5},{5,1},{9,13},{13,9},{2,6},{6,2},{1... | collective-permute-start | bytes 196616 | tf_op jit(solution)/shard_map/ppermute | solution.py:487
  9.2 7.7 %collective-permute-start.2 = (f32[128,128]{1,0:T(8,128)S(1)}, f32[128,128]{1,0:T(8,128)S(1)}, u32[]{:S(2)}, u32[]{:S(2)}) collective-permute-start(f32[128,128]{1,0:T(8,128)S(1)} %get-tuple-element.43), channel_id=1, source_target_pairs={{0,1},{1,0},{2,3},{3,2},{4,8},{5,9},{6,10},{7,11},{8,4},{9,5},{10,... | collective-permute-start | bytes 196616 | tf_op jit(solution)/shard_map/ppermute | solution.py:499
  12.9 4.0 %collective-permute-start.3 = (f32[2,32,128]{2,1,0:T(8,128)S(1)}, f32[2,32,128]{2,1,0:T(8,128)S(1)}, u32[]{:S(2)}, u32[]{:S(2)}) collective-permute-start(f32[2,32,128]{2,1,0:T(8,128)S(1)} %get-tuple-element.46.refs_6_), channel_id=1, source_target_pairs={{0,16},{16,0},{1,17},{17,1},{2,18},{18,2},{3,19},{19,3},{4,20},{20... | collective-permute-start | bytes 98312 | tf_op jit(solution)/shard_map/ppermute | solution.py:511
  17.3 4.8 %collective-permute-start.6 = (f32[2,8,128]{2,1,0:T(8,128)S(1)}, f32[2,8,128]{2,1,0:T(8,128)S(1)}, u32[]{:S(2)}, u32[]{:S(2)}) collective-permute-start(f32[2,8,128]{2,1,0:T(8,128)S(1)} %get-tuple-element.49), channel_id=1, source_target_pairs={{0,1},{1,0},{2,3},{3,2},{4,5},{5,4},{6,7},{7,6},{8,9},{9,8},{10,11... | collective-permute-start | bytes 24584 | tf_op jit(solution)/shard_map/ppermute | solution.py:487
  17.4 4.7 %collective-permute-start.7 = (f32[2,8,128]{2,1,0:T(8,128)S(1)}, f32[2,8,128]{2,1,0:T(8,128)S(1)}, u32[]{:S(2)}, u32[]{:S(2)}) collective-permute-start(f32[2,8,128]{2,1,0:T(8,128)S(1)} %get-tuple-element.50), channel_id=1, source_target_pairs={{0,3},{1,2},{2,1},{3,0},{4,7},{5,6},{6,5},{7,4},{8,11},{9,10},{10,... | collective-permute-start | bytes 24584 | tf_op jit(solution)/shard_map/ppermute | solution.py:493
  19.0 8.4 %collective-permute-start.4 = (f32[7,32,128]{2,1,0:T(8,128)S(1)}, f32[7,32,128]{2,1,0:T(8,128)S(1)}, u32[]{:S(2)}, u32[]{:S(2)}) collective-permute-start(f32[7,32,128]{2,1,0:T(8,128)S(1)} %get-tuple-element.47.pack.refs_0_.refs_5_), channel_id=1, source_target_pairs={{0,4},{4,0},{8,12},{12,8},{1,5},{5,1},{9,13},{13,9},{2,6},{6,2},{1... | collective-permute-start | bytes 344072 | tf_op jit(solution)/shard_map/ppermute | solution.py:487
  22.1 5.3 %collective-permute-start.5 = (f32[7,32,128]{2,1,0:T(8,128)S(1)}, f32[7,32,128]{2,1,0:T(8,128)S(1)}, u32[]{:S(2)}, u32[]{:S(2)}) collective-permute-start(f32[7,32,128]{2,1,0:T(8,128)S(1)} %get-tuple-element.47.pack.refs_0_.refs_5_), channel_id=1, source_target_pairs={{0,1},{1,0},{2,3},{3,2},{4,8},{5,9},{6,10},{7,11},{8,4},{9,5},{10,... | collective-permute-start | bytes 344072 | tf_op jit(solution)/shard_map/ppermute | solution.py:499
  23.6 3.8 %collective-permute-start.8 = (f32[32,128]{1,0:T(8,128)S(1)}, f32[32,128]{1,0:T(8,128)S(1)}, u32[]{:S(2)}, u32[]{:S(2)}) collective-permute-start(f32[32,128]{1,0:T(8,128)S(1)} %get-tuple-element.52.refs_3_), channel_id=1, source_target_pairs={{0,4},{4,0},{8,12},{12,8},{1,5},{5,1},{9,13},{13,9},{2,6},{6,2},{1... | collective-permute-start | bytes 49160 | tf_op jit(solution)/shard_map/ppermute | solution.py:487
  25.2 2.2 %collective-permute-start.9 = (f32[32,128]{1,0:T(8,128)S(1)}, f32[32,128]{1,0:T(8,128)S(1)}, u32[]{:S(2)}, u32[]{:S(2)}) collective-permute-start(f32[32,128]{1,0:T(8,128)S(1)} %get-tuple-element.52.refs_3_), channel_id=1, source_target_pairs={{0,1},{1,0},{2,3},{3,2},{4,8},{5,9},{6,10},{7,11},{8,4},{9,5},{10,... | collective-permute-start | bytes 49160 | tf_op jit(solution)/shard_map/ppermute | solution.py:499
  30.2 1.2 %collective-permute-start.10 = (f32[2,2,8,128]{3,2,1,0:T(8,128)S(1)}, f32[2,2,8,128]{3,2,1,0:T(8,128)S(1)}, u32[]{:S(2)}, u32[]{:S(2)}) collective-permute-start(f32[2,2,8,128]{3,2,1,0:T(8,128)S(1)} %get-tuple-element.56), channel_id=1, source_target_pairs={{0,1},{1,0},{2,3},{3,2},{4,5},{5,4},{6,7},{7,6},{8,9},{9,8},{10,11... | collective-permute-start | bytes 49160 | tf_op jit(solution)/shard_map/ppermute | solution.py:487
  30.3 3.2 %collective-permute-start.11 = (f32[2,2,8,128]{3,2,1,0:T(8,128)S(1)}, f32[2,2,8,128]{3,2,1,0:T(8,128)S(1)}, u32[]{:S(2)}, u32[]{:S(2)}) collective-permute-start(f32[2,2,8,128]{3,2,1,0:T(8,128)S(1)} %get-tuple-element.57), channel_id=1, source_target_pairs={{0,3},{1,2},{2,1},{3,0},{4,7},{5,6},{6,5},{7,4},{8,11},{9,10},{10,... | collective-permute-start | bytes 49160 | tf_op jit(solution)/shard_map/ppermute | solution.py:493
  35.7 7.6 %collective-permute-start.12 = (f32[32,128]{1,0:T(8,128)S(1)}, f32[32,128]{1,0:T(8,128)S(1)}, u32[]{:S(2)}, u32[]{:S(2)}) collective-permute-start(f32[32,128]{1,0:T(8,128)S(1)} %get-tuple-element.61.refs_6_), channel_id=1, source_target_pairs={{0,4},{4,0},{8,12},{12,8},{1,5},{5,1},{9,13},{13,9},{2,6},{6,2},{1... | collective-permute-start | bytes 49160 | tf_op jit(solution)/shard_map/ppermute | solution.py:487
  37.8 5.5 %collective-permute-start.13 = (f32[32,128]{1,0:T(8,128)S(1)}, f32[32,128]{1,0:T(8,128)S(1)}, u32[]{:S(2)}, u32[]{:S(2)}) collective-permute-start(f32[32,128]{1,0:T(8,128)S(1)} %get-tuple-element.61.refs_6_), channel_id=1, source_target_pairs={{0,1},{1,0},{2,3},{3,2},{4,8},{5,9},{6,10},{7,11},{8,4},{9,5},{10,... | collective-permute-start | bytes 49160 | tf_op jit(solution)/shard_map/ppermute | solution.py:499
  37.9 10.6 %all-to-all-start = ((f32[32,1,128]{2,1,0:T(1,128)}), f32[32,1,128]{2,1,0:T(1,128)S(1)}, u32[]{:S(2)}, u32[]{:S(2)}) async-start(f32[32,1,128]{2,1,0:T(1,128)} %bitcast.3), calls=%async_computation | async-start | bytes 32768 | tf_op jit(solution)/shard_map/all_to_all | solution.py:611
  41.6 18.5 %collective-permute-start.17 = (f32[2,5,64,128]{3,2,1,0:T(8,128)S(1)}, f32[2,5,64,128]{3,2,1,0:T(8,128)S(1)}, u32[]{:S(2)}, u32[]{:S(2)}) collective-permute-start(f32[2,5,64,128]{3,2,1,0:T(8,128)S(1)} %shard_map.95), channel_id=1, source_target_pairs={{0,16},{16,0},{1,17},{17,1},{2,18},{18,2},{3,19},{19,3},{4,20},{20... | collective-permute-start | bytes 983048 | tf_op jit(solution)/shard_map/ppermute | solution.py:511
  51.5 1.2 %collective-permute-start.14 = (f32[2,2,8,128]{3,2,1,0:T(8,128)S(1)}, f32[2,2,8,128]{3,2,1,0:T(8,128)S(1)}, u32[]{:S(2)}, u32[]{:S(2)}) collective-permute-start(f32[2,2,8,128]{3,2,1,0:T(8,128)S(1)} %get-tuple-element.65), channel_id=1, source_target_pairs={{0,1},{1,0},{2,3},{3,2},{4,5},{5,4},{6,7},{7,6},{8,9},{9,8},{10,11... | collective-permute-start | bytes 49160 | tf_op jit(solution)/shard_map/ppermute | solution.py:487
  51.6 3.2 %collective-permute-start.15 = (f32[2,2,8,128]{3,2,1,0:T(8,128)S(1)}, f32[2,2,8,128]{3,2,1,0:T(8,128)S(1)}, u32[]{:S(2)}, u32[]{:S(2)}) collective-permute-start(f32[2,2,8,128]{3,2,1,0:T(8,128)S(1)} %get-tuple-element.66), channel_id=1, source_target_pairs={{0,3},{1,2},{2,1},{3,0},{4,7},{5,6},{6,5},{7,4},{8,11},{9,10},{10,... | collective-permute-start | bytes 49160 | tf_op jit(solution)/shard_map/ppermute | solution.py:493
  54.8 12.4 %copy-start.1 = (f32[5,8,8,128]{3,2,1,0:T(8,128)S(1)}, f32[5,8,8,128]{3,2,1,0:T(8,128)}, u32[]{:S(2)}) copy-start(f32[5,8,8,128]{3,2,1,0:T(8,128)} %param.9) | copy-start | bytes 491524
  57.0 10.2 %collective-permute-start.16 = (f32[2,128,128]{2,1,0:T(8,128)S(1)}, f32[2,128,128]{2,1,0:T(8,128)S(1)}, u32[]{:S(2)}, u32[]{:S(2)}) collective-permute-start(f32[2,128,128]{2,1,0:T(8,128)S(1)} %get-tuple-element.73), channel_id=1, source_target_pairs={{0,16},{16,0},{1,17},{17,1},{2,18},{18,2},{3,19},{19,3},{4,20},{20... | collective-permute-start | bytes 393224 | tf_op jit(solution)/shard_map/ppermute | solution.py:511
  57.6 9.7 %all-to-all-start.1 = ((f32[32,1,128]{2,1,0:T(1,128)}), f32[32,1,128]{2,1,0:T(1,128)S(1)}, u32[]{:S(2)}, u32[]{:S(2)}) async-start(f32[32,1,128]{2,1,0:T(1,128)} %bitcast.6), calls=%async_computation.1 | async-start | bytes 32768 | tf_op jit(solution)/shard_map/all_to_all | solution.py:611
  (3 other events, 5.3 us)

commit v4 on v3

--- a/solution.py
+++ b/solution.py
@@ -42,6 +42,13 @@
 
 def exact_dot(a, b):
     return jnp.dot(a, b, precision=EXACT, preferred_element_type=F32)
+
+
+def split_dot(a, b):
+    rows = a[0].shape[0]
+    first = jnp.dot(jnp.concatenate(a, axis=0), b[0], preferred_element_type=F32)
+    second = jnp.dot(a[0], b[1], preferred_element_type=F32)
+    return first[:rows] + (first[rows:] + second)
 
 
 def halves(f32):
@@ -84,9 +91,8 @@
     return tables
 
 
-def from_table(tables, wide, lanes):
+def from_table(tables, wide, lanes, parts):
     per = lanes // wide
-    parts = tables[0].shape[1] // wide
     groups = []
     for first in range(0, len(tables), per):
         rows = []
@@ -101,11 +107,6 @@
     return groups
 
 
-def split_x(field):
-    half = field.shape[0] // 2
-    return jnp.concatenate([field[:half], field[half:]], axis=1)
-
-
 def onehot_rows(index, rows):
     wide = jnp.broadcast_to(index, (rows, index.shape[1]))
     return jnp.where(iota(wide.shape, 0) == wide, 1.0, 0.0).astype(BF16)
@@ -133,51 +134,68 @@
     return over(at, ty), where * ty + rem(at, ty), (where >= 0) & (where < ngy)
 
 
-def matrices(ty, ky, ky_first, kx):
-    wide, zy = ky.shape[0], ky.shape[1] // 2
-    tx = kx.shape[1]
-
-    def along_y(shape):
-        zs, ys, oks = y_geometry(iota(shape, 0), zy, ty)
-        zt, yt, okt = y_geometry(iota(shape, 1), zy, ty)
-        return jnp.where((zs == zt) & oks & okt, tap(ys - yt), 0.0)
-
-    once = along_y((wide, zy))
-    ky[:, :zy] = once
-    ky[:, zy:] = exact_dot(along_y((wide, wide)), once)
-
-    shape = ky_first.shape
+def band_y(shape, zy, ty):
+    zs, ys, oks = y_geometry(iota(shape, 0), zy, ty)
+    zt, yt, okt = y_geometry(iota(shape, 1), zy, ty)
+    return jnp.where((zs == zt) & oks & okt, tap(ys - yt), 0.0)
+
+
+def band_x(shape, tx):
+    gx, ngx = lax.axis_index("gx"), lax.axis_size("gx")
+    side = pair_side(gx)
+
+    def place(k):
+        tile, r = jnp.where(k < tx, 0, jnp.where(k < tx + HALO, 1, 2)), rem(k - tx, HALO)
+        right = (tile == 1) == (side == 1)
+        at = jnp.where(tile == 0, k, jnp.where(right, tx + r, r - HALO))
+        full = gx * tx + at
+        return at, (full >= 0) & (full < ngx * tx)
+
+    xt, okt = place(iota(shape, 0))
+    xs, oks = place(iota(shape, 1))
+    return jnp.where(oks & okt, tap(xs - xt), 0.0)
+
+
+def once_matrices(ty, ky_first, kx):
+    zy, tx = ky_first.shape[2], kx.shape[1]
+    shape = ky_first.shape[1:]
     k = iota(shape, 0)
     gy, ngy = lax.axis_index("gy"), lax.axis_size("gy")
-    tile = jnp.where(k < zy, 0, jnp.where(k < zy + zy * RADIUS // ty, 1, 2))
-    at = k - jnp.where(tile == 0, 0, jnp.where(tile == 1, zy, zy + zy * RADIUS // ty))
+    rows = zy * RADIUS // ty
+    tile = jnp.where(k < zy, 0, jnp.where(k < zy + rows, 1, 2))
+    at = k - jnp.where(tile == 0, 0, jnp.where(tile == 1, zy, zy + rows))
     side = jnp.where(tile == 1, pair_side(gy), -pair_side(gy))
     strip_row = (gy + side) * ty + rem(at, RADIUS) + jnp.where(side == 1, 0, ty - RADIUS)
     row = jnp.where(tile == 0, gy * ty + rem(at, ty), strip_row)
     level = jnp.where(tile == 0, over(at, ty), over(at, RADIUS))
     zt, yt, _ = y_geometry(iota(shape, 1), zy, ty)
-    ky_first[...] = jnp.where((level == zt) & (row >= 0) & (row < ngy * ty), tap(row - yt), 0.0)
-    gx, ngx = lax.axis_index("gx"), lax.axis_size("gx")
-    side = pair_side(gx)
-
-    def x_of(k):
-        tile, r = jnp.where(k < tx, 0, jnp.where(k < tx + HALO, 1, 2)), rem(k - tx, HALO)
-        right = (tile == 1) == (side == 1)
-        at = jnp.where(tile == 0, k, jnp.where(right, tx + r, r - HALO))
-        full = gx * tx + at
-        return at, (full >= 0) & (full < ngx * tx)
-
-    def along_x(shape):
-        xt, okt = x_of(iota(shape, 0))
-        xs, oks = x_of(iota(shape, 1))
-        return jnp.where(oks & okt, tap(xs - xt), 0.0)
-
-    long = tx + 2 * HALO
-    kx[0] = along_x((tx, long))
-    kx[1] = exact_dot(along_x((tx, long)), along_x((long, long)))
-
-
-def halves_kernel(control, mine, theirs, sems):
+    ky_first[0], ky_first[1] = halves(jnp.where((level == zt) & (row >= 0) & (row < ngy * ty), tap(row - yt), 0.0))
+    kx[0], kx[1] = halves(band_x(kx.shape[1:], tx))
+
+
+def twice_matrices(ty, ky, kx):
+    wide, zy = ky.shape[1], ky.shape[2] // 2
+    tx = kx.shape[1]
+    once = band_y((wide, zy), zy, ty)
+    ky[0, :, :zy], ky[1, :, :zy] = halves(once)
+    ky[0, :, zy:], ky[1, :, zy:] = halves(exact_dot(band_y((wide, wide), zy, ty), once))
+    long = kx.shape[2]
+    kx[0], kx[1] = halves(exact_dot(band_x((tx, long), tx), band_x((long, long), tx)))
+
+
+def y_strips(ty, value):
+    lanes, tx = value.shape
+    next_first = pair_side(lax.axis_index("gy")) == 1
+    rows = lanes * RADIUS // ty
+    value = value.reshape(lanes // (2 * ty), 2, ty, tx)
+    even, odd = value[:, 0], value[:, 1]
+    low = iota(even.shape, 1) < RADIUS
+    last = jnp.where(low, pltpu.roll(even, RADIUS, 1), odd).reshape(rows, tx)
+    initial = jnp.where(low, even, pltpu.roll(odd, RADIUS, 1)).reshape(rows, tx)
+    return jnp.where(next_first, last, initial), jnp.where(next_first, initial, last)
+
+
+def cut_kernel(control, theirs, mine, sems):
     members, zy, _ = control.shape
     wide = zy // 2
     mem = lax.axis_index("mem")
@@ -194,47 +212,25 @@
 
 def strips_kernel(ty, *refs):
     *blocks, first, second = refs
-    lanes, tx = blocks[0].shape
-    next_first = pair_side(lax.axis_index("gy")) == 1
-    rows = lanes * RADIUS // ty
+    rows = first.shape[0] // len(blocks)
     for b, block in enumerate(blocks):
-        value = block[...].reshape(lanes // (2 * ty), 2, ty, tx)
-        even, odd = value[:, 0], value[:, 1]
-        low = iota(even.shape, 1) < RADIUS
-        last = jnp.where(low, pltpu.roll(even, RADIUS, 1), odd).reshape(rows, tx)
-        initial = jnp.where(low, even, pltpu.roll(odd, RADIUS, 1)).reshape(rows, tx)
-        first[b * rows : (b + 1) * rows] = jnp.where(next_first, last, initial)
-        second[b * rows : (b + 1) * rows] = jnp.where(next_first, initial, last)
-
-
-def prep_kernel(ty, wide, pert_in, cell_in, flag_in, innov_in, prec_in, info, pobs, ky, ky_first, kx, table, pert, cell, flag, innov, prec, sems):
+        at = slice(b * rows, (b + 1) * rows)
+        first[at], second[at] = y_strips(ty, block[...])
+
+
+def pobs_kernel(wide, short, pert, cell, flag, innov, prec, info, pobs):
     members, variables, zy, tx = pert.shape
-    pairs = [(pert_in, pert), (cell_in, cell), (flag_in, flag), (innov_in, innov), (prec_in, prec)]
-    copies = [pltpu.make_async_copy(a, b, sems.at[i]) for i, (a, b) in enumerate(pairs)]
-    for copy in copies:
-        copy.start()
-    matrices(ty, ky, ky_first, kx)
-    for copy in copies:
-        copy.wait()
-    half = tx // 2
-    for m in range(members):
-        for v in range(variables):
-            block = split_x(pert[m, v].astype(F32).T)
-            at = (m * variables + v) * half
-            table[at : at + half, :] = block.astype(BF16)
+    table = jnp.concatenate([pert[m].reshape(variables * zy, tx).astype(F32).T for m in range(members)], axis=0).astype(BF16)
     for j in range(0, cell.shape[0], CHUNK):
         k = chunk_of(cell, j)
-        x, level_row = rem(k, tx), rem(over(k, tx), zy)
-        hot = onehot_rows(over(x, half) * zy + level_row, 2 * zy)
-        found = jnp.dot(table[...], hot, preferred_element_type=F32)
-        want = over(k, tx * zy) * half + rem(x, half)
-        rows = variables * half
-        mask = iota((rows, k.shape[1]), 0) == jnp.broadcast_to(want, (rows, k.shape[1]))
+        hot = onehot_rows(over(k, tx), variables * zy)
+        found = jnp.dot(table, hot, preferred_element_type=F32)
+        x = jnp.broadcast_to(rem(k, tx), (tx, k.shape[1]))
+        mask = iota(x.shape, 0) == x
         for m in range(members):
-            got = jnp.where(mask, found[m * rows : (m + 1) * rows], 0.0)
+            got = jnp.where(mask, found[m * tx : (m + 1) * tx], 0.0)
             store_chunk(pobs.at[m], j, jnp.sum(got, axis=0, keepdims=True))
     k = cell[...]
-    _, short = chunks(tx, wide, kx.shape[1])
     x = rem(k, tx)
     level_row = rem(over(k, tx), zy) - lax.axis_index("mem") * wide
     code = (over(x, short) * wide + level_row) * short + rem(x, short)
@@ -243,32 +239,8 @@
     info[2] = innov[...]
 
 
-def decode(code, short):
-    code = code.astype(jnp.int32)
-    shift = short.bit_length() - 1
-    return lax.shift_right_arithmetic(code, shift), code & (short - 1)
-
-
-def send_strips(first, second, at, field):
-    right, left = field[field.shape[0] - HALO :], field[:HALO]
-    even = pair_side(lax.axis_index("gx")) == 1
-    first[at] = jnp.where(even, right, left)
-    second[at] = jnp.where(even, left, right)
-
-
-def start_kernel(blocks, parts, *refs):
-    tiles, refs = refs[:blocks], refs[blocks:]
-    before, after, ky_first, info, refs = refs[0], refs[1], refs[2], refs[3], refs[4:]
-    pobs, (y1, state, first, second, pack) = refs[:parts], refs[parts:]
-    rows = before.shape[0] // blocks
-    for b in range(blocks):
-        own = tiles[b][...]
-        at = slice(b * rows, (b + 1) * rows)
-        wide = jnp.concatenate([own, before[at], after[at]], axis=0).T
-        out = exact_dot(wide, ky_first[...])
-        state[b] = wide[:, : own.shape[0]]
-        y1[b] = out
-        send_strips(first, second, b, out)
+def pack_kernel(info, *refs):
+    *pobs, pack = refs
     pack[0:3] = info[...]
     at = 3
     for part in pobs:
@@ -276,9 +248,33 @@
         at += part.shape[0]
 
 
+def decode(code, short):
+    code = code.astype(jnp.int32)
+    shift = short.bit_length() - 1
+    return lax.shift_right_arithmetic(code, shift), code & (short - 1)
+
+
+def send_strips(first, second, at, left, right):
+    even = pair_side(lax.axis_index("gx")) == 1
+    first[at] = jnp.where(even, right, left)
+    second[at] = jnp.where(even, left, right)
+
+
+def start_kernel(blocks, *refs):
+    tiles, (before, after, ky_first, y1, state, first, second) = refs[:blocks], refs[blocks:]
+    rows = before.shape[0] // blocks
+    for b in range(blocks):
+        at = slice(b * rows, (b + 1) * rows)
+        wide = jnp.concatenate([tiles[b][...], before[at], after[at]], axis=0).T
+        out = split_dot(halves(wide), (ky_first[0], ky_first[1]))
+        state[b] = wide[:, : tiles[b].shape[0]]
+        y1[b] = out
+        send_strips(first, second, b, out[:HALO], out[out.shape[0] - HALO :])
+
+
 def x_smooth(matrix, fields, firsts, seconds):
     wide = [jnp.concatenate([f, l, r], axis=0) for f, l, r in zip(fields, firsts, seconds)]
-    out = exact_dot(matrix, jnp.concatenate(wide, axis=1))
+    out = split_dot((matrix[0], matrix[1]), halves(jnp.concatenate(wide, axis=1)))
     zy = fields[0].shape[1]
     return [out[:, i * zy : (i + 1) * zy] for i in range(len(fields))]
 
@@ -298,14 +294,14 @@
         total = None
         for m in range(members):
             both = found[m * short : (m + 1) * short] + found[rows + m * short : rows + (m + 1) * short]
-            term = jnp.where(mask, both, 0.0) * jnp.broadcast_to(chunk_of(pack.at[3 + m], j), both.shape)
+            term = both * jnp.broadcast_to(chunk_of(pack.at[3 + m], j), both.shape)
             total = term if total is None else total + term
-        store_chunk(seen, j, jnp.sum(total, axis=0, keepdims=True))
+        store_chunk(seen, j, jnp.sum(jnp.where(mask, total, 0.0), axis=0, keepdims=True))
 
 
 def first_seen_kernel(wide, y1, from_first, from_second, kx, pack, smoothed, seen):
     each = range(y1.shape[0])
-    outs = x_smooth(kx[0], [y1[b] for b in each], [from_first[b] for b in each], [from_second[b] for b in each])
+    outs = x_smooth(kx, [y1[b] for b in each], [from_first[b] for b in each], [from_second[b] for b in each])
     for b in each:
         smoothed[b] = outs[b]
     gather_at(outs, wide, pack, seen)
@@ -319,17 +315,41 @@
     return g / (g + c)
 
 
-def scatter_kernel(has_step, wide, *refs):
+def scatter_tables(codes, vals, t, members, short, rows, decode_at):
+    acc = None
+    for j in range(0, codes.shape[0], CHUNK):
+        row, low = decode_at(chunk_of(codes, j))
+        hot = onehot_rows(row, rows)
+        low = jnp.broadcast_to(low, (short, low.shape[1]))
+        mask = iota(low.shape, 0) == low
+        parts = []
+        for i in range(2 * members):
+            value = jnp.broadcast_to(chunk_of(vals.at[t, i], j), low.shape)
+            parts.append(jnp.where(mask, value, 0.0).astype(BF16))
+        part = lax.dot_general(jnp.concatenate(parts, axis=0), hot, (((1,), (1,)), ((), ())), preferred_element_type=F32)
+        acc = part if acc is None else acc + part
+    return [acc[2 * m * short : (2 * m + 1) * short] + acc[(2 * m + 1) * short : (2 * m + 2) * short] for m in range(members)]
+
+
+def edge_kernel(has_step, wide, tx, *refs):
     packs, incs = refs[0:3], refs[3:6]
     refs = refs[6:]
     if has_step:
         steps, sums = refs[0:3], refs[3]
         refs = refs[4:]
         step = step_rows(sums[...])
-    ky, y1, y2, first, second, weights, vals = refs
-    blocks, tx, lanes = y1.shape
+    ky, first, second, weights, vals = refs
     members = packs[0].shape[0] - 3
+    lanes = ky.shape[2] // 2
     parts, short = chunks(tx, wide, lanes)
+
+    def at_edge(code):
+        row, low = decode(code, short)
+        part, level_row = over(row, wide), rem(row, wide)
+        left = (row >= 0) & (part == 0) & (low < HALO)
+        right = (row >= 0) & (part == parts - 1) & (low >= short - HALO)
+        return jnp.where(left, level_row, jnp.where(right, wide + level_row, -1)), rem(low, HALO)
+
     tiles = []
     for t in range(3):
         pack = packs[t]
@@ -346,44 +366,43 @@
         for m in range(members):
             val = pack[3 + m] * q
             high = val.astype(BF16).astype(F32)
-            vals[2 * m] = high
-            vals[2 * m + 1] = val - high
-        acc = None
-        for j in range(0, pack.shape[1], CHUNK):
-            row, low = decode(chunk_of(pack.at[0], j), short)
-            hot = onehot_rows(row, parts * wide)
-            low = jnp.broadcast_to(low, (short, low.shape[1]))
-            mask = iota(low.shape, 0) == low
-            rows = []
-            for i in range(2 * members):
-                value = jnp.broadcast_to(chunk_of(vals.at[i], j), low.shape)
-                rows.append(jnp.where(mask, value, 0.0).astype(BF16))
-            part = lax.dot_general(jnp.concatenate(rows, axis=0), hot, (((1,), (1,)), ((), ())), preferred_element_type=F32)
-            acc = part if acc is None else acc + part
-        tables = []
-        for m in range(members):
-            at = 2 * m * short
-            tables.append(acc[at : at + short] + acc[at + short : at + 2 * short])
-        tiles.append(jnp.concatenate(from_table(tables, wide, lanes), axis=0))
-    out = exact_dot(jnp.concatenate(tiles, axis=1), ky[...])
+            vals[t, 2 * m] = high
+            vals[t, 2 * m + 1] = val - high
+        tables = scatter_tables(pack.at[0], vals, t, members, HALO, lanes, at_edge)
+        tiles.append(jnp.concatenate(from_table(tables, wide, lanes, 2), axis=0))
+    out = split_dot(halves(jnp.concatenate(tiles, axis=1)), (ky[0], ky[1]))
+    for b in range(first.shape[1]):
+        for i in range(2):
+            field = out[2 * b * HALO : 2 * (b + 1) * HALO, i * lanes : (i + 1) * lanes]
+            send_strips(first, second, (i, b), field[:HALO], field[HALO:])
+
+
+def scatter_kernel(wide, *refs):
+    packs, (vals, ky, y1, y2) = refs[0:3], refs[3:]
+    blocks, tx, lanes = y1.shape
+    members = packs[0].shape[0] - 3
+    parts, short = chunks(tx, wide, lanes)
+    tiles = []
+    for t in range(3):
+        tables = scatter_tables(packs[t].at[0], vals, t, members, short, parts * wide, lambda code: decode(code, short))
+        tiles.append(jnp.concatenate(from_table(tables, wide, lanes, parts), axis=0))
+    out = split_dot(halves(jnp.concatenate(tiles, axis=1)), (ky[0], ky[1]))
     for b in range(blocks):
-        for i, y in enumerate((y1, y2)):
-            field = out[b * tx : (b + 1) * tx, i * lanes : (i + 1) * lanes]
-            y[b] = field
-            send_strips(first, second, (i, b), field)
+        y1[b] = out[b * tx : (b + 1) * tx, :lanes]
+        y2[b] = out[b * tx : (b + 1) * tx, lanes:]
 
 
 def gather_kernel(has_step, wide, *refs):
-    y1, y2, from_first, from_second, kx, pack, weights, control, smoothed = refs[:9]
-    refs = refs[9:]
+    y1, y2, from_first, from_second, kx, kxx, pack, weights, control, smoothed = refs[:10]
+    refs = refs[10:]
     each = range(y1.shape[0])
     if has_step:
         old_grad, old_smooth, sums, new_control, new_smoothed = refs[:5]
         refs = refs[5:]
         step = step_rows(sums[...])
     grad_out, smooth_out, seen, to_all = refs[:4]
-    once = x_smooth(kx[0], [y1[b] for b in each], [from_first[0, b] for b in each], [from_second[0, b] for b in each])
-    twice = x_smooth(kx[1], [y2[b] for b in each], [from_first[1, b] for b in each], [from_second[1, b] for b in each])
+    once = x_smooth(kx, [y1[b] for b in each], [from_first[0, b] for b in each], [from_second[0, b] for b in each])
+    twice = x_smooth(kxx, [y2[b] for b in each], [from_first[1, b] for b in each], [from_second[1, b] for b in each])
     squares = None
     outs = []
     for b in each:
@@ -461,8 +480,8 @@
 HBM = pl.BlockSpec(memory_space=pltpu.HBM)
 
 
-def call(kernel, ins, outs, scratch=(), us=3.0, space=VMEM):
-    shapes = [jax.ShapeDtypeStruct(s, F32) for s in outs]
+def call(kernel, ins, outs, scratch=(), us=3.0, space=VMEM, kind=F32):
+    shapes = [jax.ShapeDtypeStruct(s, kind) for s in outs]
     return pl.pallas_call(
         kernel,
         out_shape=shapes,
@@ -474,37 +493,34 @@
     )(*ins)
 
 
-def first_partner(i, n):
-    return i ^ 1 if i ^ 1 < n else i
-
-
-def second_partner(i, n):
-    return (((i + 1) ^ 1) - 1) % n
-
-
-def swap_first(value, axis):
-    n = lax.axis_size(axis)
-    return lax.ppermute(value, axis, [(i, first_partner(i, n)) for i in range(n)])
-
-
-def swap_second(value, axis):
+def swap_over(value, axis, to):
     n, k = lax.axis_size(axis), lax.axis_size("gx")
     if axis == "gx":
-        return lax.ppermute(value, axis, [(i, second_partner(i, n)) for i in range(n)])
+        return lax.ppermute(value, axis, [(i, to(i, n) % n) for i in range(n)])
     sends = []
     for i in range(n):
-        to = ((i + 1) ^ 1) - 1
         for g in range(k):
-            sends.append((i * k + g, to * k + g if 0 <= to < n else i * k + first_partner(g, k)))
+            inside = 0 <= to(i, n) < n
+            sends.append((i * k + g, to(i, n) * k + g if inside else i * k + (g ^ 1 if g ^ 1 < k else g)))
     return lax.ppermute(value, (axis, "gx"), sends)
+
+
+def swap_first(value, axis):
+    return swap_over(value, axis, lambda i, n: i ^ 1)
+
+
+def swap_second(value, axis):
+    return swap_over(value, axis, lambda i, n: ((i + 1) ^ 1) - 1)
 
 
 def swap_pairs(value, axis):
     return [swap_first(value, axis), swap_second(value, axis)]
 
 
-def swap_each(first, second, axis):
-    return swap_first(first, axis), swap_second(second, axis)
+def swap_x(first, second):
+    near = swap_first(first, "gx")
+    far = swap_second(second, "gx")
+    return near, far
 
 
 def swap_mem(value):
@@ -536,10 +552,13 @@
     strip = (blocks, HALO, lanes)
     pair = n_mem == 2 and members * wide == lanes
 
+    edge = (blocks * lanes * RADIUS // ty, tx)
+    short = chunks(tx, wide, lanes)[1]
+    long = tx + 2 * HALO
     if pair:
         theirs, mine = call(
-            lambda c, a, b, t: halves_kernel(c, b, a, t),
-            [own],
+            cut_kernel,
+            [pltpu.with_memory_space_constraint(own, pltpu.HBM)],
             [(lanes, tx)] * 2,
             [pltpu.SemaphoreType.DMA((members, 2))],
             us=1.0,
@@ -549,52 +568,41 @@
     else:
         spread = levels_out(own).reshape(blocks * lanes, tx)
         tiles = [spread[b * lanes : (b + 1) * lanes] for b in range(blocks)]
-    info, pobs, ky, ky_first, kx = call(
-        functools.partial(prep_kernel, ty, wide),
+    info, pobs = call(
+        functools.partial(pobs_kernel, wide, short),
         [pert, obs_cell, huber_flag, innovation, precision],
-        [(3,) + obs, (members,) + obs, (3 * lanes, 2 * lanes), (lanes + 2 * lanes * RADIUS // ty, lanes), (2, tx, tx + 2 * HALO)],
-        [
-            pltpu.VMEM((members * variables * tx // 2, 2 * zy), BF16),
-            pltpu.VMEM(pert.shape, BF16),
-            pltpu.VMEM(obs, jnp.int32),
-            pltpu.VMEM(obs, jnp.int32),
-            pltpu.VMEM(obs, F32),
-            pltpu.VMEM(obs, F32),
-            pltpu.SemaphoreType.DMA((5,)),
-        ],
-        us=4.0,
-        space=HBM,
+        [(3,) + obs, (members,) + obs],
+        us=2.0,
     )
-    first, second = call(functools.partial(strips_kernel, ty), tiles, [(blocks * lanes * RADIUS // ty, tx)] * 2, us=0.5)
-    before, after = swap_each(first, second, "gy")
+    first, second = call(functools.partial(strips_kernel, ty), tiles, [edge, edge], us=0.2)
+    before, after = swap_first(first, "gy"), swap_second(second, "gy")
     if pair:
         pobs_parts = [pobs, swap_mem(pobs)]
     else:
         pobs_parts = [lax.all_gather(pobs, "mem", axis=0, tiled=True)]
-    y1, state, first, second, pack = call(
-        functools.partial(start_kernel, blocks, len(pobs_parts)),
-        tiles + [before, after, ky_first, info] + pobs_parts,
-        [field, field, strip, strip, (3 + everyone,) + obs],
-        us=1.0,
+    ky_first, kx = call(
+        functools.partial(once_matrices, ty), [], [(2, lanes + 2 * lanes * RADIUS // ty, lanes), (2, tx, long)], us=0.3, kind=BF16
     )
-    from_first, from_second = swap_each(first, second, "gx")
+    y1, state, first, second = call(
+        functools.partial(start_kernel, blocks), tiles + [before, after, ky_first], [field, field, strip, strip], us=1.0
+    )
+    from_first, from_second = swap_x(first, second)
+    (pack,) = call(pack_kernel, [info] + pobs_parts, [(3 + everyone,) + obs], us=0.3)
     packs = [pack] + swap_pairs(pack, "gy")
     smoothed, seen = call(functools.partial(first_seen_kernel, wide), [y1, from_first, from_second, kx, pack], [field, obs], us=1.5)
     incs = [seen] + swap_pairs(seen, "gy")
+    ky, kxx = call(functools.partial(twice_matrices, ty), [], [(2, 3 * lanes, 2 * lanes), (2, tx, long)], us=1.5, kind=BF16)
     steps, sums, grad, smooth_grad = None, None, None, None
     double = (2,) + strip
     for iteration in range(ITERS):
         later, last = iteration > 0, iteration + 1 == ITERS
         ins = packs + incs + (steps + [sums] if later else []) + [ky]
-        y1, y2, first, second, weights = call(
-            functools.partial(scatter_kernel, later, wide),
-            ins,
-            [field, field, double, double, obs],
-            [pltpu.VMEM((2 * everyone,) + obs, F32)],
-            us=3.0,
+        first, second, weights, vals = call(
+            functools.partial(edge_kernel, later, wide, tx), ins, [double, double, obs, (3, 2 * everyone) + obs], us=1.0
         )
-        from_first, from_second = swap_each(first, second, "gx")
-        ins = [y1, y2, from_first, from_second, kx, pack, weights, state, smoothed]
+        from_first, from_second = swap_x(first, second)
+        y1, y2 = call(functools.partial(scatter_kernel, wide), packs + [vals, ky], [field, field], us=2.5)
+        ins = [y1, y2, from_first, from_second, kx, kxx, pack, weights, state, smoothed]
         outs = [field, field, obs, (n_all, 128)]
         if later:
             ins += [grad, smooth_grad, sums]

time: 68.4 us -> 61.8 us (0.904)
  waiting for transfers between devices: 23.7 us -> 8.92 us
  blocking collectives: 0 us -> 9.64 us
  starting transfers between devices: 25.9 us -> 22.9 us
  Pallas kernels: 16.8 us -> 19.2 us
  local copies, waits for them, and re-layouts: 0.92 us -> 0.02 us
    all_to_all x0 -> x1, blocking collectives: none -> 9.64 us  [per_device(): sums = lax.all_to_all(to_all, axes, 0, 0, tiled=True)]
    all_to_all x2 -> x1, waiting for transfers between devices: 12.3 us -> 5.21 us  [per_device(): sums = lax.all_to_all(to_all, axes, 0, 0, tiled=True)]
    ppermute x14, waiting for transfers between devices: 6.78 us -> 1.32 us  [the longest x8 1.18 us: swap_over(): return lax.ppermute(value, (axis, 'gx'), sends)]
    all_to_all x2 -> x1, starting transfers between devices: 6.22 us -> 3.02 us  [per_device(): sums = lax.all_to_all(to_all, axes, 0, 0, tiled=True)]
    pallas_call x11 -> x16, Pallas kernels: 16.8 us -> 19.2 us  [call(): pl.pallas_call(kernel, out_shape=shapes, in_specs=[space] * len(ins), out...]
    ppermute x4, waiting for transfers between devices: 4.64 us -> 2.39 us  [swap_mem(): return lax.ppermute(value, 'mem', [(0, 1), (1, 0)])]
    unnamed x14 -> x12, local copies, waits for them, and re-layouts: 0.92 us -> 0.02 us
  transfers between devices with their start and end apart: 20 -> 19, of which waited for: 9 -> 5; matrix products, arithmetic and copies ran while one was open for 0% -> 0% of each run, Pallas kernels for 15% -> 23%
where the time goes in v4:
time: 61.8 us; the launch traced here: 61.5 us
  starting transfers between devices  22.9 us (37%)
  Pallas kernels  19.2 us (31%)
  blocking collectives  9.64 us (16%)
  waiting for transfers between devices  8.92 us (14%)
  between operations  0.86 us (1%)
    pallas_call x16, Pallas kernels, call(): pl.pallas_call(kernel, out_shape=shapes, in_specs=[space] * len(ins), out...  19.2 us
    all_to_all x1, blocking collectives, per_device(): sums = lax.all_to_all(to_all, axes, 0, 0, tiled=True)  9.64 us
    ppermute x8, starting transfers between devices, swap_over(): return lax.ppermute(value, (axis, 'gx'), sends)  8.86 us
    ppermute x4, starting transfers between devices, swap_mem(): return lax.ppermute(value, 'mem', [(0, 1), (1, 0)])  6.89 us
    all_to_all x1, waiting for transfers between devices, per_device(): sums = lax.all_to_all(to_all, axes, 0, 0, tiled=True)  5.21 us
    ppermute x6, starting transfers between devices, swap_over(): return lax.ppermute(value, axis, [(i, to(i, n) % n) for i in range(n)])  4.13 us
    all_to_all x1, starting transfers between devices, per_device(): sums = lax.all_to_all(to_all, axes, 0, 0, tiled=True)  3.02 us
    ppermute x4, waiting for transfers between devices, swap_mem(): return lax.ppermute(value, 'mem', [(0, 1), (1, 0)])  2.39 us
  transfers between devices with their start and end apart: 19, of which 5 were waited for; matrix products, arithmetic and copies ran while one was open for 0% of the time, Pallas kernels for 23%

profile of v4, /device:TPU:0, one launch (start us, length us, event | category | flops | bytes accessed | tf_op | source)
XLA Modules:
  0.0 61.5 jit_solution(996275700116335819)
XLA Ops:
  1.5 3.1 %collective-permute-start.3 = (f32[128,128]{1,0:T(8,128)S(1)}, f32[128,128]{1,0:T(8,128)S(1)}, u32[]{:S(2)}, u32[]{:S(2)}) collective-permute-start(f32[128,128]{1,0:T(8,128)S(1)} %get-tuple-element.45), channel_id=1, source_target_pairs={{0,16},{16,0},{1,17},{17,1},{2,18},{18,2},{3,19},{19,3},{4,20},{20... | collective-permute-start | bytes 196616 | tf_op jit(solution)/shard_map/ppermute | solution.py:527
  4.5 2.2 %collective-permute-done.3.refs_1_ = f32[128,128]{1,0:T(8,128)S(1)} collective-permute-done((f32[128,128]{1,0:T(8,128)S(1)}, f32[128,128]{1,0:T(8,128)S(1)}, u32[]{:S(2)}, u32[]{:S(2)}) %collective-permute-start.3) | collective-permute-done | bytes 65568 | tf_op jit(solution)/shard_map/ppermute | solution.py:527
  6.8 2.1 %collective-permute-start.4 = (f32[128,128]{1,0:T(8,128)S(1)}, f32[128,128]{1,0:T(8,128)S(1)}, u32[]{:S(2)}, u32[]{:S(2)}) collective-permute-start(f32[128,128]{1,0:T(8,128)S(1)} %get-tuple-element.46), channel_id=1, source_target_pairs={{0,4},{1,5},{2,6},{3,7},{4,0},{5,1},{6,2},{7,3},{8,12},{9,13},{10,... | collective-permute-start | bytes 196616 | tf_op jit(solution)/shard_map/ppermute | solution.py:505
  9.0 2.5 %shard_map.86 = (f32[3,32,128]{2,1,0:T(8,128)S(1)}, f32[2,32,128]{2,1,0:T(8,128)S(1)}) custom-call(bf16[2,5,128,128]{3,2,1,0:T(8,128)(2,1)S(1)} %bitcast.17, s32[32,128]{1,0:T(8,128)S(1)} %copy-done.2, s32[32,128]{1,0:T(8,128)S(1)} %copy-done.3, f32[32,128]{1,0:T(8,128)S(1)} %copy-done.4, f32[32,128]{1,0:T(8,128)S(1)} %copy-done.5), custom_call_target="tpu_custom_call" | custom-call | flops 2000000000 | bytes 1048576 | tf_op jit(solution)/shard_map/pallas_call | solution.py:485
  11.5 1.6 %collective-permute-start = (f32[2,32,128]{2,1,0:T(8,128)S(1)}, f32[2,32,128]{2,1,0:T(8,128)S(1)}, u32[]{:S(2)}, u32[]{:S(2)}) collective-permute-start(f32[2,32,128]{2,1,0:T(8,128)S(1)} %get-tuple-element.43.refs_0_), channel_id=1, source_target_pairs={{0,16},{16,0},{1,17},{17,1},{2,18},{18,2},{3,19},{19,3},{4,20},{20... | collective-permute-start | bytes 98312 | tf_op jit(solution)/shard_map/ppermute | solution.py:527
  14.0 1.4 %collective-permute-start.7 = (f32[2,8,128]{2,1,0:T(8,128)S(1)}, f32[2,8,128]{2,1,0:T(8,128)S(1)}, u32[]{:S(2)}, u32[]{:S(2)}) collective-permute-start(f32[2,8,128]{2,1,0:T(8,128)S(1)} %get-tuple-element.51), channel_id=1, source_target_pairs={{0,3},{1,2},{2,1},{3,0},{4,7},{5,6},{6,5},{7,4},{8,11},{9,10},{10,... | collective-permute-start | bytes 24584 | tf_op jit(solution)/shard_map/ppermute | solution.py:499
  15.5 3.2 %collective-permute-start.1 = (f32[7,32,128]{2,1,0:T(8,128)S(1)}, f32[7,32,128]{2,1,0:T(8,128)S(1)}, u32[]{:S(2)}, u32[]{:S(2)}) collective-permute-start(f32[7,32,128]{2,1,0:T(8,128)S(1)} %shard_map.87.pack.refs_0_.refs_6_), channel_id=1, source_target_pairs={{0,4},{1,5},{2,6},{3,7},{4,0},{5,1},{6,2},{7,3},{8,12},{9,13},{10,... | collective-permute-start | bytes 344072 | tf_op jit(solution)/shard_map/ppermute | solution.py:505
  18.8 1.2 %shard_map.92 = (f32[2,128,128]{2,1,0:T(8,128)S(1)}, f32[32,128]{1,0:T(8,128)S(1)}) custom-call(f32[2,128,128]{2,1,0:T(8,128)S(1)} %get-tuple-element.49.y1, f32[2,8,128]{2,1,0:T(8,128)S(1)} %collective-permute-done.6.from_first, f32[2,8,128]{2,1,0:T(8,128)S(1)} %collective-permute-done.7.from_second, bf16[2,128,144]{2,1,0:T(8,128)(2,1)S(1)} %get-tuple-element.52.kx.refs_4_, ...), custom_call_target="tpu_custom_call" | custom-call | flops 1500000000 | bytes 1048576 | tf_op jit(solution)/shard_map/pallas_call | solution.py:485
  20.0 1.3 %collective-permute-start.8 = (f32[32,128]{1,0:T(8,128)S(1)}, f32[32,128]{1,0:T(8,128)S(1)}, u32[]{:S(2)}, u32[]{:S(2)}) collective-permute-start(f32[32,128]{1,0:T(8,128)S(1)} %get-tuple-element.53.refs_3_), channel_id=1, source_target_pairs={{0,4},{1,5},{2,6},{3,7},{4,0},{5,1},{6,2},{7,3},{8,12},{9,13},{10,... | collective-permute-start | bytes 49160 | tf_op jit(solution)/shard_map/ppermute | solution.py:505
  21.4 1.1 %shard_map.93 = (bf16[2,384,256]{2,1,0:T(8,128)(2,1)S(1)}, bf16[2,128,144]{2,1,0:T(8,128)(2,1)S(1)}) custom-call(), custom_call_target="tpu_custom_call" | custom-call | flops 1500000000 | bytes 1048576 | tf_op jit(solution)/shard_map/pallas_call | solution.py:485
  22.6 1.2 %collective-permute-done.8.refs_4_ = f32[32,128]{1,0:T(8,128)S(1)} collective-permute-done((f32[32,128]{1,0:T(8,128)S(1)}, f32[32,128]{1,0:T(8,128)S(1)}, u32[]{:S(2)}, u32[]{:S(2)}) %collective-permute-start.8) | collective-permute-done | bytes 16416 | tf_op jit(solution)/shard_map/ppermute | solution.py:505
  23.8 1.6 %shard_map.94 = (f32[2,2,8,128]{3,2,1,0:T(8,128)S(1)}, f32[2,2,8,128]{3,2,1,0:T(8,128)S(1)}, f32[32,128]{1,0:T(8,128)S(1)}, f32[3,8,32,128]{3,2,1,0:T(8,128)S(1)}) custom-call(f32[7,32,128]{2,1,0:T(8,128)S(1)} %shard_map.87.pack.refs_0_.refs_6_, f32[7,32,128]{2,1,0:T(8,128)S(1)} %collective-permute-done.1.refs_1_, ...), custom_call_target="tpu_custom_call" | custom-call | flops 1000000000 | bytes 1048576 | tf_op jit(solution)/shard_map/pallas_call | solution.py:485
  25.5 1.6 %collective-permute-start.11 = (f32[2,2,8,128]{3,2,1,0:T(8,128)S(1)}, f32[2,2,8,128]{3,2,1,0:T(8,128)S(1)}, u32[]{:S(2)}, u32[]{:S(2)}) collective-permute-start(f32[2,2,8,128]{3,2,1,0:T(8,128)S(1)} %get-tuple-element.59), channel_id=1, source_target_pairs={{0,3},{1,2},{2,1},{3,0},{4,7},{5,6},{6,5},{7,4},{8,11},{9,10},{10,... | collective-permute-start | bytes 49160 | tf_op jit(solution)/shard_map/ppermute | solution.py:499
  27.1 2.5 %shard_map.95 = (f32[2,128,128]{2,1,0:T(8,128)S(1)}, f32[2,128,128]{2,1,0:T(8,128)S(1)}) custom-call(f32[7,32,128]{2,1,0:T(8,128)S(1)} %shard_map.87.pack.refs_0_.refs_6_, f32[7,32,128]{2,1,0:T(8,128)S(1)} %collective-permute-done.1.refs_1_, f32[7,32,128]{2,1,0:T(8,128)S(1)} %collective-permute-done.2.refs_2_, ...), custom_call_target="tpu_custom_call" | custom-call | flops 2500000000 | bytes 1048576 | tf_op jit(solution)/shard_map/pallas_call | solution.py:485
  29.6 1.9 %shard_map.96 = (f32[2,128,128]{2,1,0:T(8,128)S(1)}, f32[2,128,128]{2,1,0:T(8,128)S(1)}, f32[32,128]{1,0:T(8,128)S(1)}, f32[32,128]{1,0:T(8,128)}) custom-call(f32[2,128,128]{2,1,0:T(8,128)S(1)} %get-tuple-element.56.refs_0_, f32[2,128,128]{2,1,0:T(8,128)S(1)} %get-tuple-element.57.refs_1_, f32[2,2,8,128]{3,2,1,0:T(8,128)S(1)} %collective-permute-done.10.refs_2_, ...), custom_call_target="tpu_custom_call" | custom-call | flops 1500000000 | bytes 1048576 | tf_op jit(solution)/shard_map/pallas_call | solution.py:485
  31.4 2.0 %collective-permute-start.12 = (f32[32,128]{1,0:T(8,128)S(1)}, f32[32,128]{1,0:T(8,128)S(1)}, u32[]{:S(2)}, u32[]{:S(2)}) collective-permute-start(f32[32,128]{1,0:T(8,128)S(1)} %get-tuple-element.64.refs_6_), channel_id=1, source_target_pairs={{0,4},{1,5},{2,6},{3,7},{4,0},{5,1},{6,2},{7,3},{8,12},{9,13},{10,... | collective-permute-start | bytes 49160 | tf_op jit(solution)/shard_map/ppermute | solution.py:505
  33.5 3.0 %all-to-all-start = ((f32[32,1,128]{2,1,0:T(1,128)}), f32[32,1,128]{2,1,0:T(1,128)S(1)}, u32[]{:S(2)}, u32[]{:S(2)}) async-start(f32[32,1,128]{2,1,0:T(1,128)} %bitcast.3), calls=%async_computation | async-start | bytes 32768 | tf_op jit(solution)/shard_map/all_to_all | solution.py:619
  36.6 1.7 %collective-permute-start.17 = (f32[2,5,64,128]{3,2,1,0:T(8,128)S(1)}, f32[2,5,64,128]{3,2,1,0:T(8,128)S(1)}, u32[]{:S(2)}, u32[]{:S(2)}) collective-permute-start(f32[2,5,64,128]{3,2,1,0:T(8,128)S(1)} %shard_map.100), channel_id=1, source_target_pairs={{0,16},{16,0},{1,17},{17,1},{2,18},{18,2},{3,19},{19,3},{4,20},{20... | collective-permute-start | bytes 983048 | tf_op jit(solution)/shard_map/ppermute | solution.py:527
  38.2 5.2 %all-to-all-done = f32[32,1,128]{2,1,0:T(1,128)S(1)} async-done(((f32[32,1,128]{2,1,0:T(1,128)}), f32[32,1,128]{2,1,0:T(1,128)S(1)}, u32[]{:S(2)}, u32[]{:S(2)}) %all-to-all-start) | async-done | bytes 16416 | tf_op jit(solution)/shard_map/all_to_all | solution.py:619
  43.4 1.8 %shard_map.97 = (f32[2,2,8,128]{3,2,1,0:T(8,128)S(1)}, f32[2,2,8,128]{3,2,1,0:T(8,128)S(1)}, f32[32,128]{1,0:T(8,128)S(1)}, f32[3,8,32,128]{3,2,1,0:T(8,128)S(1)}) custom-call(f32[7,32,128]{2,1,0:T(8,128)S(1)} %shard_map.87.pack.refs_0_.refs_6_, f32[7,32,128]{2,1,0:T(8,128)S(1)} %collective-permute-done.1.refs_1_, ...), custom_call_target="tpu_custom_call" | custom-call | flops 1000000000 | bytes 1048576 | tf_op jit(solution)/shard_map/pallas_call | solution.py:485
  46.0 2.5 %shard_map.98 = (f32[2,128,128]{2,1,0:T(8,128)S(1)}, f32[2,128,128]{2,1,0:T(8,128)S(1)}) custom-call(f32[7,32,128]{2,1,0:T(8,128)S(1)} %shard_map.87.pack.refs_0_.refs_6_, f32[7,32,128]{2,1,0:T(8,128)S(1)} %collective-permute-done.1.refs_1_, f32[7,32,128]{2,1,0:T(8,128)S(1)} %collective-permute-done.2.refs_2_, ...), custom_call_target="tpu_custom_call" | custom-call | flops 2500000000 | bytes 1048576 | tf_op jit(solution)/shard_map/pallas_call | solution.py:485
  48.6 1.8 %shard_map.99 = (f32[2,128,128]{2,1,0:T(8,128)S(1)}, f32[2,128,128]{2,1,0:T(8,128)S(1)}, f32[2,128,128]{2,1,0:T(8,128)S(1)}, f32[2,128,128]{2,1,0:T(8,128)S(1)},...) custom-call(f32[2,128,128]{2,1,0:T(8,128)S(1)} %get-tuple-element.67.refs_0_, ...), custom_call_target="tpu_custom_call" | custom-call | flops 1500000000 | bytes 1048576 | tf_op jit(solution)/shard_map/pallas_call | solution.py:485
  51.0 9.6 %all_to_all.22 = f32[32,1,128]{2,1,0:T(1,128)S(1)} all-to-all(f32[32,1,128]{2,1,0:T(1,128)S(1)} %bitcast.15), channel_id=1, replica_groups=mesh['mem'=2,'gy'=4,'gx'=4] {'mem','gy','gx'}, dimensions={0} | all-to-all | bytes 32768 | tf_op jit(solution)/shard_map/all_to_all | solution.py:619
  60.6 0.9 %shard_map.101 = (f32[2,128,128]{2,1,0:T(8,128)}, f32[5,64,128]{2,1,0:T(8,128)}) custom-call(f32[32,128]{1,0:T(8,128)S(1)} %bitcast.16, f32[2,128,128]{2,1,0:T(8,128)S(1)} %get-tuple-element.75.control, f32[2,128,128]{2,1,0:T(8,128)S(1)} %get-tuple-element.76.grad, f32[2,128,128]{2,1,0:T(8,128)S(1)} %collective-permute-done.16.back, ...), custom_call_target="tpu_custom_call" | custom-call | flops 1500000000 | bytes 1048576 | tf_op jit(solution)/shard_map/pallas_call | solution.py:485
  (43 shorter events, 3.6 us)
Async XLA Ops:
  1.5 5.3 %collective-permute-start.3 = (f32[128,128]{1,0:T(8,128)S(1)}, f32[128,128]{1,0:T(8,128)S(1)}, u32[]{:S(2)}, u32[]{:S(2)}) collective-permute-start(f32[128,128]{1,0:T(8,128)S(1)} %get-tuple-element.45), channel_id=1, source_target_pairs={{0,16},{16,0},{1,17},{17,1},{2,18},{18,2},{3,19},{19,3},{4,20},{20... | collective-permute-start | bytes 196616 | tf_op jit(solution)/shard_map/ppermute | solution.py:527
  6.8 2.2 %copy-start.2 = (s32[32,128]{1,0:T(8,128)S(1)}, s32[32,128]{1,0:T(8,128)}, u32[]{:S(2)}) copy-start(s32[32,128]{1,0:T(8,128)} %cell.1) | copy-start | bytes 49156
  6.8 2.2 %copy-start.3 = (s32[32,128]{1,0:T(8,128)S(1)}, s32[32,128]{1,0:T(8,128)}, u32[]{:S(2)}) copy-start(s32[32,128]{1,0:T(8,128)} %flag.1) | copy-start | bytes 49156
  6.8 2.2 %copy-start.4 = (f32[32,128]{1,0:T(8,128)S(1)}, f32[32,128]{1,0:T(8,128)}, u32[]{:S(2)}) copy-start(f32[32,128]{1,0:T(8,128)} %innov.1) | copy-start | bytes 49156
  6.8 2.2 %copy-start.5 = (f32[32,128]{1,0:T(8,128)S(1)}, f32[32,128]{1,0:T(8,128)}, u32[]{:S(2)}) copy-start(f32[32,128]{1,0:T(8,128)} %prec.1) | copy-start | bytes 49156
  6.8 6.5 %collective-permute-start.4 = (f32[128,128]{1,0:T(8,128)S(1)}, f32[128,128]{1,0:T(8,128)S(1)}, u32[]{:S(2)}, u32[]{:S(2)}) collective-permute-start(f32[128,128]{1,0:T(8,128)S(1)} %get-tuple-element.46), channel_id=1, source_target_pairs={{0,4},{1,5},{2,6},{3,7},{4,0},{5,1},{6,2},{7,3},{8,12},{9,13},{10,... | collective-permute-start | bytes 196616 | tf_op jit(solution)/shard_map/ppermute | solution.py:505
  9.0 4.4 %collective-permute-start.5 = (f32[128,128]{1,0:T(8,128)S(1)}, f32[128,128]{1,0:T(8,128)S(1)}, u32[]{:S(2)}, u32[]{:S(2)}) collective-permute-start(f32[128,128]{1,0:T(8,128)S(1)} %get-tuple-element.47), channel_id=1, source_target_pairs={{0,1},{1,0},{2,3},{3,2},{4,8},{5,9},{6,10},{7,11},{8,4},{9,5},{10,... | collective-permute-start | bytes 196616 | tf_op jit(solution)/shard_map/ppermute | solution.py:505
  11.5 4.0 %collective-permute-start = (f32[2,32,128]{2,1,0:T(8,128)S(1)}, f32[2,32,128]{2,1,0:T(8,128)S(1)}, u32[]{:S(2)}, u32[]{:S(2)}) collective-permute-start(f32[2,32,128]{2,1,0:T(8,128)S(1)} %get-tuple-element.43.refs_0_), channel_id=1, source_target_pairs={{0,16},{16,0},{1,17},{17,1},{2,18},{18,2},{3,19},{19,3},{4,20},{20... | collective-permute-start | bytes 98312 | tf_op jit(solution)/shard_map/ppermute | solution.py:527
  13.7 5.1 %collective-permute-start.6 = (f32[2,8,128]{2,1,0:T(8,128)S(1)}, f32[2,8,128]{2,1,0:T(8,128)S(1)}, u32[]{:S(2)}, u32[]{:S(2)}) collective-permute-start(f32[2,8,128]{2,1,0:T(8,128)S(1)} %get-tuple-element.50), channel_id=1, source_target_pairs={{0,1},{1,0},{2,3},{3,2},{4,5},{5,4},{6,7},{7,6},{8,9},{9,8},{10,11... | collective-permute-start | bytes 24584 | tf_op jit(solution)/shard_map/ppermute | solution.py:499
  14.0 4.8 %collective-permute-start.7 = (f32[2,8,128]{2,1,0:T(8,128)S(1)}, f32[2,8,128]{2,1,0:T(8,128)S(1)}, u32[]{:S(2)}, u32[]{:S(2)}) collective-permute-start(f32[2,8,128]{2,1,0:T(8,128)S(1)} %get-tuple-element.51), channel_id=1, source_target_pairs={{0,3},{1,2},{2,1},{3,0},{4,7},{5,6},{6,5},{7,4},{8,11},{9,10},{10,... | collective-permute-start | bytes 24584 | tf_op jit(solution)/shard_map/ppermute | solution.py:499
  15.5 7.0 %collective-permute-start.1 = (f32[7,32,128]{2,1,0:T(8,128)S(1)}, f32[7,32,128]{2,1,0:T(8,128)S(1)}, u32[]{:S(2)}, u32[]{:S(2)}) collective-permute-start(f32[7,32,128]{2,1,0:T(8,128)S(1)} %shard_map.87.pack.refs_0_.refs_6_), channel_id=1, source_target_pairs={{0,4},{1,5},{2,6},{3,7},{4,0},{5,1},{6,2},{7,3},{8,12},{9,13},{10,... | collective-permute-start | bytes 344072 | tf_op jit(solution)/shard_map/ppermute | solution.py:505
  18.7 3.8 %collective-permute-start.2 = (f32[7,32,128]{2,1,0:T(8,128)S(1)}, f32[7,32,128]{2,1,0:T(8,128)S(1)}, u32[]{:S(2)}, u32[]{:S(2)}) collective-permute-start(f32[7,32,128]{2,1,0:T(8,128)S(1)} %shard_map.87.pack.refs_0_.refs_6_), channel_id=1, source_target_pairs={{0,1},{1,0},{2,3},{3,2},{4,8},{5,9},{6,10},{7,11},{8,4},{9,5},{10,... | collective-permute-start | bytes 344072 | tf_op jit(solution)/shard_map/ppermute | solution.py:505
  20.0 3.8 %collective-permute-start.8 = (f32[32,128]{1,0:T(8,128)S(1)}, f32[32,128]{1,0:T(8,128)S(1)}, u32[]{:S(2)}, u32[]{:S(2)}) collective-permute-start(f32[32,128]{1,0:T(8,128)S(1)} %get-tuple-element.53.refs_3_), channel_id=1, source_target_pairs={{0,4},{1,5},{2,6},{3,7},{4,0},{5,1},{6,2},{7,3},{8,12},{9,13},{10,... | collective-permute-start | bytes 49160 | tf_op jit(solution)/shard_map/ppermute | solution.py:505
  21.3 2.5 %collective-permute-start.9 = (f32[32,128]{1,0:T(8,128)S(1)}, f32[32,128]{1,0:T(8,128)S(1)}, u32[]{:S(2)}, u32[]{:S(2)}) collective-permute-start(f32[32,128]{1,0:T(8,128)S(1)} %get-tuple-element.53.refs_3_), channel_id=1, source_target_pairs={{0,1},{1,0},{2,3},{3,2},{4,8},{5,9},{6,10},{7,11},{8,4},{9,5},{10,... | collective-permute-start | bytes 49160 | tf_op jit(solution)/shard_map/ppermute | solution.py:505
  25.4 4.2 %collective-permute-start.10 = (f32[2,2,8,128]{3,2,1,0:T(8,128)S(1)}, f32[2,2,8,128]{3,2,1,0:T(8,128)S(1)}, u32[]{:S(2)}, u32[]{:S(2)}) collective-permute-start(f32[2,2,8,128]{3,2,1,0:T(8,128)S(1)} %get-tuple-element.58), channel_id=1, source_target_pairs={{0,1},{1,0},{2,3},{3,2},{4,5},{5,4},{6,7},{7,6},{8,9},{9,8},{10,11... | collective-permute-start | bytes 49160 | tf_op jit(solution)/shard_map/ppermute | solution.py:499
  25.5 4.1 %collective-permute-start.11 = (f32[2,2,8,128]{3,2,1,0:T(8,128)S(1)}, f32[2,2,8,128]{3,2,1,0:T(8,128)S(1)}, u32[]{:S(2)}, u32[]{:S(2)}) collective-permute-start(f32[2,2,8,128]{3,2,1,0:T(8,128)S(1)} %get-tuple-element.59), channel_id=1, source_target_pairs={{0,3},{1,2},{2,1},{3,0},{4,7},{5,6},{6,5},{7,4},{8,11},{9,10},{10,... | collective-permute-start | bytes 49160 | tf_op jit(solution)/shard_map/ppermute | solution.py:499
  31.4 6.8 %collective-permute-start.12 = (f32[32,128]{1,0:T(8,128)S(1)}, f32[32,128]{1,0:T(8,128)S(1)}, u32[]{:S(2)}, u32[]{:S(2)}) collective-permute-start(f32[32,128]{1,0:T(8,128)S(1)} %get-tuple-element.64.refs_6_), channel_id=1, source_target_pairs={{0,4},{1,5},{2,6},{3,7},{4,0},{5,1},{6,2},{7,3},{8,12},{9,13},{10,... | collective-permute-start | bytes 49160 | tf_op jit(solution)/shard_map/ppermute | solution.py:505
  33.5 4.7 %collective-permute-start.13 = (f32[32,128]{1,0:T(8,128)S(1)}, f32[32,128]{1,0:T(8,128)S(1)}, u32[]{:S(2)}, u32[]{:S(2)}) collective-permute-start(f32[32,128]{1,0:T(8,128)S(1)} %get-tuple-element.64.refs_6_), channel_id=1, source_target_pairs={{0,1},{1,0},{2,3},{3,2},{4,8},{5,9},{6,10},{7,11},{8,4},{9,5},{10,... | collective-permute-start | bytes 49160 | tf_op jit(solution)/shard_map/ppermute | solution.py:505
  33.5 10.0 %all-to-all-start = ((f32[32,1,128]{2,1,0:T(1,128)}), f32[32,1,128]{2,1,0:T(1,128)S(1)}, u32[]{:S(2)}, u32[]{:S(2)}) async-start(f32[32,1,128]{2,1,0:T(1,128)} %bitcast.3), calls=%async_computation | async-start | bytes 32768 | tf_op jit(solution)/shard_map/all_to_all | solution.py:619
  36.6 24.0 %collective-permute-start.17 = (f32[2,5,64,128]{3,2,1,0:T(8,128)S(1)}, f32[2,5,64,128]{3,2,1,0:T(8,128)S(1)}, u32[]{:S(2)}, u32[]{:S(2)}) collective-permute-start(f32[2,5,64,128]{3,2,1,0:T(8,128)S(1)} %shard_map.100), channel_id=1, source_target_pairs={{0,16},{16,0},{1,17},{17,1},{2,18},{18,2},{3,19},{19,3},{4,20},{20... | collective-permute-start | bytes 983048 | tf_op jit(solution)/shard_map/ppermute | solution.py:527
  45.3 3.2 %collective-permute-start.14 = (f32[2,2,8,128]{3,2,1,0:T(8,128)S(1)}, f32[2,2,8,128]{3,2,1,0:T(8,128)S(1)}, u32[]{:S(2)}, u32[]{:S(2)}) collective-permute-start(f32[2,2,8,128]{3,2,1,0:T(8,128)S(1)} %get-tuple-element.69), channel_id=1, source_target_pairs={{0,1},{1,0},{2,3},{3,2},{4,5},{5,4},{6,7},{7,6},{8,9},{9,8},{10,11... | collective-permute-start | bytes 49160 | tf_op jit(solution)/shard_map/ppermute | solution.py:499
  45.4 3.2 %collective-permute-start.15 = (f32[2,2,8,128]{3,2,1,0:T(8,128)S(1)}, f32[2,2,8,128]{3,2,1,0:T(8,128)S(1)}, u32[]{:S(2)}, u32[]{:S(2)}) collective-permute-start(f32[2,2,8,128]{3,2,1,0:T(8,128)S(1)} %get-tuple-element.70), channel_id=1, source_target_pairs={{0,3},{1,2},{2,1},{3,0},{4,7},{5,6},{6,5},{7,4},{8,11},{9,10},{10,... | collective-permute-start | bytes 49160 | tf_op jit(solution)/shard_map/ppermute | solution.py:499
  48.6 12.0 %copy-start.1 = (f32[5,8,8,128]{3,2,1,0:T(8,128)S(1)}, f32[5,8,8,128]{3,2,1,0:T(8,128)}, u32[]{:S(2)}) copy-start(f32[5,8,8,128]{3,2,1,0:T(8,128)} %param.9) | copy-start | bytes 491524
  50.4 10.2 %collective-permute-start.16 = (f32[2,128,128]{2,1,0:T(8,128)S(1)}, f32[2,128,128]{2,1,0:T(8,128)S(1)}, u32[]{:S(2)}, u32[]{:S(2)}) collective-permute-start(f32[2,128,128]{2,1,0:T(8,128)S(1)} %get-tuple-element.77), channel_id=1, source_target_pairs={{0,16},{16,0},{1,17},{17,1},{2,18},{18,2},{3,19},{19,3},{4,20},{20... | collective-permute-start | bytes 393224 | tf_op jit(solution)/shard_map/ppermute | solution.py:527
  (1 other events, 2.2 us)

commit v5 on v4

--- a/solution.py
+++ b/solution.py
@@ -279,16 +279,17 @@
     return [out[:, i * zy : (i + 1) * zy] for i in range(len(fields))]
 
 
-def gather_at(groups, wide, pack, seen):
+def gather_at(groups, wide, pack, seen, places):
     tables = to_table(groups, wide)
     members, short = len(tables), tables[0].shape[0]
     parts = [halves(t) for t in tables]
     stacked = jnp.concatenate([p[0] for p in parts] + [p[1] for p in parts], axis=0)
     rows = members * short
+    places[0], places[1] = decode(pack[0], short)
     for j in range(0, pack.shape[1], CHUNK):
-        row, low = decode(chunk_of(pack.at[0], j), short)
-        hot = onehot_rows(row, stacked.shape[1])
+        hot = onehot_rows(chunk_of(places.at[0], j), stacked.shape[1])
         found = jnp.dot(stacked, hot, preferred_element_type=F32)
+        low = chunk_of(places.at[1], j)
         low = jnp.broadcast_to(low, (short, low.shape[1]))
         mask = iota(low.shape, 0) == low
         total = None
@@ -299,12 +300,12 @@
         store_chunk(seen, j, jnp.sum(jnp.where(mask, total, 0.0), axis=0, keepdims=True))
 
 
-def first_seen_kernel(wide, y1, from_first, from_second, kx, pack, smoothed, seen):
+def first_seen_kernel(wide, y1, from_first, from_second, kx, pack, smoothed, seen, places):
     each = range(y1.shape[0])
     outs = x_smooth(kx, [y1[b] for b in each], [from_first[b] for b in each], [from_second[b] for b in each])
     for b in each:
         smoothed[b] = outs[b]
-    gather_at(outs, wide, pack, seen)
+    gather_at(outs, wide, pack, seen, places)
 
 
 def step_rows(sums):
@@ -315,11 +316,11 @@
     return g / (g + c)
 
 
-def scatter_tables(codes, vals, t, members, short, rows, decode_at):
+def scatter_tables(places, vals, t, members, short, rows):
     acc = None
-    for j in range(0, codes.shape[0], CHUNK):
-        row, low = decode_at(chunk_of(codes, j))
-        hot = onehot_rows(row, rows)
+    for j in range(0, places.shape[1], CHUNK):
+        hot = onehot_rows(chunk_of(places.at[0], j), rows)
+        low = chunk_of(places.at[1], j)
         low = jnp.broadcast_to(low, (short, low.shape[1]))
         mask = iota(low.shape, 0) == low
         parts = []
@@ -331,45 +332,73 @@
     return [acc[2 * m * short : (2 * m + 1) * short] + acc[(2 * m + 1) * short : (2 * m + 2) * short] for m in range(members)]
 
 
+def beside(tables, per):
+    return [jnp.concatenate(tables[i : i + per], axis=1) for i in range(0, len(tables), per)]
+
+
+def observation_terms(pack, inc, vals, t):
+    misfit = inc - pack[2]
+    prec = pack[1]
+    weight = jnp.where(prec < 0, 1.0 / jnp.sqrt(1.0 + misfit * misfit), 1.0)
+    pw = jnp.abs(prec) * weight
+    q = pw * misfit
+    for m in range(pack.shape[0] - 3):
+        val = pack[3 + m] * q
+        high = val.astype(BF16).astype(F32)
+        vals[t, 2 * m] = high
+        vals[t, 2 * m + 1] = val - high
+    return pw
+
+
+def edge_tile(pack, vals, t, wide, tx, lanes, places):
+    members = pack.shape[0] - 3
+    parts, short = chunks(tx, wide, lanes)
+    row, low = decode(pack[0], short)
+    part, level_row = over(row, wide), rem(row, wide)
+    left = (row >= 0) & (part == 0) & (low < HALO)
+    right = (row >= 0) & (part == parts - 1) & (low >= short - HALO)
+    places[t, 0] = jnp.where(left | right, level_row, -1)
+    places[t, 1] = jnp.where(right, HALO, 0) + rem(low, HALO)
+    tables = scatter_tables(places.at[t], vals, t, members, 2 * HALO, wide)
+    return jnp.concatenate(beside(tables, lanes // wide), axis=0)
+
+
+def full_tile(pack, vals, t, wide, tx, lanes, places):
+    members = pack.shape[0] - 3
+    parts, short = chunks(tx, wide, lanes)
+    places[t, 0], places[t, 1] = decode(pack[0], short)
+    tables = scatter_tables(places.at[t], vals, t, members, short, parts * wide)
+    return jnp.concatenate(from_table(tables, wide, lanes, parts), axis=0)
+
+
+def own_kernel(wide, tx, lanes, pack, inc, weights, edge, full, vals, edge_places, places):
+    weights[...] = observation_terms(pack, inc[...], vals, 0)
+    edge[...] = edge_tile(pack, vals, 0, wide, tx, lanes, edge_places)
+    full[...] = full_tile(pack, vals, 0, wide, tx, lanes, places)
+
+
 def edge_kernel(has_step, wide, tx, *refs):
-    packs, incs = refs[0:3], refs[3:6]
-    refs = refs[6:]
+    count = 3 if has_step else 2
+    packs, incs = refs[:count], refs[count : 2 * count]
+    refs = refs[2 * count :]
+    tiles = []
     if has_step:
         steps, sums = refs[0:3], refs[3]
         refs = refs[4:]
         step = step_rows(sums[...])
-    ky, first, second, weights, vals = refs
-    members = packs[0].shape[0] - 3
+        ky, first, second, vals, weights, places = refs
+    else:
+        own, ky, first, second, vals, places = refs
+        tiles.append(own[...])
     lanes = ky.shape[2] // 2
-    parts, short = chunks(tx, wide, lanes)
-
-    def at_edge(code):
-        row, low = decode(code, short)
-        part, level_row = over(row, wide), rem(row, wide)
-        left = (row >= 0) & (part == 0) & (low < HALO)
-        right = (row >= 0) & (part == parts - 1) & (low >= short - HALO)
-        return jnp.where(left, level_row, jnp.where(right, wide + level_row, -1)), rem(low, HALO)
-
-    tiles = []
-    for t in range(3):
-        pack = packs[t]
+    for t in range(count):
         inc = incs[t][...]
         if has_step:
             inc = inc - step * steps[t][...]
-        misfit = inc - pack[2]
-        prec = pack[1]
-        weight = jnp.where(prec < 0, 1.0 / jnp.sqrt(1.0 + misfit * misfit), 1.0)
-        pw = jnp.abs(prec) * weight
-        q = pw * misfit
-        if t == 0:
+        pw = observation_terms(packs[t], inc, vals, t)
+        if has_step and t == 0:
             weights[...] = pw
-        for m in range(members):
-            val = pack[3 + m] * q
-            high = val.astype(BF16).astype(F32)
-            vals[t, 2 * m] = high
-            vals[t, 2 * m + 1] = val - high
-        tables = scatter_tables(pack.at[0], vals, t, members, HALO, lanes, at_edge)
-        tiles.append(jnp.concatenate(from_table(tables, wide, lanes, 2), axis=0))
+        tiles.append(edge_tile(packs[t], vals, t, wide, tx, lanes, places))
     out = split_dot(halves(jnp.concatenate(tiles, axis=1)), (ky[0], ky[1]))
     for b in range(first.shape[1]):
         for i in range(2):
@@ -377,22 +406,24 @@
             send_strips(first, second, (i, b), field[:HALO], field[HALO:])
 
 
-def scatter_kernel(wide, *refs):
-    packs, (vals, ky, y1, y2) = refs[0:3], refs[3:]
+def scatter_kernel(given, wide, *refs):
+    count = 2 if given else 3
+    packs, refs = refs[:count], refs[count:]
+    tiles = []
+    if given:
+        tiles.append(refs[0][...])
+        refs = refs[1:]
+    vals, ky, y1, y2, places = refs
     blocks, tx, lanes = y1.shape
-    members = packs[0].shape[0] - 3
-    parts, short = chunks(tx, wide, lanes)
-    tiles = []
-    for t in range(3):
-        tables = scatter_tables(packs[t].at[0], vals, t, members, short, parts * wide, lambda code: decode(code, short))
-        tiles.append(jnp.concatenate(from_table(tables, wide, lanes, parts), axis=0))
+    for t in range(count):
+        tiles.append(full_tile(packs[t], vals, t, wide, tx, lanes, places))
     out = split_dot(halves(jnp.concatenate(tiles, axis=1)), (ky[0], ky[1]))
     for b in range(blocks):
         y1[b] = out[b * tx : (b + 1) * tx, :lanes]
         y2[b] = out[b * tx : (b + 1) * tx, lanes:]
 
 
-def gather_kernel(has_step, wide, *refs):
+def gather_kernel(has_step, sent, wide, *refs):
     y1, y2, from_first, from_second, kx, kxx, pack, weights, control, smoothed = refs[:10]
     refs = refs[10:]
     each = range(y1.shape[0])
@@ -400,7 +431,10 @@
         old_grad, old_smooth, sums, new_control, new_smoothed = refs[:5]
         refs = refs[5:]
         step = step_rows(sums[...])
-    grad_out, smooth_out, seen, to_all = refs[:4]
+    if sent:
+        grad_out, smooth_out, row, back, seen, places = refs
+    else:
+        grad_out, smooth_out, row, seen, places = refs
     once = x_smooth(kx, [y1[b] for b in each], [from_first[0, b] for b in each], [from_second[0, b] for b in each])
     twice = x_smooth(kxx, [y2[b] for b in each], [from_first[1, b] for b in each], [from_second[1, b] for b in each])
     squares = None
@@ -419,15 +453,15 @@
         outs.append(smooth_grad)
         part = jnp.sum(grad * grad, axis=0, keepdims=True)
         squares = part if squares is None else squares + part
-        if len(refs) > 4 and b == y1.shape[0] - 1:
-            refs[4][0] = v
-            refs[4][1] = grad
-    gather_at(outs, wide, pack, seen)
+        if sent and b == y1.shape[0] - 1:
+            back[0] = v
+            back[1] = grad
+    gather_at(outs, wide, pack, seen, places)
     total = seen[...]
     c = jnp.sum(jnp.sum(weights[...] * total * total, axis=0, keepdims=True), axis=1, keepdims=True)
     g = jnp.sum(squares, axis=1, keepdims=True)
-    lane = iota(to_all.shape, 1)
-    to_all[...] = jnp.where(lane == 0, g, jnp.where(lane == 1, c, 0.0))
+    lane = iota(row.shape, 1)
+    row[...] = jnp.where(lane == 0, g, jnp.where(lane == 1, c, 0.0))
 
 
 def widen_kernel(pert, out):
@@ -589,39 +623,61 @@
     from_first, from_second = swap_x(first, second)
     (pack,) = call(pack_kernel, [info] + pobs_parts, [(3 + everyone,) + obs], us=0.3)
     packs = [pack] + swap_pairs(pack, "gy")
-    smoothed, seen = call(functools.partial(first_seen_kernel, wide), [y1, from_first, from_second, kx, pack], [field, obs], us=1.5)
+    where = pltpu.VMEM((2,) + obs, jnp.int32)
+    where_all = pltpu.VMEM((3, 2) + obs, jnp.int32)
+    smoothed, seen = call(
+        functools.partial(first_seen_kernel, wide), [y1, from_first, from_second, kx, pack], [field, obs], [where], us=1.5
+    )
     incs = [seen] + swap_pairs(seen, "gy")
     ky, kxx = call(functools.partial(twice_matrices, ty), [], [(2, 3 * lanes, 2 * lanes), (2, tx, long)], us=1.5, kind=BF16)
+    weights, own_edge, own_full = call(
+        functools.partial(own_kernel, wide, tx, lanes),
+        [pack, seen],
+        [obs, (blocks * 2 * HALO, lanes), (blocks * tx, lanes)],
+        [pltpu.VMEM((1, 2 * everyone) + obs, F32), where_all, where_all],
+        us=1.5,
+    )
     steps, sums, grad, smooth_grad = None, None, None, None
     double = (2,) + strip
     for iteration in range(ITERS):
         later, last = iteration > 0, iteration + 1 == ITERS
-        ins = packs + incs + (steps + [sums] if later else []) + [ky]
-        first, second, weights, vals = call(
-            functools.partial(edge_kernel, later, wide, tx), ins, [double, double, obs, (3, 2 * everyone) + obs], us=1.0
+        count = 3 if later else 2
+        known = [] if later else [own_edge]
+        ins = packs[-count:] + incs[-count:] + (steps + [sums] if later else known) + [ky]
+        outs = [double, double, (count, 2 * everyone) + obs] + ([obs] if later else [])
+        first, second, vals, *own_weights = call(
+            functools.partial(edge_kernel, later, wide, tx), ins, outs, [where_all], us=1.0
         )
+        weights = own_weights[0] if later else weights
         from_first, from_second = swap_x(first, second)
-        y1, y2 = call(functools.partial(scatter_kernel, wide), packs + [vals, ky], [field, field], us=2.5)
+        ins = packs[-count:] + ([] if later else [own_full]) + [vals, ky]
+        y1, y2 = call(functools.partial(scatter_kernel, not later, wide), ins, [field, field], [where_all], us=2.5)
         ins = [y1, y2, from_first, from_second, kx, kxx, pack, weights, state, smoothed]
-        outs = [field, field, obs, (n_all, 128)]
+        outs = [field, field, (1, 128)]
         if later:
             ins += [grad, smooth_grad, sums]
             outs = [field, field] + outs
-        if last and pair:
+        sent = last and pair
+        if sent:
             outs = outs + [(2, tx, lanes)]
-        result = list(call(functools.partial(gather_kernel, later, wide), ins, outs, us=1.5))
+        scratch = ([pltpu.VMEM(obs, F32)] if last else []) + [where]
+        if not last:
+            outs = outs + [obs]
+        result = list(call(functools.partial(gather_kernel, later, sent, wide), ins, outs, scratch, us=1.5))
         if later:
             state, smoothed = result[:2]
             result = result[2:]
-        grad, smooth_grad, seen, to_all = result[:4]
+        grad, smooth_grad, row = result[:3]
+        seen = result[-1]
         if not last:
             steps = [seen] + swap_pairs(seen, "gy")
-        sums = lax.all_to_all(to_all, axes, 0, 0, tiled=True)
+        to_all = jnp.broadcast_to(row[None], (n_all, 1, 128))
+        sums = lax.all_to_all(to_all, axes, 0, 0, tiled=True).reshape(n_all, 128)
     back_ground = background.reshape(variables, wide, tx)
     if pair:
         (sent,) = call(widen_kernel, [pert], [(members, variables, wide, tx)], us=1.0)
         pert_other = swap_mem(sent)
-        back = swap_mem(result[4])
+        back = swap_mem(result[3])
         control_out, analysis = call(
             final_pair_kernel,
             [sums, state, grad, back, smoothed, smooth_grad, pert, pert_other, back_ground],

time: 61.8 us -> 59.7 us (0.966)
  waiting for transfers between devices: 8.92 us -> 7.17 us
  Pallas kernels: 19.2 us -> 18 us
  local copies, waits for them, and re-layouts: 0.02 us -> 0.65 us
    ppermute x4, waiting for transfers between devices: 2.39 us -> 0.01 us  [swap_mem(): return lax.ppermute(value, 'mem', [(0, 1), (1, 0)])]
    all_to_all x1, starting transfers between devices: 3.02 us -> 4.7 us  [per_device(): sums = lax.all_to_all(to_all, axes, 0, 0, tiled=True).reshape(n_all, 128)]
    ppermute x4, starting transfers between devices: 6.89 us -> 5.39 us  [swap_mem(): return lax.ppermute(value, 'mem', [(0, 1), (1, 0)])]
    pallas_call x16 -> x17, Pallas kernels: 19.2 us -> 18 us  [call(): pl.pallas_call(kernel, out_shape=shapes, in_specs=[space] * len(ins), out...]
    broadcast_in_dim x0 -> x2, local copies, waits for them, and re-layouts: none -> 0.62 us  [per_device(): to_all = jnp.broadcast_to(row[None], (n_all, 1, 128))]
  transfers between devices with their start and end apart: 19 -> 19, of which waited for: 5 -> 5; matrix products, arithmetic and copies ran while one was open for 0% -> 1% of each run, Pallas kernels for 23% -> 23%
where the time goes in v5:
time: 59.7 us; the launch traced here: 59.5 us
  starting transfers between devices  23.2 us (39%)
  Pallas kernels  18 us (30%)
  blocking collectives  9.63 us (16%)
  waiting for transfers between devices  7.17 us (12%)
  between operations  0.87 us (1%)
  local copies, waits for them, and re-layouts  0.65 us (1%)
    pallas_call x17, Pallas kernels, call(): pl.pallas_call(kernel, out_shape=shapes, in_specs=[space] * len(ins), out...  18 us
    all_to_all x1, blocking collectives, per_device(): sums = lax.all_to_all(to_all, axes, 0, 0, tiled=True).reshape(n_all, 128)  9.63 us
    ppermute x8, starting transfers between devices, swap_over(): return lax.ppermute(value, (axis, 'gx'), sends)  9.27 us
    ppermute x4, starting transfers between devices, swap_mem(): return lax.ppermute(value, 'mem', [(0, 1), (1, 0)])  5.39 us
    all_to_all x1, waiting for transfers between devices, per_device(): sums = lax.all_to_all(to_all, axes, 0, 0, tiled=True).reshape(n_all, 128)  5.21 us
    all_to_all x1, starting transfers between devices, per_device(): sums = lax.all_to_all(to_all, axes, 0, 0, tiled=True).reshape(n_all, 128)  4.7 us
    ppermute x6, starting transfers between devices, swap_over(): return lax.ppermute(value, axis, [(i, to(i, n) % n) for i in range(n)])  3.84 us
    ppermute x8, waiting for transfers between devices, swap_over(): return lax.ppermute(value, (axis, 'gx'), sends)  1.31 us
  transfers between devices with their start and end apart: 19, of which 5 were waited for; matrix products, arithmetic and copies ran while one was open for 1% of the time, Pallas kernels for 23%

profile of v5, /device:TPU:0, one launch (start us, length us, event | category | flops | bytes accessed | tf_op | source)
XLA Modules:
  0.0 59.5 jit_solution(935258681019756722)
XLA Ops:
  0.7 0.9 %shard_map.88 = (f32[128,128]{1,0:T(8,128)S(1)}, f32[128,128]{1,0:T(8,128)S(1)}) custom-call(f32[2,128,128]{2,1,0:T(8,128)} %bitcast.18), custom_call_target="tpu_custom_call" | custom-call | flops 1000000000 | bytes 1048576 | tf_op jit(solution)/shard_map/pallas_call | solution.py:519
  1.6 3.1 %collective-permute-start.3 = (f32[128,128]{1,0:T(8,128)S(1)}, f32[128,128]{1,0:T(8,128)S(1)}, u32[]{:S(2)}, u32[]{:S(2)}) collective-permute-start(f32[128,128]{1,0:T(8,128)S(1)} %get-tuple-element.47), channel_id=1, source_target_pairs={{0,16},{16,0},{1,17},{17,1},{2,18},{18,2},{3,19},{19,3},{4,20},{20... | collective-permute-start | bytes 196616 | tf_op jit(solution)/shard_map/ppermute | solution.py:561
  4.7 2.5 %shard_map.86 = (f32[3,32,128]{2,1,0:T(8,128)S(1)}, f32[2,32,128]{2,1,0:T(8,128)S(1)}) custom-call(bf16[2,5,128,128]{3,2,1,0:T(8,128)(2,1)S(1)} %bitcast.14, s32[32,128]{1,0:T(8,128)S(1)} %copy-done.2, s32[32,128]{1,0:T(8,128)S(1)} %copy-done.3, f32[32,128]{1,0:T(8,128)S(1)} %copy-done.4, f32[32,128]{1,0:T(8,128)S(1)} %copy-done.5), custom_call_target="tpu_custom_call" | custom-call | flops 2000000000 | bytes 1048576 | tf_op jit(solution)/shard_map/pallas_call | solution.py:519
  7.3 2.1 %collective-permute-start.4 = (f32[128,128]{1,0:T(8,128)S(1)}, f32[128,128]{1,0:T(8,128)S(1)}, u32[]{:S(2)}, u32[]{:S(2)}) collective-permute-start(f32[128,128]{1,0:T(8,128)S(1)} %get-tuple-element.48), channel_id=1, source_target_pairs={{0,4},{1,5},{2,6},{3,7},{4,0},{5,1},{6,2},{7,3},{8,12},{9,13},{10,... | collective-permute-start | bytes 196616 | tf_op jit(solution)/shard_map/ppermute | solution.py:539
  9.4 1.1 %shard_map.94 = (bf16[2,384,256]{2,1,0:T(8,128)(2,1)S(1)}, bf16[2,128,144]{2,1,0:T(8,128)(2,1)S(1)}) custom-call(), custom_call_target="tpu_custom_call" | custom-call | flops 1500000000 | bytes 1048576 | tf_op jit(solution)/shard_map/pallas_call | solution.py:519
  10.8 0.9 %collective-permute-done.4.refs_2_ = f32[128,128]{1,0:T(8,128)S(1)} collective-permute-done((f32[128,128]{1,0:T(8,128)S(1)}, f32[128,128]{1,0:T(8,128)S(1)}, u32[]{:S(2)}, u32[]{:S(2)}) %collective-permute-start.4) | collective-permute-done | bytes 65568 | tf_op jit(solution)/shard_map/ppermute | solution.py:539
  12.1 2.0 %collective-permute-start.7 = (f32[2,8,128]{2,1,0:T(8,128)S(1)}, f32[2,8,128]{2,1,0:T(8,128)S(1)}, u32[]{:S(2)}, u32[]{:S(2)}) collective-permute-start(f32[2,8,128]{2,1,0:T(8,128)S(1)} %get-tuple-element.53), channel_id=1, source_target_pairs={{0,3},{1,2},{2,1},{3,0},{4,7},{5,6},{6,5},{7,4},{8,11},{9,10},{10,... | collective-permute-start | bytes 24584 | tf_op jit(solution)/shard_map/ppermute | solution.py:533
  14.1 2.8 %collective-permute-start.1 = (f32[7,32,128]{2,1,0:T(8,128)S(1)}, f32[7,32,128]{2,1,0:T(8,128)S(1)}, u32[]{:S(2)}, u32[]{:S(2)}) collective-permute-start(f32[7,32,128]{2,1,0:T(8,128)S(1)} %shard_map.87.pack.refs_6_.refs_0_), channel_id=1, source_target_pairs={{0,4},{1,5},{2,6},{3,7},{4,0},{5,1},{6,2},{7,3},{8,12},{9,13},{10,... | collective-permute-start | bytes 344072 | tf_op jit(solution)/shard_map/ppermute | solution.py:539
  16.9 1.2 %shard_map.92 = (f32[2,128,128]{2,1,0:T(8,128)S(1)}, f32[32,128]{1,0:T(8,128)S(1)}) custom-call(f32[2,128,128]{2,1,0:T(8,128)S(1)} %get-tuple-element.51.y1, f32[2,8,128]{2,1,0:T(8,128)S(1)} %collective-permute-done.6.from_first, f32[2,8,128]{2,1,0:T(8,128)S(1)} %collective-permute-done.7.from_second, bf16[2,128,144]{2,1,0:T(8,128)(2,1)S(1)} %get-tuple-element.54.kx.refs_4_, ...), custom_call_target="tpu_custom_call" | custom-call | flops 1500000000 | bytes 1048576 | tf_op jit(solution)/shard_map/pallas_call | solution.py:519
  18.1 2.2 %collective-permute-start.8 = (f32[32,128]{1,0:T(8,128)S(1)}, f32[32,128]{1,0:T(8,128)S(1)}, u32[]{:S(2)}, u32[]{:S(2)}) collective-permute-start(f32[32,128]{1,0:T(8,128)S(1)} %get-tuple-element.55.inc.refs_3_), channel_id=1, source_target_pairs={{0,4},{1,5},{2,6},{3,7},{4,0},{5,1},{6,2},{7,3},{8,12},{9,13},{10,... | collective-permute-start | bytes 49160 | tf_op jit(solution)/shard_map/ppermute | solution.py:539
  20.3 1.3 %shard_map.93 = (f32[32,128]{1,0:T(8,128)S(1)}, f32[32,128]{1,0:T(8,128)S(1)}, f32[256,128]{1,0:T(8,128)S(1)}) custom-call(f32[7,32,128]{2,1,0:T(8,128)S(1)} %shard_map.87.pack.refs_6_.refs_0_, f32[32,128]{1,0:T(8,128)S(1)} %get-tuple-element.55.inc.refs_3_), custom_call_target="tpu_custom_call" | custom-call | flops 1500000000 | bytes 1048576 | tf_op jit(solution)/shard_map/pallas_call | solution.py:519
  22.0 1.1 %shard_map.95 = (f32[2,2,8,128]{3,2,1,0:T(8,128)S(1)}, f32[2,2,8,128]{3,2,1,0:T(8,128)S(1)}, f32[2,8,32,128]{3,2,1,0:T(8,128)S(1)}) custom-call(f32[7,32,128]{2,1,0:T(8,128)S(1)} %collective-permute-done.1.refs_0_.refs_1_, f32[7,32,128]{2,1,0:T(8,128)S(1)} %collective-permute-done.2.refs_1_.refs_2_, f32[32,128]{1,0:T(8,128)S(1)} %collective-permute-done.8.refs_2_.refs_4_, ...), custom_call_target="tpu_custom_call" | custom-call | flops 1000000000 | bytes 1048576 | tf_op jit(solution)/shard_map/pallas_call | solution.py:519
  23.3 0.8 %collective-permute-start.11 = (f32[2,2,8,128]{3,2,1,0:T(8,128)S(1)}, f32[2,2,8,128]{3,2,1,0:T(8,128)S(1)}, u32[]{:S(2)}, u32[]{:S(2)}) collective-permute-start(f32[2,2,8,128]{3,2,1,0:T(8,128)S(1)} %get-tuple-element.63), channel_id=1, source_target_pairs={{0,3},{1,2},{2,1},{3,0},{4,7},{5,6},{6,5},{7,4},{8,11},{9,10},{10,... | collective-permute-start | bytes 49160 | tf_op jit(solution)/shard_map/ppermute | solution.py:533
  24.1 1.8 %shard_map.96 = (f32[2,128,128]{2,1,0:T(8,128)S(1)}, f32[2,128,128]{2,1,0:T(8,128)S(1)}) custom-call(f32[7,32,128]{2,1,0:T(8,128)S(1)} %collective-permute-done.1.refs_0_.refs_1_, f32[7,32,128]{2,1,0:T(8,128)S(1)} %collective-permute-done.2.refs_1_.refs_2_, f32[256,128]{1,0:T(8,128)S(1)} %get-tuple-element.56.refs_2_, ...), custom_call_target="tpu_custom_call" | custom-call | flops 2500000000 | bytes 1048576 | tf_op jit(solution)/shard_map/pallas_call | solution.py:519
  26.5 1.2 %shard_map.97 = (f32[2,128,128]{2,1,0:T(8,128)S(1)}, f32[2,128,128]{2,1,0:T(8,128)S(1)}, f32[1,128]{1,0:T(1,128)S(1)}, f32[32,128]{1,0:T(8,128)S(1)}) custom-call(f32[2,128,128]{2,1,0:T(8,128)S(1)} %get-tuple-element.60.refs_0_, f32[2,128,128]{2,1,0:T(8,128)S(1)} %get-tuple-element.61.refs_1_, f32[2,2,8,128]{3,2,1,0:T(8,128)S(1)} %collective-permute-done.10.refs_2_, ...), custom_call_target="tpu_custom_call" | custom-call | flops 1500000000 | bytes 1048576 | tf_op jit(solution)/shard_map/pallas_call | solution.py:519
  27.7 2.1 %collective-permute-start.12 = (f32[32,128]{1,0:T(8,128)S(1)}, f32[32,128]{1,0:T(8,128)S(1)}, u32[]{:S(2)}, u32[]{:S(2)}) collective-permute-start(f32[32,128]{1,0:T(8,128)S(1)} %get-tuple-element.68.refs_6_), channel_id=1, source_target_pairs={{0,4},{1,5},{2,6},{3,7},{4,0},{5,1},{6,2},{7,3},{8,12},{9,13},{10,... | collective-permute-start | bytes 49160 | tf_op jit(solution)/shard_map/ppermute | solution.py:539
  30.5 4.7 %all-to-all-start = ((f32[32,1,128]{2,1,0:T(1,128)}), f32[32,1,128]{2,1,0:T(1,128)S(1)}, u32[]{:S(2)}, u32[]{:S(2)}) async-start(f32[32,1,128]{2,1,0:T(1,128)} %broadcast_in_dim.17), calls=%async_computation | async-start | bytes 32768 | tf_op jit(solution)/shard_map/all_to_all | solution.py:675
  35.3 1.7 %collective-permute-start.17 = (f32[2,5,64,128]{3,2,1,0:T(8,128)S(1)}, f32[2,5,64,128]{3,2,1,0:T(8,128)S(1)}, u32[]{:S(2)}, u32[]{:S(2)}) collective-permute-start(f32[2,5,64,128]{3,2,1,0:T(8,128)S(1)} %shard_map.101), channel_id=1, source_target_pairs={{0,16},{16,0},{1,17},{17,1},{2,18},{18,2},{3,19},{19,3},{4,20},{20... | collective-permute-start | bytes 983048 | tf_op jit(solution)/shard_map/ppermute | solution.py:561
  37.0 5.2 %all-to-all-done = f32[32,1,128]{2,1,0:T(1,128)S(1)} async-done(((f32[32,1,128]{2,1,0:T(1,128)}), f32[32,1,128]{2,1,0:T(1,128)S(1)}, u32[]{:S(2)}, u32[]{:S(2)}) %all-to-all-start) | async-done | bytes 16416 | tf_op jit(solution)/shard_map/all_to_all | solution.py:675
  42.2 1.6 %shard_map.98 = (f32[2,2,8,128]{3,2,1,0:T(8,128)S(1)}, f32[2,2,8,128]{3,2,1,0:T(8,128)S(1)}, f32[3,8,32,128]{3,2,1,0:T(8,128)S(1)}, f32[32,128]{1,0:T(8,128)S(1)}) custom-call(f32[7,32,128]{2,1,0:T(8,128)S(1)} %shard_map.87.pack.refs_6_.refs_0_, f32[7,32,128]{2,1,0:T(8,128)S(1)} %collective-permute-done.1.refs_0_.refs_1_, ...), custom_call_target="tpu_custom_call" | custom-call | flops 1000000000 | bytes 1048576 | tf_op jit(solution)/shard_map/pallas_call | solution.py:519
  44.5 2.5 %shard_map.99 = (f32[2,128,128]{2,1,0:T(8,128)S(1)}, f32[2,128,128]{2,1,0:T(8,128)S(1)}) custom-call(f32[7,32,128]{2,1,0:T(8,128)S(1)} %shard_map.87.pack.refs_6_.refs_0_, f32[7,32,128]{2,1,0:T(8,128)S(1)} %collective-permute-done.1.refs_0_.refs_1_, f32[7,32,128]{2,1,0:T(8,128)S(1)} %collective-permute-done.2.refs_1_.refs_2_, ...), custom_call_target="tpu_custom_call" | custom-call | flops 2500000000 | bytes 1048576 | tf_op jit(solution)/shard_map/pallas_call | solution.py:519
  47.1 1.2 %shard_map.100 = (f32[2,128,128]{2,1,0:T(8,128)S(1)}, f32[2,128,128]{2,1,0:T(8,128)S(1)}, f32[2,128,128]{2,1,0:T(8,128)S(1)}, f32[2,128,128]{2,1,0:T(8,128)S(1)}...) custom-call(f32[2,128,128]{2,1,0:T(8,128)S(1)} %get-tuple-element.71.refs_0_, ...), custom_call_target="tpu_custom_call" | custom-call | flops 1500000000 | bytes 1048576 | tf_op jit(solution)/shard_map/pallas_call | solution.py:519
  48.9 9.6 %all_to_all.10 = f32[32,1,128]{2,1,0:T(1,128)S(1)} all-to-all(f32[32,1,128]{2,1,0:T(1,128)S(1)} %broadcast_in_dim.19), channel_id=1, replica_groups=mesh['mem'=2,'gy'=4,'gx'=4] {'mem','gy','gx'}, dimensions={0} | all-to-all | bytes 32768 | tf_op jit(solution)/shard_map/all_to_all | solution.py:675
  58.6 0.9 %shard_map.102 = (f32[2,128,128]{2,1,0:T(8,128)}, f32[5,64,128]{2,1,0:T(8,128)}) custom-call(f32[32,128]{1,0:T(8,128)S(1)} %bitcast.11, f32[2,128,128]{2,1,0:T(8,128)S(1)} %get-tuple-element.79.control, f32[2,128,128]{2,1,0:T(8,128)S(1)} %get-tuple-element.80.grad, f32[2,128,128]{2,1,0:T(8,128)S(1)} %collective-permute-done.16.back, ...), custom_call_target="tpu_custom_call" | custom-call | flops 1500000000 | bytes 1048576 | tf_op jit(solution)/shard_map/pallas_call | solution.py:519
  (46 shorter events, 4.1 us)
Async XLA Ops:
  0.6 4.0 %copy-start = (bf16[2,5,16,8,128]{4,3,2,1,0:T(8,128)(2,1)S(1)}, bf16[2,5,16,8,128]{4,3,2,1,0:T(8,128)(2,1)}, u32[]{:S(2)}) copy-start(bf16[2,5,16,8,128]{4,3,2,1,0:T(8,128)(2,1)} %param.7) | copy-start | bytes 983044
  0.6 4.0 %copy-start.2 = (s32[32,128]{1,0:T(8,128)S(1)}, s32[32,128]{1,0:T(8,128)}, u32[]{:S(2)}) copy-start(s32[32,128]{1,0:T(8,128)} %cell.1) | copy-start | bytes 49156
  0.7 4.0 %copy-start.3 = (s32[32,128]{1,0:T(8,128)S(1)}, s32[32,128]{1,0:T(8,128)}, u32[]{:S(2)}) copy-start(s32[32,128]{1,0:T(8,128)} %flag.1) | copy-start | bytes 49156
  0.7 4.0 %copy-start.4 = (f32[32,128]{1,0:T(8,128)S(1)}, f32[32,128]{1,0:T(8,128)}, u32[]{:S(2)}) copy-start(f32[32,128]{1,0:T(8,128)} %innov.1) | copy-start | bytes 49156
  1.6 5.7 %collective-permute-start.3 = (f32[128,128]{1,0:T(8,128)S(1)}, f32[128,128]{1,0:T(8,128)S(1)}, u32[]{:S(2)}, u32[]{:S(2)}) collective-permute-start(f32[128,128]{1,0:T(8,128)S(1)} %get-tuple-element.47), channel_id=1, source_target_pairs={{0,16},{16,0},{1,17},{17,1},{2,18},{18,2},{3,19},{19,3},{4,20},{20... | collective-permute-start | bytes 196616 | tf_op jit(solution)/shard_map/ppermute | solution.py:561
  7.2 6.9 %collective-permute-start = (f32[2,32,128]{2,1,0:T(8,128)S(1)}, f32[2,32,128]{2,1,0:T(8,128)S(1)}, u32[]{:S(2)}, u32[]{:S(2)}) collective-permute-start(f32[2,32,128]{2,1,0:T(8,128)S(1)} %get-tuple-element.45.refs_0_), channel_id=1, source_target_pairs={{0,16},{16,0},{1,17},{17,1},{2,18},{18,2},{3,19},{19,3},{4,20},{20... | collective-permute-start | bytes 98312 | tf_op jit(solution)/shard_map/ppermute | solution.py:561
  7.3 4.4 %collective-permute-start.4 = (f32[128,128]{1,0:T(8,128)S(1)}, f32[128,128]{1,0:T(8,128)S(1)}, u32[]{:S(2)}, u32[]{:S(2)}) collective-permute-start(f32[128,128]{1,0:T(8,128)S(1)} %get-tuple-element.48), channel_id=1, source_target_pairs={{0,4},{1,5},{2,6},{3,7},{4,0},{5,1},{6,2},{7,3},{8,12},{9,13},{10,... | collective-permute-start | bytes 196616 | tf_op jit(solution)/shard_map/ppermute | solution.py:539
  9.4 2.2 %collective-permute-start.5 = (f32[128,128]{1,0:T(8,128)S(1)}, f32[128,128]{1,0:T(8,128)S(1)}, u32[]{:S(2)}, u32[]{:S(2)}) collective-permute-start(f32[128,128]{1,0:T(8,128)S(1)} %get-tuple-element.49), channel_id=1, source_target_pairs={{0,1},{1,0},{2,3},{3,2},{4,8},{5,9},{6,10},{7,11},{8,4},{9,5},{10,... | collective-permute-start | bytes 196616 | tf_op jit(solution)/shard_map/ppermute | solution.py:539
  12.0 4.9 %collective-permute-start.6 = (f32[2,8,128]{2,1,0:T(8,128)S(1)}, f32[2,8,128]{2,1,0:T(8,128)S(1)}, u32[]{:S(2)}, u32[]{:S(2)}) collective-permute-start(f32[2,8,128]{2,1,0:T(8,128)S(1)} %get-tuple-element.52), channel_id=1, source_target_pairs={{0,1},{1,0},{2,3},{3,2},{4,5},{5,4},{6,7},{7,6},{8,9},{9,8},{10,11... | collective-permute-start | bytes 24584 | tf_op jit(solution)/shard_map/ppermute | solution.py:533
  12.1 4.8 %collective-permute-start.7 = (f32[2,8,128]{2,1,0:T(8,128)S(1)}, f32[2,8,128]{2,1,0:T(8,128)S(1)}, u32[]{:S(2)}, u32[]{:S(2)}) collective-permute-start(f32[2,8,128]{2,1,0:T(8,128)S(1)} %get-tuple-element.53), channel_id=1, source_target_pairs={{0,3},{1,2},{2,1},{3,0},{4,7},{5,6},{6,5},{7,4},{8,11},{9,10},{10,... | collective-permute-start | bytes 24584 | tf_op jit(solution)/shard_map/ppermute | solution.py:533
  14.1 7.5 %collective-permute-start.1 = (f32[7,32,128]{2,1,0:T(8,128)S(1)}, f32[7,32,128]{2,1,0:T(8,128)S(1)}, u32[]{:S(2)}, u32[]{:S(2)}) collective-permute-start(f32[7,32,128]{2,1,0:T(8,128)S(1)} %shard_map.87.pack.refs_6_.refs_0_), channel_id=1, source_target_pairs={{0,4},{1,5},{2,6},{3,7},{4,0},{5,1},{6,2},{7,3},{8,12},{9,13},{10,... | collective-permute-start | bytes 344072 | tf_op jit(solution)/shard_map/ppermute | solution.py:539
  16.9 4.7 %collective-permute-start.2 = (f32[7,32,128]{2,1,0:T(8,128)S(1)}, f32[7,32,128]{2,1,0:T(8,128)S(1)}, u32[]{:S(2)}, u32[]{:S(2)}) collective-permute-start(f32[7,32,128]{2,1,0:T(8,128)S(1)} %shard_map.87.pack.refs_6_.refs_0_), channel_id=1, source_target_pairs={{0,1},{1,0},{2,3},{3,2},{4,8},{5,9},{6,10},{7,11},{8,4},{9,5},{10,... | collective-permute-start | bytes 344072 | tf_op jit(solution)/shard_map/ppermute | solution.py:539
  18.1 3.9 %collective-permute-start.8 = (f32[32,128]{1,0:T(8,128)S(1)}, f32[32,128]{1,0:T(8,128)S(1)}, u32[]{:S(2)}, u32[]{:S(2)}) collective-permute-start(f32[32,128]{1,0:T(8,128)S(1)} %get-tuple-element.55.inc.refs_3_), channel_id=1, source_target_pairs={{0,4},{1,5},{2,6},{3,7},{4,0},{5,1},{6,2},{7,3},{8,12},{9,13},{10,... | collective-permute-start | bytes 49160 | tf_op jit(solution)/shard_map/ppermute | solution.py:539
  20.3 1.7 %collective-permute-start.9 = (f32[32,128]{1,0:T(8,128)S(1)}, f32[32,128]{1,0:T(8,128)S(1)}, u32[]{:S(2)}, u32[]{:S(2)}) collective-permute-start(f32[32,128]{1,0:T(8,128)S(1)} %get-tuple-element.55.inc.refs_3_), channel_id=1, source_target_pairs={{0,1},{1,0},{2,3},{3,2},{4,8},{5,9},{6,10},{7,11},{8,4},{9,5},{10,... | collective-permute-start | bytes 49160 | tf_op jit(solution)/shard_map/ppermute | solution.py:539
  23.1 2.8 %collective-permute-start.10 = (f32[2,2,8,128]{3,2,1,0:T(8,128)S(1)}, f32[2,2,8,128]{3,2,1,0:T(8,128)S(1)}, u32[]{:S(2)}, u32[]{:S(2)}) collective-permute-start(f32[2,2,8,128]{3,2,1,0:T(8,128)S(1)} %get-tuple-element.62), channel_id=1, source_target_pairs={{0,1},{1,0},{2,3},{3,2},{4,5},{5,4},{6,7},{7,6},{8,9},{9,8},{10,11... | collective-permute-start | bytes 49160 | tf_op jit(solution)/shard_map/ppermute | solution.py:533
  23.3 3.2 %collective-permute-start.11 = (f32[2,2,8,128]{3,2,1,0:T(8,128)S(1)}, f32[2,2,8,128]{3,2,1,0:T(8,128)S(1)}, u32[]{:S(2)}, u32[]{:S(2)}) collective-permute-start(f32[2,2,8,128]{3,2,1,0:T(8,128)S(1)} %get-tuple-element.63), channel_id=1, source_target_pairs={{0,3},{1,2},{2,1},{3,0},{4,7},{5,6},{6,5},{7,4},{8,11},{9,10},{10,... | collective-permute-start | bytes 49160 | tf_op jit(solution)/shard_map/ppermute | solution.py:533
  27.7 9.2 %collective-permute-start.12 = (f32[32,128]{1,0:T(8,128)S(1)}, f32[32,128]{1,0:T(8,128)S(1)}, u32[]{:S(2)}, u32[]{:S(2)}) collective-permute-start(f32[32,128]{1,0:T(8,128)S(1)} %get-tuple-element.68.refs_6_), channel_id=1, source_target_pairs={{0,4},{1,5},{2,6},{3,7},{4,0},{5,1},{6,2},{7,3},{8,12},{9,13},{10,... | collective-permute-start | bytes 49160 | tf_op jit(solution)/shard_map/ppermute | solution.py:539
  29.8 7.2 %collective-permute-start.13 = (f32[32,128]{1,0:T(8,128)S(1)}, f32[32,128]{1,0:T(8,128)S(1)}, u32[]{:S(2)}, u32[]{:S(2)}) collective-permute-start(f32[32,128]{1,0:T(8,128)S(1)} %get-tuple-element.68.refs_6_), channel_id=1, source_target_pairs={{0,1},{1,0},{2,3},{3,2},{4,8},{5,9},{6,10},{7,11},{8,4},{9,5},{10,... | collective-permute-start | bytes 49160 | tf_op jit(solution)/shard_map/ppermute | solution.py:539
  30.5 11.6 %all-to-all-start = ((f32[32,1,128]{2,1,0:T(1,128)}), f32[32,1,128]{2,1,0:T(1,128)S(1)}, u32[]{:S(2)}, u32[]{:S(2)}) async-start(f32[32,1,128]{2,1,0:T(1,128)} %broadcast_in_dim.17), calls=%async_computation | async-start | bytes 32768 | tf_op jit(solution)/shard_map/all_to_all | solution.py:675
  35.3 23.3 %collective-permute-start.17 = (f32[2,5,64,128]{3,2,1,0:T(8,128)S(1)}, f32[2,5,64,128]{3,2,1,0:T(8,128)S(1)}, u32[]{:S(2)}, u32[]{:S(2)}) collective-permute-start(f32[2,5,64,128]{3,2,1,0:T(8,128)S(1)} %shard_map.101), channel_id=1, source_target_pairs={{0,16},{16,0},{1,17},{17,1},{2,18},{18,2},{3,19},{19,3},{4,20},{20... | collective-permute-start | bytes 983048 | tf_op jit(solution)/shard_map/ppermute | solution.py:561
  43.8 3.2 %collective-permute-start.14 = (f32[2,2,8,128]{3,2,1,0:T(8,128)S(1)}, f32[2,2,8,128]{3,2,1,0:T(8,128)S(1)}, u32[]{:S(2)}, u32[]{:S(2)}) collective-permute-start(f32[2,2,8,128]{3,2,1,0:T(8,128)S(1)} %get-tuple-element.73), channel_id=1, source_target_pairs={{0,1},{1,0},{2,3},{3,2},{4,5},{5,4},{6,7},{7,6},{8,9},{9,8},{10,11... | collective-permute-start | bytes 49160 | tf_op jit(solution)/shard_map/ppermute | solution.py:533
  43.8 3.2 %collective-permute-start.15 = (f32[2,2,8,128]{3,2,1,0:T(8,128)S(1)}, f32[2,2,8,128]{3,2,1,0:T(8,128)S(1)}, u32[]{:S(2)}, u32[]{:S(2)}) collective-permute-start(f32[2,2,8,128]{3,2,1,0:T(8,128)S(1)} %get-tuple-element.74), channel_id=1, source_target_pairs={{0,3},{1,2},{2,1},{3,0},{4,7},{5,6},{6,5},{7,4},{8,11},{9,10},{10,... | collective-permute-start | bytes 49160 | tf_op jit(solution)/shard_map/ppermute | solution.py:533
  47.1 11.5 %copy-start.1 = (f32[5,8,8,128]{3,2,1,0:T(8,128)S(1)}, f32[5,8,8,128]{3,2,1,0:T(8,128)}, u32[]{:S(2)}) copy-start(f32[5,8,8,128]{3,2,1,0:T(8,128)} %param.9) | copy-start | bytes 491524
  48.3 10.2 %collective-permute-start.16 = (f32[2,128,128]{2,1,0:T(8,128)S(1)}, f32[2,128,128]{2,1,0:T(8,128)S(1)}, u32[]{:S(2)}, u32[]{:S(2)}) collective-permute-start(f32[2,128,128]{2,1,0:T(8,128)S(1)} %get-tuple-element.81), channel_id=1, source_target_pairs={{0,16},{16,0},{1,17},{17,1},{2,18},{18,2},{3,19},{19,3},{4,20},{20... | collective-permute-start | bytes 393224 | tf_op jit(solution)/shard_map/ppermute | solution.py:561
  (1 other events, 4.0 us)
